TPU v7x, 256 devices: a whole 4x4x8 slice. The times are simulated.
256 devices in a mesh: row: 16 (over z, x_hi), col: 16 (over y, x_lo, core).
Axes of the slice: x: 4 (x_hi: 2, x_lo: 2; x = x_hi * 2 + x_lo), y: 4, z: 8, core: 2. Of those that a mesh axis runs over, the one named last changes fastest.
Arguments:
- x_rhs: bfloat16 [32, 1024, 1024], P('col', 'row'), may hold values from -6 to 6
- panel_u: bfloat16 [32, 1024, 256], P('row', 'col'), may hold values from -0.1875 to 0.1875
- panel_v: bfloat16 [32, 1024, 256], P('row', 'col'), may hold values from -0.1875 to 0.1875
- panel_rank: int32 [32], replicated, may hold values from 32 to 256, as said below
- tile_p: bfloat16 [32, 32, 1024, 256], P('row', 'col'), may hold values from -0.0625 to 0.0625
- tile_q: bfloat16 [32, 32, 1024, 256], P('row', 'col'), may hold values from -0.1875 to 0.1875
- tile_rank: int32 [32, 32], P('row', 'col'), may hold values from 32 to 256, as said below
Outputs:
- kriged: bfloat16 [32, 1024, 1024], P('row', None, 'col')
Inputs may be any that keep to these rules, and one draw needn't show every extreme that they name: `panel_rank`: each panel tile's rank; the columns at or beyond it carry no part of the tile. `tile_rank`: each trailing tile's rank; the columns at or beyond it carry no part of the tile.
All inputs are finite; a program needn't handle non-finite values.
Results may differ from a plain program's by a relative error of at most 0.018.
Values may be sent and summed in bfloat16 or wider, within the bound.
No kernel may reach another device: no remote copies, remote signals or barrier semaphores. Data moves between devices by JAX's collectives and lax.ppermute only.
A program may use at most 64 MiB of HBM per device.

v0:
```python
import jax
import jax.numpy as jnp
from jax import lax
from jax.sharding import Mesh
from jax.sharding import PartitionSpec as P

ROW = ("row_0", "row_1")


def gather_axes(shard, axes, dim):
    whole = shard
    for number in range(len(axes) - 1, -1, -1):
        whole = lax.all_gather(whole, axes[number], axis=dim, tiled=True)
    return whole


def side_by_side(arrays, axis, dim, along):
    both = jnp.concatenate(arrays, axis=along)
    whole, at, finished = (lax.all_gather(both, axis, axis=dim, tiled=True), 0, [])
    for a in arrays:
        finished.append(lax.slice_in_dim(whole, at, at + a.shape[along], axis=along))
        at += a.shape[along]
    return tuple(finished)


def in_blocks(shard, dim, length):
    before, after = (shard.shape[:dim], shard.shape[dim + 1 :])
    return jnp.moveaxis(shard.reshape(*before, length, -1, *after), dim, 0)


def summed_on_arrival(shard, axis, dim):
    parts = in_blocks(shard, dim, lax.axis_size(axis))
    arrived = lax.all_to_all(parts, axis, split_axis=0, concat_axis=0, tiled=True)
    return arrived.astype(jnp.float32).sum(axis=0)


def from_everyone(shard, axis):
    length = lax.axis_size(axis)
    return lax.all_to_all(
        jnp.broadcast_to(shard[None], (length, *shard.shape)), axis, 0, 0, tiled=True
    )


def of_everyone(shard, axis):
    everything = from_everyone(shard, axis)
    return jnp.sum(everything.astype(jnp.float32), axis=0)


def shards(x_rhs, panel_u, panel_v, panel_rank, tile_p, tile_q, tile_rank):
    exact = lax.Precision.HIGHEST
    row_at = lax.axis_index(ROW)
    col_at = lax.axis_index("col")
    t_rows = tile_p.shape[0]
    t_cols = tile_p.shape[1]
    rank_cap = tile_p.shape[3]
    gathered = gather_axes(x_rhs, ROW, 1)
    full_u, full_v = side_by_side((panel_u, panel_v), "col", 1, 0)
    tile_slot = lax.broadcasted_iota(jnp.int32, (1, 1, rank_cap, 1), 2)
    tile_proj = jnp.einsum("ijbr,jbn->ijrn", tile_q, gathered, preferred_element_type=jnp.float32)
    tile_proj = jnp.where(tile_slot < tile_rank[:, :, None, None], tile_proj, 0.0).astype(
        jnp.bfloat16
    )
    base_sum = jnp.einsum("ijbr,ijrn->ibn", tile_p, tile_proj, preferred_element_type=jnp.float32)
    rank_slot = lax.broadcasted_iota(jnp.int32, (1, rank_cap, 1), 1)
    row_rank = lax.dynamic_slice_in_dim(panel_rank, row_at * t_rows, t_rows)
    row_keep = rank_slot < row_rank[:, None, None]
    u_wide = full_u.astype(jnp.float32)
    tile_ids = row_at * t_rows + jnp.arange(t_rows, dtype=jnp.int32)
    inside = tile_ids // t_cols == col_at
    where_rhs = jnp.clip(tile_ids - col_at * t_cols, 0, t_cols - 1)
    picked = jnp.take(gathered, where_rhs, axis=0)
    keep = jnp.logical_and(inside[:, None, None], row_keep)
    panel_proj = jnp.einsum("jbr,jbn->jrn", full_u, picked, preferred_element_type=jnp.float32)
    panel_proj = jnp.where(keep, panel_proj, 0.0).astype(jnp.bfloat16)
    sweep_part = jnp.einsum("jbr,jrn->bn", full_v, panel_proj, preferred_element_type=jnp.float32)
    sweep_share = summed_on_arrival(sweep_part.astype(jnp.bfloat16), "col", 1)
    sweep = of_everyone(sweep_share.astype(jnp.bfloat16), ROW).astype(jnp.float32)
    back_proj = jnp.einsum("ibr,bn->irn", full_v.astype(jnp.float32), sweep, precision=exact)
    back_proj = jnp.where(row_keep, back_proj, 0.0)
    late_term = jnp.einsum("ibr,irn->ibn", u_wide, back_proj, precision=exact)
    summed = lax.psum_scatter(
        base_sum.astype(jnp.bfloat16), "col", scatter_dimension=2, tiled=True
    ).astype(jnp.float32)
    return (summed - late_term).astype(jnp.bfloat16)


def solution(mesh):
    finer = Mesh(mesh.devices.reshape(8, 2, mesh.shape["col"]), ("row_0", "row_1", "col"))
    return jax.shard_map(
        shards,
        mesh=finer,
        in_specs=(
            P("col", ROW, None),
            P(ROW, "col", None),
            P(ROW, "col", None),
            P(),
            P(ROW, "col", None, None),
            P(ROW, "col", None, None),
            P(ROW, "col"),
        ),
        out_specs=P(ROW, None, "col"),
        check_vma=False,
    )
```

profile of v0, /device:TPU:16, one launch (start us, length us, event | category | flops | bytes accessed | tf_op | source)
XLA Modules:
  0.0 274.1 jit_solution(4695324869739393426)
XLA Ops:
  6.5 0.0 copy-start
  6.5 0.0 copy-start.2
  6.5 0.0 copy-start.3
  6.5 0.0 copy-start.4
  6.5 0.0 all-gather.3.cloned.1.call-start
  6.6 1.4 copy.16
  8.0 10.2 %all_gather.9 = bf16[2,128,1024]{2,0,1:T(2,128)(2,1)S(1)} all-gather(bf16[2,64,1024]{2,0,1:T(2,128)(2,1)S(1)} %copy.16), channel_id=1, replica_groups=mesh['row_0'=8,'row_1'=2,'col'=16] {'row_1'}, dimensions={1}, use_global_device_ids=true | all-gather | bytes 786432 | tf_op jit(solution)/shard_map/all_gather | solution.py:13
  18.2 1.2 copy.17
  19.3 0.0 all-gather.3.cloned.1.call-update
  19.4 0.0 all-gather.5.cloned.1.call-start
  19.4 0.0 copy-done.2
  19.4 0.1 copy.18
  19.5 0.0 copy-done.3
  19.5 0.1 copy.19
  19.6 0.8 pad_maximum_fusion
  20.4 0.0 all-gather.5.cloned.1.call-update
  20.4 0.0 reduce-scatter.2.cloned.1.call-start
  20.5 0.0 copy-done.4
  20.5 0.1 iota_compare_fusion
  20.6 64.2 %all-gather.3.cloned.1.call-done = bf16[2,1024,1024]{1,2,0:T(8,128)(2,1)} async-done(((bf16[2,128,1024]{1,2,0:T(8,128)(2,1)}), bf16[2,1024,1024]{1,2,0:T(8,128)(2,1)}) %all-gather.3.cloned.1.call-update) | async-done | bytes 4194320 | tf_op jit(solution)/shard_map/all_gather | solution.py:13
  84.8 0.0 copy-done
  84.8 9.3 %fusion = bf16[2,1024,1024]{1,2,0:T(8,128)(2,1)} fusion(bf16[2,2,1024,256]{3,2,1,0:T(8,128)(2,1)S(1)} %copy-done, pred[2,2,256]{2,1,0:T(4,128)(4,1)S(1)} %iota_compare_fusion, bf16[2,2,1024,256]{3,2,1,0:T(8,128)(2,1)} %param.12, bf16[2,1024,1024]{1,2,0:T(8,128)(2,1)} %all-gather.3.cloned.1.call-done), kind=kOutput, calls=%fused_computation.3 | convolution fusion | flops 4299161600 | bytes 12583936 | tf_op jit(solution)/shard_map/ijbr,ijrn->ibn/dot_general | solution.py:63
  94.1 0.0 copy-start.5
  94.1 0.0 reduce-scatter.2.cloned.1.call-update
  94.1 0.6 copy-done.5
  94.7 0.1 dynamic_slice.3
  94.8 0.1 iota_compare_fusion.1
  94.9 25.8 %all-gather.5.cloned.1.call-done = bf16[4,1024,256]{2,0,1:T(4,128)(2,1)} async-done(((bf16[4,64,256]{2,0,1:T(4,128)(2,1)}), bf16[4,1024,256]{2,0,1:T(4,128)(2,1)}) %all-gather.5.cloned.1.call-update) | async-done | bytes 2097168 | tf_op jit(solution)/shard_map/all_gather | solution.py:19
  120.7 5.1 %fusion.31 = (bf16[2,1024,256]{2,0,1:T(2,128)(2,1)}, bf16[2,1024,256]{2,0,1:T(2,128)(2,1)}) fusion(bf16[4,1024,256]{2,0,1:T(4,128)(2,1)} %all-gather.5.cloned.1.call-done), kind=kLoop, calls=%fused_computation.47 | loop fusion | bytes 4194304 | tf_op jit(solution)/shard_map/slice | solution.py:21
  125.8 2.4 copy.29
  128.2 4.5 %fusion.30 = (bf16[2,512,1024]{1,2,0:T(8,128)(2,1)}, bf16[2,512,1024]{1,2,0:T(8,128)(2,1)}) fusion(bf16[2,1024,1024]{1,2,0:T(8,128)(2,1)} %all-gather.3.cloned.1.call-done), kind=kLoop, calls=%fused_computation.46 | loop fusion | bytes 8388608 | tf_op jit(solution)/shard_map/jit(_take)/gather | solution.py:71
  132.7 3.6 %gather_fusion = bf16[2,512,1024]{1,2,0:T(8,128)(2,1)} fusion(bf16[2,512,1024]{1,2,0:T(8,128)(2,1)} %get-tuple-element.5, s32[1024]{0:T(1024)S(1)} %pad_clamp_fusion), kind=kCustom, calls=%fused_computation | custom fusion | bytes 4194312 | tf_op jit(solution)/shard_map/jit(_take)/gather | solution.py:71
  136.3 3.6 %gather_fusion.1 = bf16[2,512,1024]{1,2,0:T(8,128)(2,1)} fusion(bf16[2,512,1024]{1,2,0:T(8,128)(2,1)} %get-tuple-element.6, s32[1024]{0:T(1024)S(1)} %pad_clamp_fusion), kind=kCustom, calls=%fused_computation.1 | custom fusion | bytes 4194312 | tf_op jit(solution)/shard_map/jit(_take)/gather | solution.py:71
  139.9 6.4 %bitcast_convert_fusion.1 = bf16[1024,1024]{0,1:T(8,128)(2,1)} fusion(bf16[2,1024,256]{1,2,0:T(8,128)(2,1)S(1)} %copy.29, bf16[2,512,1024]{1,2,0:T(8,128)(2,1)} %gather_fusion.1, bf16[2,512,1024]{1,2,0:T(8,128)(2,1)} %gather_fusion, pred[2]{0:T(512)(128)(4,1)S(1)} %compare_and_fusion, pred[2,256]{1,0:T(4,128)(4,1)S(1)} %get-tuple-element.10, ...), kind=kOutput, calls=%fused_computation.8 | convolution fusion | flops 2160066560 | bytes 8389122 | tf_op jit(solution)/shard_map/jbr,jrn->bn/dot_general | solution.py:75
  146.3 53.4 %all_to_all.10 = bf16[16,1024,64]{1,2,0:T(8,128)(2,1)} all-to-all(bf16[16,1024,64]{1,2,0:T(8,128)(2,1)} %bitcast.34), channel_id=1, replica_groups=mesh['row_0'=8,'row_1'=2,'col'=16] {'col'}, dimensions={0} | all-to-all | bytes 4194304 | tf_op jit(solution)/shard_map/all_to_all | solution.py:33
  199.8 2.0 reduce_sum.21
  201.8 0.3 broadcast_in_dim.62
  202.0 61.3 %all_to_all.11 = bf16[16,1024,64]{1,2,0:T(8,128)(2,1)S(1)} all-to-all(bf16[16,1024,64]{1,2,0:T(8,128)(2,1)S(1)} %broadcast_in_dim.62), channel_id=1, replica_groups=mesh['row_0'=8,'row_1'=2,'col'=16] {'row_0','row_1'}, dimensions={0} | all-to-all | bytes 4194304 | tf_op jit(solution)/shard_map/all_to_all | solution.py:39
  263.3 0.0 copy-start.1
  263.3 0.4 convert_reduce_fusion
  263.7 0.8 copy-done.1
  264.6 0.6 convolution_select_fusion
  265.2 0.0 reduce-scatter.2.cloned.1.call-done
  265.2 2.3 fusion.16
  (4 shorter events, 0.0 us)
Async XLA Ops:
  6.5 78.2 %copy-start = (bf16[2,2,1024,256]{3,2,1,0:T(8,128)(2,1)S(1)}, bf16[2,2,1024,256]{3,2,1,0:T(8,128)(2,1)}, u32[]{:S(2)}) copy-start(bf16[2,2,1024,256]{3,2,1,0:T(8,128)(2,1)} %param.11) | copy-start | bytes 6291460
  6.5 12.9 %copy-start.2 = (bf16[2,64,256]{2,1,0:T(8,128)(2,1)S(1)}, bf16[2,64,256]{2,1,0:T(8,128)(2,1)}, u32[]{:S(2)}) copy-start(bf16[2,64,256]{2,1,0:T(8,128)(2,1)} %param.8) | copy-start | bytes 196612
  6.5 13.0 %copy-start.3 = (bf16[2,64,256]{2,1,0:T(8,128)(2,1)S(1)}, bf16[2,64,256]{2,1,0:T(8,128)(2,1)}, u32[]{:S(2)}) copy-start(bf16[2,64,256]{2,1,0:T(8,128)(2,1)} %param.9) | copy-start | bytes 196612
  6.5 13.9 %copy-start.4 = (s32[2,2]{1,0:T(2,128)S(1)}, s32[2,2]{1,0:T(2,128)}, u32[]{:S(2)}) copy-start(s32[2,2]{1,0:T(2,128)} %param.13) | copy-start | bytes 52
  6.5 78.2 %all-gather.3.cloned.1.call-start = ((), (), s32[]{:S(2)}) async-start(), calls=%async_computation.3 | async-start | bytes 4718592 | tf_op jit(solution)/shard_map/all_gather | solution.py:13
  19.4 101.3 %all-gather.5.cloned.1.call-start = ((), (), s32[]{:S(2)}) async-start(), calls=%async_computation.5 | async-start | bytes 2228224 | tf_op jit(solution)/shard_map/all_gather | solution.py:19
  20.4 244.8 %reduce-scatter.2.cloned.1.call-start = ((), (), s32[]{:S(2)}) async-start(), calls=%async_computation.4 | async-start | bytes 4456448 | tf_op jit(solution)/shard_map/reduce_scatter | solution.py:81
  94.1 0.7 copy-start.5
  263.3 1.2 copy-start.1
Sparse Core Ops, SparseCore 0:
  19.5 65.2 all-gather.2
  86.6 34.0 all-gather.4
  123.3 83.1 reduce-scatter.1
where the time goes:
time: 275 us; the launch traced here: 274 us
  blocking collectives  125 us (45%)
  waiting for transfers between devices  90.1 us (33%)
  local copies, waits for them, and re-layouts  23.6 us (9%)
  matrix products  18.7 us (7%)
  between operations  13.2 us (5%)
  other arithmetic  3.39 us (1%)
    all_gather x1, waiting for transfers between devices, gather_axes(): whole = lax.all_gather(whole, axes[number], axis=dim, tiled=True)  64.2 us
    all_to_all x1, blocking collectives, from_everyone(): lax.all_to_all(jnp.broadcast_to(shard[None], (length, *shard.shape)), axi...  61.3 us
    all_to_all x1, blocking collectives, summed_on_arrival(): lax.all_to_all(parts, axis, split_axis=0, concat_axis=0, tiled=True)  53.4 us
    all_gather x1, waiting for transfers between devices, side_by_side(): lax.all_gather(both, axis, axis=dim, tiled=True)  25.8 us
    gather x3, local copies, waits for them, and re-layouts, shards(): picked = jnp.take(gathered, where_rhs, axis=0)  11.7 us
    all_gather x1, blocking collectives, gather_axes(): whole = lax.all_gather(whole, axes[number], axis=dim, tiled=True)  10.2 us
    dot_general x1, matrix products, shards(): jnp.einsum('ijbr,ijrn->ibn', tile_p, tile_proj, preferred_element_type=jn...  9.32 us
    dot_general x1, matrix products, shards(): jnp.einsum('jbr,jrn->bn', full_v, panel_proj, preferred_element_type=jnp....  6.43 us
  transfers between devices with their start and end apart: 3, of which 2 were waited for; matrix products, arithmetic and copies ran while one was open for 14% of the time, Pallas kernels for 0%

commit v1 on v0

v1 whole, which is shorter than its diff:
```python
import functools

import jax
import jax.numpy as jnp
from jax import lax
from jax.experimental import pallas as pl
from jax.experimental.pallas import tpu as pltpu
from jax.sharding import Mesh
from jax.sharding import PartitionSpec as P

ALL = ("z", "xh", "y", "xl", "co")
ROW = ("z", "xh")
COL = ("y", "xl", "co")
BF = jnp.bfloat16
F32 = jnp.float32
ANY = pl.BlockSpec(memory_space=pl.ANY)
SMEM = pl.BlockSpec(memory_space=pltpu.SMEM)
VMEM = pl.BlockSpec(memory_space=pltpu.VMEM)


def shift(axis, k):
    n = lax.axis_size(axis)
    return [(i, (i + k) % n) for i in range(n)]


def move(a, axis, k):
    return lax.ppermute(a, axis, shift(axis, k))


def swap(a, axis, k=1):
    n = lax.axis_size(axis)
    return lax.ppermute(a, axis, [(i, i ^ k) for i in range(n)])


def split_kernel(at, x_ref, mine_ref, theirs_ref):
    first = at[4] == 0
    for y in range(4):
        a = x_ref[:, :, 256 * y : 256 * y + 128]
        b = x_ref[:, :, 256 * y + 128 : 256 * y + 256]
        low = jnp.concatenate([a[..., :64], b[..., :64]], axis=-1)
        high = jnp.concatenate([a[..., 64:], b[..., 64:]], axis=-1)
        mine_ref[:, :, 128 * y : 128 * y + 128] = jnp.where(first, low, high)
        theirs_ref[:, :, 128 * y : 128 * y + 128] = jnp.where(first, high, low)


def split_columns(at, x):
    half = jax.ShapeDtypeStruct((2, 64, 512), BF)
    return pl.pallas_call(
        split_kernel,
        out_shape=(half, half),
        in_specs=[SMEM, VMEM],
        out_specs=(VMEM, VMEM),
        compiler_params=pltpu.CompilerParams(vmem_limit_bytes=8 << 20),
        name="split_columns",
    )(at, x)


def fetch_x(at, pieces, x_s, sem, group=None):
    z, xh = at[0], at[1]
    copies = []
    for k, (ref, step, halves) in enumerate(pieces):
        for n, h in enumerate(halves):
            rows = lax.rem(z + step + 8, 8) * 128 + (xh if h == 0 else 1 - xh) * 64
            rows = pl.multiple_of(rows, 64)
            src = ref.at[n] if group is None else ref.at[n, group]
            dst = x_s.at[:, :, pl.ds(rows, 64), :] if group is None else x_s.at[:, pl.ds(rows, 64), :]
            copies.append(pltpu.make_async_copy(src, dst, sem))
    for c in copies:
        c.start()
    return copies


STEPS = ((0, (0, 1)), (-1, (0, 1)), (1, (0, 1)), (-2, (0, 1)), (2, (0, 1)), (-3, (0, 1)), (3, (0, 1)), (4, (0,)), (4, (1,)))


def proj_kernel(at, rank, *refs):
    pieces = [(r, s, h) for r, (s, h) in zip(refs[:9], STEPS, strict=True)]
    u_ref, out_ref, x_s, sem = refs[9:]
    group = jnp.where(at[4] == at[1], 0, 1)
    copies = fetch_x(at, pieces, x_s, sem, group)
    for c in copies:
        c.wait()
    slot = lax.broadcasted_iota(jnp.int32, (256, 1), 0)
    both = []
    for j in range(2):
        p = lax.dot_general(u_ref[j], x_s[j], (((0,), (0,)), ((), ())), preferred_element_type=F32)
        p = jnp.where(slot < rank[2 * (2 * at[0] + at[1]) + j], p, 0.0)
        both.append(p)
    for y in range(4):
        a, b = (p[:, 128 * y : 128 * y + 128] for p in both)
        out_ref[0, y] = jnp.concatenate([a[:, :64], b[:, :64]], axis=-1).astype(BF)
        out_ref[1, y] = jnp.concatenate([a[:, 64:], b[:, 64:]], axis=-1).astype(BF)


def project(at, panel_rank, pieces, u):
    return pl.pallas_call(
        proj_kernel,
        out_shape=jax.ShapeDtypeStruct((2, 4, 256, 128), BF),
        in_specs=[SMEM, SMEM] + [ANY] * 9 + [VMEM],
        out_specs=VMEM,
        scratch_shapes=[pltpu.VMEM((2, 1024, 512), BF), pltpu.SemaphoreType.DMA(())],
        compiler_params=pltpu.CompilerParams(vmem_limit_bytes=16 << 20),
        cost_estimate=pl.CostEstimate(flops=2 * 2 * 256 * 1024 * 512, bytes_accessed=4 << 20, transcendentals=0),
        name="project",
    )(at, panel_rank, *pieces, u)


def part_kernel(p_ref, v_ref, out_ref):
    lane = lax.broadcasted_iota(jnp.int32, (1, 128), 1)
    p = p_ref[...]
    zero = jnp.zeros_like(p)
    s = jnp.dot(v_ref[0], jnp.where(lane < 64, p, zero), preferred_element_type=F32)
    s += jnp.dot(v_ref[1], jnp.where(lane < 64, zero, p), preferred_element_type=F32)
    s += jnp.concatenate([s[:, 64:], s[:, :64]], axis=-1)
    out_ref[...] = jnp.where(lane < 64, s[:512], s[512:]).astype(BF)


def sweep_part(p, v):
    return pl.pallas_call(
        part_kernel,
        out_shape=jax.ShapeDtypeStruct((512, 128), BF),
        in_specs=[VMEM, VMEM],
        out_specs=VMEM,
        compiler_params=pltpu.CompilerParams(vmem_limit_bytes=8 << 20),
        cost_estimate=pl.CostEstimate(flops=2 * 2 * 256 * 1024 * 128, bytes_accessed=2 << 20, transcendentals=0),
        name="sweep_part",
    )(p, v)


def late_kernel(at, rank, s_ref, u_ref, v_ref, out_ref):
    lane = lax.broadcasted_iota(jnp.int32, (1, 128), 1)
    slot = lax.broadcasted_iota(jnp.int32, (256, 1), 0)
    packed = s_ref[...].astype(F32)
    turned = jnp.concatenate([packed[:, 64:], packed[:, :64]], axis=-1)
    s = jnp.concatenate([jnp.where(lane < 64, packed, turned), jnp.where(lane < 64, turned, packed)], axis=0)
    high = s.astype(BF)
    total = None
    for i in range(2):
        back = lax.dot_general(v_ref[i], high, (((0,), (0,)), ((), ())), preferred_element_type=F32)
        keep = jnp.logical_and(slot < rank[2 * (2 * at[0] + at[1]) + i], (lane < 64) == (i == 0))
        back = jnp.where(keep, back, 0.0).astype(BF)
        t = jnp.dot(u_ref[i], back, preferred_element_type=F32)
        total = t if total is None else total + t
    out_ref[...] = total


def late(at, panel_rank, s, u, v):
    return pl.pallas_call(
        late_kernel,
        out_shape=jax.ShapeDtypeStruct((1024, 128), F32),
        in_specs=[SMEM, SMEM, VMEM, VMEM, VMEM],
        out_specs=VMEM,
        compiler_params=pltpu.CompilerParams(vmem_limit_bytes=12 << 20),
        cost_estimate=pl.CostEstimate(flops=4 * 2 * 256 * 1024 * 128, bytes_accessed=3 << 20, transcendentals=0),
        name="late",
    )(at, panel_rank, s, u, v)


def base_kernel(at, rank_a, rank_b, *refs):
    pieces = [(r, s, h) for r, (s, h) in zip(refs[:9], STEPS, strict=True)]
    qa, qb, pa, pb = refs[9:13]
    plus_ref, minus_ref, own_ref, next_ref, prev_ref = refs[13:18]
    x_s, acc, sem = refs[18:]
    i, j = pl.program_id(0), pl.program_id(1)

    @pl.when(jnp.logical_and(i == 0, j == 0))
    def _():
        for c in fetch_x(at, pieces, x_s, sem):
            c.wait()

    slot = lax.broadcasted_iota(jnp.int32, (256, 1), 0)

    def term(q_ref, p_ref, rank, g, b):
        t = lax.dot_general(q_ref[0, 0], x_s[g, b], (((0,), (0,)), ((), ())), preferred_element_type=F32)
        t = jnp.where(slot < rank[i, b], t, 0.0).astype(BF)
        return jnp.dot(p_ref[0, 0], t, preferred_element_type=F32)

    @pl.when(j == 0)
    def _():
        acc[i] = term(qa, pa, rank_a, 0, 0)

    @pl.when(j == 1)
    def _():
        acc[i] += term(qa, pa, rank_a, 0, 1)

    @pl.when(j == 2)
    def _():
        acc[i] += term(qb, pb, rank_b, 1, 0)

    @pl.when(j == 3)
    def _():
        acc[i] += term(qb, pb, rank_b, 1, 1)

    @pl.when(jnp.logical_and(i == 1, j == 3))
    def _():
        def block(n, d):
            lanes = pl.multiple_of(lax.rem(at[2] + d, 4) * 128, 128)
            return acc[n, :, pl.ds(lanes, 128)]

        plus_ref[0] = block(0, 2).astype(BF)
        plus_ref[1] = block(1, 1).astype(BF)
        minus_ref[0] = block(1, 2).astype(BF)
        minus_ref[1] = block(0, 3).astype(BF)
        own_ref[0] = block(0, 0)
        own_ref[1] = block(1, 0)
        next_ref[...] = block(0, 1)
        prev_ref[...] = block(1, 3)


def base(at, rank_a, rank_b, pieces, qa, qb, pa, pb):
    first = pl.BlockSpec((1, 1, 1024, 256), lambda i, j: (i, jnp.minimum(j, 1), 0, 0))
    second = pl.BlockSpec((1, 1, 1024, 256), lambda i, j: (i, jnp.maximum(j - 2, 0), 0, 0))
    whole = lambda *s: pl.BlockSpec(s, lambda i, j: (0,) * len(s))
    return pl.pallas_call(
        base_kernel,
        grid=(2, 4),
        out_shape=(
            jax.ShapeDtypeStruct((2, 1024, 128), BF),
            jax.ShapeDtypeStruct((2, 1024, 128), BF),
            jax.ShapeDtypeStruct((2, 1024, 128), F32),
            jax.ShapeDtypeStruct((1024, 128), F32),
            jax.ShapeDtypeStruct((1024, 128), F32),
        ),
        in_specs=[SMEM, SMEM, SMEM] + [ANY] * 9 + [first, second, first, second],
        out_specs=(whole(2, 1024, 128), whole(2, 1024, 128), whole(2, 1024, 128), whole(1024, 128), whole(1024, 128)),
        scratch_shapes=[
            pltpu.VMEM((2, 2, 1024, 512), BF),
            pltpu.VMEM((2, 1024, 512), F32),
            pltpu.SemaphoreType.DMA(()),
        ],
        compiler_params=pltpu.CompilerParams(vmem_limit_bytes=40 << 20),
        cost_estimate=pl.CostEstimate(flops=8 * 2 * 2 * 256 * 1024 * 512, bytes_accessed=14 << 20, transcendentals=0),
        name="base",
    )(at, rank_a, rank_b, *pieces, qa, qb, pa, pb)


def pack_kernel(at, own_ref, plus_ref, minus_ref, low_ref, high_ref, keep_ref, send_ref):
    lane = lax.broadcasted_iota(jnp.int32, (1, 128), 1)
    a = own_ref[0] + minus_ref[1].astype(F32) + low_ref[...].astype(F32)
    b = own_ref[1] + plus_ref[1].astype(F32) + high_ref[...].astype(F32)
    turn = lambda v: jnp.concatenate([v[:, 64:], v[:, :64]], axis=-1)
    low = jnp.where(lane < 64, a, turn(b))
    high = jnp.where(lane < 64, turn(a), b)
    first = at[3] == 0
    keep_ref[...] = jnp.where(first, low, high)
    send_ref[...] = jnp.where(first, high, low).astype(BF)


def pack(at, own, plus, minus, low, high):
    return pl.pallas_call(
        pack_kernel,
        out_shape=(jax.ShapeDtypeStruct((1024, 128), F32), jax.ShapeDtypeStruct((1024, 128), BF)),
        in_specs=[SMEM] + [VMEM] * 5,
        out_specs=(VMEM, VMEM),
        compiler_params=pltpu.CompilerParams(vmem_limit_bytes=12 << 20),
        name="pack",
    )(at, own, plus, minus, low, high)


def last_kernel(keep_ref, came_ref, late_ref, out_ref):
    v = keep_ref[...] + came_ref[...].astype(F32) - late_ref[...]
    t = v.T.astype(BF)
    out_ref[0] = t[:64]
    out_ref[1] = t[64:]


def last(keep, came, correction):
    return pl.pallas_call(
        last_kernel,
        out_shape=jax.ShapeDtypeStruct((2, 64, 1024), BF),
        in_specs=[VMEM] * 3,
        out_specs=VMEM,
        compiler_params=pltpu.CompilerParams(vmem_limit_bytes=8 << 20),
        name="last",
    )(keep, came, correction)


def whole_panel(u, v):
    both = jnp.stack([u, v])
    other = swap(both, "xl")
    xl = lax.axis_index("xl")
    co = lax.axis_index("co")
    first = jnp.where(xl == 0, both, other)
    second = jnp.where(xl == 0, other, both)
    pair = jnp.stack([first, second])
    fp = move(pair, "y", 1)
    fm = move(pair, "y", -1)
    far = move(fp, "y", 1)
    y = lax.axis_index("y")
    four = jnp.stack([pair, fm, far, fp])
    mate = swap(four, "co")
    a = jnp.where(co == 0, four, mate)
    b = jnp.where(co == 0, mate, four)
    rows = jnp.stack([a, b], axis=2)
    rows = jnp.roll(rows, y, axis=0)
    rows = rows.transpose(3, 4, 0, 1, 2, 5, 6).reshape(2, 2, 1024, 256)
    return rows[0], rows[1]


def plane_pairs(axis_pairs):
    return axis_pairs


def shards(x_rhs, panel_u, panel_v, panel_rank, tile_p, tile_q, tile_rank):
    z, xh, y, xl, co = (lax.axis_index(a) for a in ALL)
    at = jnp.stack([z, xh, y, xl, co]).astype(jnp.int32)

    mine, theirs = split_columns(at, x_rhs)
    own = jnp.stack([mine, swap(theirs, "co")])
    piece = jnp.stack([own, swap(own, "xh")])
    qb = swap(tile_q, "co")
    pb = swap(tile_p, "co")
    rank_b = swap(tile_rank, "co")
    u, v = whole_panel(panel_u, panel_v)

    fp1, fm1 = move(piece, "z", 1), move(piece, "z", -1)
    fp2, fm2 = move(fp1, "z", 1), move(fm1, "z", -1)
    fp3, fm3 = move(fp2, "z", 1), move(fm2, "z", -1)
    fp4, fm4 = move(fp3[:1], "z", 1), move(fm3[1:], "z", -1)
    pieces = (piece, fp1, fm1, fp2, fm2, fp3, fm3, fp4, fm4)

    proj = project(at, panel_rank, pieces, u)
    n_z, n_h, n_y, n_l, n_c = (lax.axis_size(a) for a in ALL)

    def device(a, b, c, d, e):
        return (((a * n_h + b) * n_y + c) * n_l + d) * n_c + e

    spread = [(a, b, e) for a in range(n_z) for b in range(n_h) for e in range(n_c)]
    across = [(device(a, b, a >> 1, a & 1, e), device(a, b, a >> 1, 1 - (a & 1), e)) for a, b, e in spread]
    came = lax.ppermute(lax.dynamic_index_in_dim(proj, 1 - xl, 0, False), ALL, across)
    here = lax.dynamic_index_in_dim(proj, xl, 0, False)
    row = jnp.where(xl == lax.rem(z, 2), here, came)
    got = lax.dynamic_index_in_dim(row, y, 0, False)
    got = jnp.where(y == z // 2, got, jnp.zeros_like(got))
    for d in range(1, 4):
        along = [
            (device(a, b, a >> 1, f, e), device(a, b, ((a >> 1) + d) % 4, f, e)) for a, b, e in spread for f in range(n_l)
        ]
        got = got + lax.ppermute(lax.dynamic_index_in_dim(row, lax.rem(y + d, 4), 0, False), ALL, along)
    s = sweep_part(got, v)
    for axis, k in (("xh", 1), ("z", 1), ("z", 2), ("z", 4)):
        s = s + swap(s, axis, k)
    correction = late(at, panel_rank, s, u, v)

    plus, minus, own_sum, after, before = base(at, tile_rank, rank_b, pieces, tile_q, qb, tile_p, pb)
    plus, minus = move(plus, "y", 1), move(minus, "y", -1)
    low = move((after + plus[0].astype(F32)).astype(BF), "y", 1)
    high = move((before + minus[0].astype(F32)).astype(BF), "y", -1)
    keep, send = pack(at, own_sum, plus, minus, low, high)
    out = last(keep, swap(send, "xl"), correction)
    return out.swapaxes(1, 2)


def solution(mesh):
    finer = Mesh(mesh.devices.reshape(8, 2, 4, 2, 2), ALL)
    return jax.shard_map(
        shards,
        mesh=finer,
        in_specs=(
            P(COL, ROW, None),
            P(ROW, COL, None),
            P(ROW, COL, None),
            P(),
            P(ROW, COL, None, None),
            P(ROW, COL, None, None),
            P(ROW, COL),
        ),
        out_specs=P(ROW, None, COL),
        check_vma=False,
    )
```

time: 275 us -> 141 us (0.51)
  blocking collectives: 125 us -> 0 us
  starting transfers between devices: 0.12 us -> 42.5 us
  waiting for transfers between devices: 90.1 us -> 64.7 us
  Pallas kernels: 0 us -> 19.2 us
  matrix products: 18.7 us -> 0 us
  local copies, waits for them, and re-layouts: 23.6 us -> 6.54 us
  between operations: 13.2 us -> 0.39 us
  other arithmetic: 3.39 us -> 6.77 us
    all_to_all x2 -> x0, blocking collectives: 115 us -> none  [the longest x1 61.3 us: from_everyone(): lax.all_to_all(jnp.broadcast_to(shard[None], (length, *shard.shape)), axi...]
    all_gather x2 -> x0, waiting for transfers between devices: 90 us -> none  [the longest x1 64.2 us: gather_axes(): whole = lax.all_gather(whole, axes[number], axis=dim, tiled=True)]
    ppermute x0 -> x31, waiting for transfers between devices: none -> 64.7 us  [the longest x15 33.3 us: move(): return lax.ppermute(a, axis, shift(axis, k))]
    ppermute x0 -> x31, starting transfers between devices: none -> 42.5 us  [the longest x15 23.2 us: move(): return lax.ppermute(a, axis, shift(axis, k))]
    pallas_call x0 -> x7, Pallas kernels: none -> 19.2 us  [the longest x1 12 us: base(): pl.pallas_call(base_kernel, grid=(2, 4), out_shape=(jax.ShapeDtypeStruct(...]
    dot_general x4 -> x0, matrix products: 18.7 us -> none  [the longest x1 9.32 us: shards(): jnp.einsum('ijbr,ijrn->ibn', tile_p, tile_proj, preferred_element_type=jn...]
    gather x3 -> x0, local copies, waits for them, and re-layouts: 11.7 us -> none  [shards(): picked = jnp.take(gathered, where_rhs, axis=0)]
    all_gather x1 -> x0, blocking collectives: 10.2 us -> none  [gather_axes(): whole = lax.all_gather(whole, axes[number], axis=dim, tiled=True)]
  transfers between devices with their start and end apart: 3 -> 31, of which waited for: 2 -> 12; matrix products, arithmetic and copies ran while one was open for 14% -> 7% of each run, Pallas kernels for 0% -> 13%
where the time goes in v1:
time: 141 us; the launch traced here: 140 us
  waiting for transfers between devices  64.7 us (46%)
  starting transfers between devices  42.5 us (30%)
  Pallas kernels  19.2 us (14%)
  other arithmetic  6.77 us (5%)
  local copies, waits for them, and re-layouts  6.54 us (5%)
    ppermute x15, waiting for transfers between devices, move(): return lax.ppermute(a, axis, shift(axis, k))  33.3 us
    ppermute x15, starting transfers between devices, move(): return lax.ppermute(a, axis, shift(axis, k))  23.2 us
    ppermute x12, waiting for transfers between devices, swap(): return lax.ppermute(a, axis, [(i, i ^ k) for i in range(n)])  22.1 us
    ppermute x12, starting transfers between devices, swap(): return lax.ppermute(a, axis, [(i, i ^ k) for i in range(n)])  15.3 us
    pallas_call x1, Pallas kernels, base(): pl.pallas_call(base_kernel, grid=(2, 4), out_shape=(jax.ShapeDtypeStruct(...  12 us
    ppermute x3, waiting for transfers between devices, shards(): lax.ppermute(lax.dynamic_index_in_dim(row, lax.rem(y + d, 4), 0, False),...  9.33 us
    ppermute x3, starting transfers between devices, shards(): lax.ppermute(lax.dynamic_index_in_dim(row, lax.rem(y + d, 4), 0, False),...  3.22 us
    unnamed x28, local copies, waits for them, and re-layouts  3.07 us
  transfers between devices with their start and end apart: 31, of which 12 were waited for; matrix products, arithmetic and copies ran while one was open for 7% of the time, Pallas kernels for 13%

profile of v1, /device:TPU:16, one launch (start us, length us, event | category | flops | bytes accessed | tf_op | source)
XLA Modules:
  0.0 140.1 jit_solution(14805298452364944069)
XLA Ops:
  0.0 0.9 pad_maximum_fusion.4
  0.9 1.6 %collective-permute-start.18 = (bf16[2,2,64,256]{3,2,1,0:T(8,128)(2,1)S(1)}, bf16[2,2,64,256]{3,2,1,0:T(8,128)(2,1)S(1)}, u32[]{:S(2)}, u32[]{:S(2)}) collective-permute-start(bf16[2,2,64,256]{3,2,1,0:T(8,128)(2,1)S(1)} %pad_maximum_fusion.4), channel_id=1, source_target_pairs={{0,2},{2,0},{1,3},{3,1},{4,6},{6,4},{5,7},{7,5},{8,10},{10,8},{9,1... | collective-permute-start | bytes 393224 | tf_op jit(solution)/shard_map/ppermute | solution.py:32
  2.5 0.1 stack.83.at
  2.6 0.9 copy-done.10
  3.5 0.7 split_columns.1
  4.2 0.1 collective-permute-start.1
  4.3 1.9 %collective-permute-done.18 = bf16[2,2,64,256]{3,2,1,0:T(8,128)(2,1)S(1)} collective-permute-done((bf16[2,2,64,256]{3,2,1,0:T(8,128)(2,1)S(1)}, bf16[2,2,64,256]{3,2,1,0:T(8,128)(2,1)S(1)}, u32[]{:S(2)}, u32[]{:S(2)}) %collective-permute-start.18) | collective-permute-done | bytes 131104 | tf_op jit(solution)/shard_map/ppermute | solution.py:32
  6.2 0.9 select_bitcast_fusion.3
  7.2 0.0 copy-start.12
  7.2 1.4 collective-permute-start.20
  8.6 3.1 %collective-permute-start.2 = (bf16[2,2,64,512]{3,2,1,0:T(8,128)(2,1)S(1)}, bf16[2,2,64,512]{3,2,1,0:T(8,128)(2,1)S(1)}, u32[]{:S(2)}, u32[]{:S(2)}) collective-permute-start(bf16[2,2,64,512]{3,2,1,0:T(8,128)(2,1)S(1)} %get-tuple-element.35), channel_id=1, source_target_pairs={{0,16},{16,0},{1,17},{17,1},{2,18},{18,2},{3,19},{19,3},{4,20},{20... | collective-permute-start | bytes 786440 | tf_op jit(solution)/shard_map/ppermute | solution.py:32
  11.7 0.7 collective-permute-start.19
  12.4 2.0 %collective-permute-done.20 = bf16[2,2,2,64,256]{4,3,2,1,0:T(8,128)(2,1)S(1)} collective-permute-done((bf16[2,2,2,64,256]{4,3,2,1,0:T(8,128)(2,1)S(1)}, bf16[2,2,2,64,256]{4,3,2,1,0:T(8,128)(2,1)S(1)}, u32[]{:S(2)}, u32[]{:S(2)}) %collective-permute-start.20) | collective-permute-done | bytes 262176 | tf_op jit(solution)/shard_map/ppermute | solution.py:27
  14.4 1.3 collective-permute-start.21
  15.7 1.4 collective-permute-done.2
  17.1 0.1 pad_maximum_fusion.1.refs_0_
  17.1 2.0 %collective-permute-start.3 = (bf16[2,2,2,64,512]{4,3,2,1,0:T(8,128)(2,1)S(1)}, bf16[2,2,2,64,512]{4,3,2,1,0:T(8,128)(2,1)S(1)}, u32[]{:S(2)}, u32[]{:S(2)}) collective-permute-start(bf16[2,2,2,64,512]{4,3,2,1,0:T(8,128)(2,1)S(1)} %pad_maximum_fusion.1.refs_0_), channel_id=1, source_target_pairs={{0,32},{32,64},{64,96},{96,128},{128,160},{160,192},{192,224},{224... | collective-permute-start | bytes 1572872 | tf_op jit(solution)/shard_map/ppermute | solution.py:27
  19.1 4.0 %collective-permute-start.4 = (bf16[2,2,2,64,512]{4,3,2,1,0:T(8,128)(2,1)S(1)}, bf16[2,2,2,64,512]{4,3,2,1,0:T(8,128)(2,1)S(1)}, u32[]{:S(2)}, u32[]{:S(2)}) collective-permute-start(bf16[2,2,2,64,512]{4,3,2,1,0:T(8,128)(2,1)S(1)} %pad_maximum_fusion.1.refs_0_), channel_id=1, source_target_pairs={{0,224},{32,0},{64,32},{96,64},{128,96},{160,128},{192,160},{224,1... | collective-permute-start | bytes 1572872 | tf_op jit(solution)/shard_map/ppermute | solution.py:27
  23.2 1.1 pad_maximum_fusion
  24.3 0.5 collective-permute-start.11
  24.8 8.2 %collective-permute-done.3.refs_1_ = bf16[2,2,2,64,512]{4,3,2,1,0:T(8,128)(2,1)S(1)} collective-permute-done((bf16[2,2,2,64,512]{4,3,2,1,0:T(8,128)(2,1)S(1)}, bf16[2,2,2,64,512]{4,3,2,1,0:T(8,128)(2,1)S(1)}, u32[]{:S(2)}, u32[]{:S(2)}) %collective-permute-start.3) | collective-permute-done | bytes 524320 | tf_op jit(solution)/shard_map/ppermute | solution.py:27
  33.0 3.2 %collective-permute-start.6 = (bf16[2,2,2,64,512]{4,3,2,1,0:T(8,128)(2,1)S(1)}, bf16[2,2,2,64,512]{4,3,2,1,0:T(8,128)(2,1)S(1)}, u32[]{:S(2)}, u32[]{:S(2)}) collective-permute-start(bf16[2,2,2,64,512]{4,3,2,1,0:T(8,128)(2,1)S(1)} %collective-permute-done.4.refs_2_), channel_id=1, source_target_pairs={{0,224},{32,0},{64,32},{96,64},{128,96},{160,128},{192,160},{224,1... | collective-permute-start | bytes 1572872 | tf_op jit(solution)/shard_map/ppermute | solution.py:27
  36.2 9.1 %collective-permute-done.5.refs_3_ = bf16[2,2,2,64,512]{4,3,2,1,0:T(8,128)(2,1)S(1)} collective-permute-done((bf16[2,2,2,64,512]{4,3,2,1,0:T(8,128)(2,1)S(1)}, bf16[2,2,2,64,512]{4,3,2,1,0:T(8,128)(2,1)S(1)}, u32[]{:S(2)}, u32[]{:S(2)}) %collective-permute-start.5) | collective-permute-done | bytes 524320 | tf_op jit(solution)/shard_map/ppermute | solution.py:27
  45.3 0.1 collective-permute-start.7
  45.4 3.2 %collective-permute-start.8 = (bf16[2,2,2,64,512]{4,3,2,1,0:T(8,128)(2,1)S(1)}, bf16[2,2,2,64,512]{4,3,2,1,0:T(8,128)(2,1)S(1)}, u32[]{:S(2)}, u32[]{:S(2)}) collective-permute-start(bf16[2,2,2,64,512]{4,3,2,1,0:T(8,128)(2,1)S(1)} %collective-permute-done.6.refs_4_), channel_id=1, source_target_pairs={{0,224},{32,0},{64,32},{96,64},{128,96},{160,128},{192,160},{224,1... | collective-permute-start | bytes 1572872 | tf_op jit(solution)/shard_map/ppermute | solution.py:27
  48.7 1.5 %select_bitcast_fusion = (bf16[4,2,1,2,2,64,256]{6,5,4,3,1,0,2:T(8,128)(2,1)S(1)}, bf16[4,2,1,2,2,64,256]{6,5,4,3,1,0,2:T(8,128)(2,1)S(1)}) fusion(bf16[4,2,2,2,64,256]{5,4,3,2,1,0:T(8,128)(2,1)} %collective-permute-done.22, pred[]{:T(512)S(6)} %eq.19, bf16[1,2,2,2,64,256]{5,4,3,2,1,0:T(8,128)(2,1)S(1)} %bitcast.62, ...), kind=kLoop, calls=%fused_computation.9 | loop fusion | flops 2621440 | bytes 4194305 | tf_op jit(solution)/shard_map/stack | solution.py:294
  50.2 1.1 fusion.2
  51.2 9.6 %collective-permute-done.7.refs_5_ = bf16[2,2,2,64,512]{4,3,2,1,0:T(8,128)(2,1)S(1)} collective-permute-done((bf16[2,2,2,64,512]{4,3,2,1,0:T(8,128)(2,1)S(1)}, bf16[2,2,2,64,512]{4,3,2,1,0:T(8,128)(2,1)S(1)}, u32[]{:S(2)}, u32[]{:S(2)}) %collective-permute-start.7) | collective-permute-done | bytes 524320 | tf_op jit(solution)/shard_map/ppermute | solution.py:27
  60.9 0.1 collective-permute-start.9
  61.0 3.3 %collective-permute-start.10 = (bf16[1,2,2,64,512]{4,3,2,1,0:T(8,128)(2,1)S(1)}, bf16[1,2,2,64,512]{4,3,2,1,0:T(8,128)(2,1)S(1)}, u32[]{:S(2)}, u32[]{:S(2)}) collective-permute-start(bf16[1,2,2,64,512]{4,3,2,1,0:T(8,128)(2,1)S(1)} %slice.27), channel_id=1, source_target_pairs={{0,224},{32,0},{64,32},{96,64},{128,96},{160,128},{192,160},{224,1... | collective-permute-start | bytes 786440 | tf_op jit(solution)/shard_map/ppermute | solution.py:27
  64.3 1.1 fusion.10
  65.4 0.1 copy.8
  65.6 4.4 %collective-permute-done.9.refs_7_ = bf16[1,2,2,64,512]{4,3,2,1,0:T(8,128)(2,1)S(1)} collective-permute-done((bf16[1,2,2,64,512]{4,3,2,1,0:T(8,128)(2,1)S(1)}, bf16[1,2,2,64,512]{4,3,2,1,0:T(8,128)(2,1)S(1)}, u32[]{:S(2)}, u32[]{:S(2)}) %collective-permute-start.9) | collective-permute-done | bytes 262176 | tf_op jit(solution)/shard_map/ppermute | solution.py:27
  70.0 2.8 %project.1 = bf16[2,4,256,128]{3,2,1,0:T(8,128)(2,1)S(1)} custom-call(s32[5]{0:T(128)S(1)} %stack.83.at, s32[32]{0:T(128)S(1)} %copy-done.11, bf16[2,2,2,64,512]{4,3,2,1,0:T(8,128)(2,1)S(1)} %pad_maximum_fusion.1.refs_0_, bf16[2,2,2,64,512]{4,3,2,1,0:T(8,128)(2,1)S(1)} %collective-permute-done.3.refs_1_, ...), custom_call_target="tpu_custom_call" | custom-call | flops 536870912 | bytes 4194304 | tf_op jit(solution)/shard_map/project/pallas_call | solution.py:96
  72.8 0.7 collective-permute-start.23
  73.5 1.0 copy-done.1
  74.6 1.0 copy-done.3
  75.6 12.0 %base.1 = (bf16[2,1024,128]{2,1,0:T(8,128)(2,1)}, bf16[2,1024,128]{2,1,0:T(8,128)(2,1)}, f32[2,1024,128]{2,1,0:T(8,128)S(1)}, f32[1024,128]{1,0:T(8,128)S(1)}, f32[1024,128]{1,0:T(8,128)S(1)}) custom-call(s32[5]{0:T(128)S(1)} %stack.83.at, s32[2,2]{1,0:T(2,128)S(1)} %copy-done.12, s32[2,2]{1,0:T(2,128)S(1)} %collective-permute-done.rank_b, ...), custom_call_target="tpu_custom_call" | custom-call | flops 4294967296 | bytes 14680064 | tf_op jit(solution)/shard_map/base/pallas_call | solution.py:214
  87.6 0.6 collective-permute-start.13
  88.2 0.7 dynamic-slice_bitcast_fusion.3
  88.9 0.7 collective-permute-start.26
  89.6 1.3 collective-permute-start.25
  90.9 1.3 collective-permute-start.24
  92.2 1.0 collective-permute-start.14
  93.2 1.4 copy.9
  94.5 9.3 %collective-permute-done.25 = bf16[256,128]{1,0:T(8,128)(2,1)S(1)} collective-permute-done((bf16[256,128]{1,0:T(8,128)(2,1)}, bf16[256,128]{1,0:T(8,128)(2,1)S(1)}, u32[]{:S(2)}, u32[]{:S(2)}) %collective-permute-start.25) | collective-permute-done | bytes 65568 | tf_op jit(solution)/shard_map/ppermute | solution.py:339
  103.9 0.9 fusion.7.p_ref
  104.7 0.5 sweep_part.1
  105.2 2.8 %collective-permute-start.27 = (bf16[512,128]{1,0:T(8,128)(2,1)S(1)}, bf16[512,128]{1,0:T(8,128)(2,1)S(1)}, u32[]{:S(2)}, u32[]{:S(2)}) collective-permute-start(bf16[512,128]{1,0:T(8,128)(2,1)S(1)} %sweep_part.1), channel_id=1, source_target_pairs={{0,16},{16,0},{1,17},{17,1},{2,18},{18,2},{3,19},{19,3},{4,20},{20... | collective-permute-start | bytes 393224 | tf_op jit(solution)/shard_map/ppermute | solution.py:32
  108.1 0.1 fusion.5
  108.2 0.1 collective-permute-start.15
  108.3 0.1 fusion.4
  108.3 2.3 %collective-permute-start.16 = (bf16[1024,128]{1,0:T(8,128)(2,1)S(1)}, bf16[1024,128]{1,0:T(8,128)(2,1)S(1)}, u32[]{:S(2)}, u32[]{:S(2)}) collective-permute-start(bf16[1024,128]{1,0:T(8,128)(2,1)S(1)} %fusion.4), channel_id=1, source_target_pairs={{0,12},{4,0},{8,4},{12,8},{1,13},{5,1},{9,5},{13,9},{2,14},{6,2},{... | collective-permute-start | bytes 786440 | tf_op jit(solution)/shard_map/ppermute | solution.py:27
  110.6 1.2 collective-permute-done.27
  111.8 0.3 collective-permute-start.28
  112.2 5.4 %collective-permute-done.28 = bf16[512,128]{1,0:T(8,128)(2,1)S(1)} collective-permute-done((bf16[512,128]{1,0:T(8,128)(2,1)S(1)}, bf16[512,128]{1,0:T(8,128)(2,1)S(1)}, u32[]{:S(2)}, u32[]{:S(2)}) %collective-permute-start.28) | collective-permute-done | bytes 131104 | tf_op jit(solution)/shard_map/ppermute | solution.py:32
  117.6 1.6 %collective-permute-start.29 = (bf16[512,128]{1,0:T(8,128)(2,1)S(1)}, bf16[512,128]{1,0:T(8,128)(2,1)S(1)}, u32[]{:S(2)}, u32[]{:S(2)}) collective-permute-start(bf16[512,128]{1,0:T(8,128)(2,1)S(1)} %add.85), channel_id=1, source_target_pairs={{0,64},{32,96},{64,0},{96,32},{128,192},{160,224},{192,128},{224,1... | collective-permute-start | bytes 393224 | tf_op jit(solution)/shard_map/ppermute | solution.py:32
  119.2 0.9 pack.1
  120.2 1.7 %collective-permute-start.17 = (bf16[1024,128]{1,0:T(8,128)(2,1)S(1)}, bf16[1024,128]{1,0:T(8,128)(2,1)S(1)}, u32[]{:S(2)}, u32[]{:S(2)}) collective-permute-start(bf16[1024,128]{1,0:T(8,128)(2,1)S(1)} %get-tuple-element.22), channel_id=1, source_target_pairs={{0,2},{2,0},{1,3},{3,1},{4,6},{6,4},{5,7},{7,5},{8,10},{10,8},{9,1... | collective-permute-start | bytes 786440 | tf_op jit(solution)/shard_map/ppermute | solution.py:32
  121.9 5.4 %collective-permute-done.29 = bf16[512,128]{1,0:T(8,128)(2,1)S(1)} collective-permute-done((bf16[512,128]{1,0:T(8,128)(2,1)S(1)}, bf16[512,128]{1,0:T(8,128)(2,1)S(1)}, u32[]{:S(2)}, u32[]{:S(2)}) %collective-permute-start.29) | collective-permute-done | bytes 131104 | tf_op jit(solution)/shard_map/ppermute | solution.py:32
  127.3 3.5 %collective-permute-start.30 = (bf16[512,128]{1,0:T(8,128)(2,1)S(1)}, bf16[512,128]{1,0:T(8,128)(2,1)S(1)}, u32[]{:S(2)}, u32[]{:S(2)}) collective-permute-start(bf16[512,128]{1,0:T(8,128)(2,1)S(1)} %add.86), channel_id=1, source_target_pairs={{0,128},{32,160},{64,192},{96,224},{128,0},{160,32},{192,64},{224,... | collective-permute-start | bytes 393224 | tf_op jit(solution)/shard_map/ppermute | solution.py:32
  130.8 6.8 %collective-permute-done.30 = bf16[512,128]{1,0:T(8,128)(2,1)S(1)} collective-permute-done((bf16[512,128]{1,0:T(8,128)(2,1)S(1)}, bf16[512,128]{1,0:T(8,128)(2,1)S(1)}, u32[]{:S(2)}, u32[]{:S(2)}) %collective-permute-start.30) | collective-permute-done | bytes 131104 | tf_op jit(solution)/shard_map/ppermute | solution.py:32
  137.7 1.5 %late.1.late_ref = f32[1024,128]{1,0:T(8,128)S(1)} custom-call(s32[5]{0:T(128)S(1)} %stack.83.at, s32[32]{0:T(128)S(1)} %copy-done.11, bf16[512,128]{1,0:T(8,128)(2,1)S(1)} %add.87.s_ref, bf16[2,1024,256]{2,1,0:T(8,128)(2,1)S(1)} %bitcast.59, bf16[2,1024,256]{2,1,0:T(8,128)(2,1)S(1)} %bitcast.57), custom_call_target="tpu_custom_call" | custom-call | flops 268435456 | bytes 3145728 | tf_op jit(solution)/shard_map/late/pallas_call | solution.py:148
  139.2 0.9 last.1
  (57 shorter events, 0.4 us)
Async XLA Ops:
  0.9 5.3 %collective-permute-start.18 = (bf16[2,2,64,256]{3,2,1,0:T(8,128)(2,1)S(1)}, bf16[2,2,64,256]{3,2,1,0:T(8,128)(2,1)S(1)}, u32[]{:S(2)}, u32[]{:S(2)}) collective-permute-start(bf16[2,2,64,256]{3,2,1,0:T(8,128)(2,1)S(1)} %pad_maximum_fusion.4), channel_id=1, source_target_pairs={{0,2},{2,0},{1,3},{3,1},{4,6},{6,4},{5,7},{7,5},{8,10},{10,8},{9,1... | collective-permute-start | bytes 393224 | tf_op jit(solution)/shard_map/ppermute | solution.py:32
  2.6 1.0 copy-start.10
  4.2 4.4 %collective-permute-start.1 = (bf16[2,64,512]{2,1,0:T(8,128)(2,1)S(1)}, bf16[2,64,512]{2,1,0:T(8,128)(2,1)S(1)}, u32[]{:S(2)}, u32[]{:S(2)}) collective-permute-start(bf16[2,64,512]{2,1,0:T(8,128)(2,1)S(1)} %get-tuple-element.15), channel_id=1, source_target_pairs={{0,1},{1,0},{2,3},{3,2},{4,5},{5,4},{6,7},{7,6},{8,9},{9,8},{10,11... | collective-permute-start | bytes 393224 | tf_op jit(solution)/shard_map/ppermute | solution.py:32
  7.2 38.1 %copy-start.12 = (s32[2,2]{1,0:T(2,128)S(1)}, s32[2,2]{1,0:T(2,128)}, u32[]{:S(2)}) copy-start(s32[2,2]{1,0:T(2,128)} %rank_a.1) | copy-start | bytes 52
  7.2 7.3 %collective-permute-start.20 = (bf16[2,2,2,64,256]{4,3,2,1,0:T(8,128)(2,1)S(1)}, bf16[2,2,2,64,256]{4,3,2,1,0:T(8,128)(2,1)S(1)}, u32[]{:S(2)}, u32[]{:S(2)}) collective-permute-start(bf16[2,2,2,64,256]{4,3,2,1,0:T(8,128)(2,1)S(1)} %get-tuple-element.31), channel_id=1, source_target_pairs={{0,4},{4,8},{8,12},{12,0},{1,5},{5,9},{9,13},{13,1},{2,6},{6,10},{... | collective-permute-start | bytes 786440 | tf_op jit(solution)/shard_map/ppermute | solution.py:27
  8.6 8.5 %collective-permute-start.2 = (bf16[2,2,64,512]{3,2,1,0:T(8,128)(2,1)S(1)}, bf16[2,2,64,512]{3,2,1,0:T(8,128)(2,1)S(1)}, u32[]{:S(2)}, u32[]{:S(2)}) collective-permute-start(bf16[2,2,64,512]{3,2,1,0:T(8,128)(2,1)S(1)} %get-tuple-element.35), channel_id=1, source_target_pairs={{0,16},{16,0},{1,17},{17,1},{2,18},{18,2},{3,19},{19,3},{4,20},{20... | collective-permute-start | bytes 786440 | tf_op jit(solution)/shard_map/ppermute | solution.py:32
  11.7 11.5 %collective-permute-start.19 = (bf16[2,2,2,64,256]{4,3,2,1,0:T(8,128)(2,1)S(1)}, bf16[2,2,2,64,256]{4,3,2,1,0:T(8,128)(2,1)S(1)}, u32[]{:S(2)}, u32[]{:S(2)}) collective-permute-start(bf16[2,2,2,64,256]{4,3,2,1,0:T(8,128)(2,1)S(1)} %get-tuple-element.31), channel_id=1, source_target_pairs={{0,12},{4,0},{8,4},{12,8},{1,13},{5,1},{9,5},{13,9},{2,14},{6,2},{... | collective-permute-start | bytes 786440 | tf_op jit(solution)/shard_map/ppermute | solution.py:27
  14.4 8.7 %collective-permute-start.21 = (bf16[2,2,2,64,256]{4,3,2,1,0:T(8,128)(2,1)S(1)}, bf16[2,2,2,64,256]{4,3,2,1,0:T(8,128)(2,1)S(1)}, u32[]{:S(2)}, u32[]{:S(2)}) collective-permute-start(bf16[2,2,2,64,256]{4,3,2,1,0:T(8,128)(2,1)S(1)} %collective-permute-done.20), channel_id=1, source_target_pairs={{0,4},{4,8},{8,12},{12,0},{1,5},{5,9},{9,13},{13,1},{2,6},{6,10},{... | collective-permute-start | bytes 786440 | tf_op jit(solution)/shard_map/ppermute | solution.py:27
  17.1 15.9 %collective-permute-start.3 = (bf16[2,2,2,64,512]{4,3,2,1,0:T(8,128)(2,1)S(1)}, bf16[2,2,2,64,512]{4,3,2,1,0:T(8,128)(2,1)S(1)}, u32[]{:S(2)}, u32[]{:S(2)}) collective-permute-start(bf16[2,2,2,64,512]{4,3,2,1,0:T(8,128)(2,1)S(1)} %pad_maximum_fusion.1.refs_0_), channel_id=1, source_target_pairs={{0,32},{32,64},{64,96},{96,128},{128,160},{160,192},{192,224},{224... | collective-permute-start | bytes 1572872 | tf_op jit(solution)/shard_map/ppermute | solution.py:27
  19.1 13.9 %collective-permute-start.4 = (bf16[2,2,2,64,512]{4,3,2,1,0:T(8,128)(2,1)S(1)}, bf16[2,2,2,64,512]{4,3,2,1,0:T(8,128)(2,1)S(1)}, u32[]{:S(2)}, u32[]{:S(2)}) collective-permute-start(bf16[2,2,2,64,512]{4,3,2,1,0:T(8,128)(2,1)S(1)} %pad_maximum_fusion.1.refs_0_), channel_id=1, source_target_pairs={{0,224},{32,0},{64,32},{96,64},{128,96},{160,128},{192,160},{224,1... | collective-permute-start | bytes 1572872 | tf_op jit(solution)/shard_map/ppermute | solution.py:27
  23.2 1.7 %copy-start.13 = (bf16[2,2,2,64,256]{4,3,2,1,0:T(8,128)(2,1)}, bf16[2,2,2,64,256]{4,3,2,1,0:T(8,128)(2,1)S(1)}, u32[]{:S(2)}) copy-start(bf16[2,2,2,64,256]{4,3,2,1,0:T(8,128)(2,1)S(1)} %collective-permute-done.21) | copy-start | bytes 786436
  24.3 21.1 %collective-permute-start.22 = (bf16[4,2,2,2,64,256]{5,4,3,2,1,0:T(8,128)(2,1)}, bf16[4,2,2,2,64,256]{5,4,3,2,1,0:T(8,128)(2,1)}, u32[]{:S(2)}, u32[]{:S(2)}) collective-permute-start(bf16[4,2,2,2,64,256]{5,4,3,2,1,0:T(8,128)(2,1)} %pad_maximum_fusion), channel_id=1, source_target_pairs={{0,1},{1,0},{2,3},{3,2},{4,5},{5,4},{6,7},{7,6},{8,9},{9,8},{10,11... | collective-permute-start | bytes 3145736 | tf_op jit(solution)/shard_map/ppermute | solution.py:32
  24.3 49.2 %collective-permute-start.11 = (bf16[2,2,1024,256]{3,2,1,0:T(8,128)(2,1)}, bf16[2,2,1024,256]{3,2,1,0:T(8,128)(2,1)}, u32[]{:S(2)}, u32[]{:S(2)}) collective-permute-start(bf16[2,2,1024,256]{3,2,1,0:T(8,128)(2,1)} %refs_9_.1), channel_id=1, source_target_pairs={{0,1},{1,0},{2,3},{3,2},{4,5},{5,4},{6,7},{7,6},{8,9},{9,8},{10,11... | collective-permute-start | bytes 6291464 | tf_op jit(solution)/shard_map/ppermute | solution.py:32
  24.8 48.7 %collective-permute-start.12 = (bf16[2,2,1024,256]{3,2,1,0:T(8,128)(2,1)}, bf16[2,2,1024,256]{3,2,1,0:T(8,128)(2,1)}, u32[]{:S(2)}, u32[]{:S(2)}) collective-permute-start(bf16[2,2,1024,256]{3,2,1,0:T(8,128)(2,1)} %refs_11_.1), channel_id=1, source_target_pairs={{0,1},{1,0},{2,3},{3,2},{4,5},{5,4},{6,7},{7,6},{8,9},{9,8},{10,11... | collective-permute-start | bytes 6291464 | tf_op jit(solution)/shard_map/ppermute | solution.py:32
  33.0 12.3 %collective-permute-start.5 = (bf16[2,2,2,64,512]{4,3,2,1,0:T(8,128)(2,1)S(1)}, bf16[2,2,2,64,512]{4,3,2,1,0:T(8,128)(2,1)S(1)}, u32[]{:S(2)}, u32[]{:S(2)}) collective-permute-start(bf16[2,2,2,64,512]{4,3,2,1,0:T(8,128)(2,1)S(1)} %collective-permute-done.3.refs_1_), channel_id=1, source_target_pairs={{0,32},{32,64},{64,96},{96,128},{128,160},{160,192},{192,224},{224... | collective-permute-start | bytes 1572872 | tf_op jit(solution)/shard_map/ppermute | solution.py:27
  33.0 36.9 %copy-start = (bf16[2,2,2,64,512]{4,3,2,1,0:T(8,128)(2,1)}, bf16[2,2,2,64,512]{4,3,2,1,0:T(8,128)(2,1)S(1)}, u32[]{:S(2)}) copy-start(bf16[2,2,2,64,512]{4,3,2,1,0:T(8,128)(2,1)S(1)} %collective-permute-done.4.refs_2_) | copy-start | bytes 1572868
  33.0 12.3 %collective-permute-start.6 = (bf16[2,2,2,64,512]{4,3,2,1,0:T(8,128)(2,1)S(1)}, bf16[2,2,2,64,512]{4,3,2,1,0:T(8,128)(2,1)S(1)}, u32[]{:S(2)}, u32[]{:S(2)}) collective-permute-start(bf16[2,2,2,64,512]{4,3,2,1,0:T(8,128)(2,1)S(1)} %collective-permute-done.4.refs_2_), channel_id=1, source_target_pairs={{0,224},{32,0},{64,32},{96,64},{128,96},{160,128},{192,160},{224,1... | collective-permute-start | bytes 1572872 | tf_op jit(solution)/shard_map/ppermute | solution.py:27
  45.3 24.6 %copy-start.2 = (bf16[2,2,2,64,512]{4,3,2,1,0:T(8,128)(2,1)}, bf16[2,2,2,64,512]{4,3,2,1,0:T(8,128)(2,1)S(1)}, u32[]{:S(2)}) copy-start(bf16[2,2,2,64,512]{4,3,2,1,0:T(8,128)(2,1)S(1)} %collective-permute-done.5.refs_3_) | copy-start | bytes 1572868
  45.3 28.2 %collective-permute-start = (s32[2,2]{1,0:T(2,128)S(1)}, s32[2,2]{1,0:T(2,128)S(1)}, u32[]{:S(2)}, u32[]{:S(2)}) collective-permute-start(s32[2,2]{1,0:T(2,128)S(1)} %copy-done.12), channel_id=1, source_target_pairs={{0,1},{1,0},{2,3},{3,2},{4,5},{5,4},{6,7},{7,6},{8,9},{9,8},{10,11... | collective-permute-start | bytes 56 | tf_op jit(solution)/shard_map/ppermute | solution.py:32
  45.3 4.8 %copy-start.4 = (bf16[2,2,2,64,512]{4,3,2,1,0:T(8,128)(2,1)}, bf16[2,2,2,64,512]{4,3,2,1,0:T(8,128)(2,1)S(1)}, u32[]{:S(2)}) copy-start(bf16[2,2,2,64,512]{4,3,2,1,0:T(8,128)(2,1)S(1)} %collective-permute-done.6.refs_4_) | copy-start | bytes 1572868
  45.3 15.5 %collective-permute-start.7 = (bf16[2,2,2,64,512]{4,3,2,1,0:T(8,128)(2,1)S(1)}, bf16[2,2,2,64,512]{4,3,2,1,0:T(8,128)(2,1)S(1)}, u32[]{:S(2)}, u32[]{:S(2)}) collective-permute-start(bf16[2,2,2,64,512]{4,3,2,1,0:T(8,128)(2,1)S(1)} %collective-permute-done.5.refs_3_), channel_id=1, source_target_pairs={{0,32},{32,64},{64,96},{96,128},{128,160},{160,192},{192,224},{224... | collective-permute-start | bytes 1572872 | tf_op jit(solution)/shard_map/ppermute | solution.py:27
  45.4 15.5 %collective-permute-start.8 = (bf16[2,2,2,64,512]{4,3,2,1,0:T(8,128)(2,1)S(1)}, bf16[2,2,2,64,512]{4,3,2,1,0:T(8,128)(2,1)S(1)}, u32[]{:S(2)}, u32[]{:S(2)}) collective-permute-start(bf16[2,2,2,64,512]{4,3,2,1,0:T(8,128)(2,1)S(1)} %collective-permute-done.6.refs_4_), channel_id=1, source_target_pairs={{0,224},{32,0},{64,32},{96,64},{128,96},{160,128},{192,160},{224,1... | collective-permute-start | bytes 1572872 | tf_op jit(solution)/shard_map/ppermute | solution.py:27
  60.9 9.1 %collective-permute-start.9 = (bf16[1,2,2,64,512]{4,3,2,1,0:T(8,128)(2,1)S(1)}, bf16[1,2,2,64,512]{4,3,2,1,0:T(8,128)(2,1)S(1)}, u32[]{:S(2)}, u32[]{:S(2)}) collective-permute-start(bf16[1,2,2,64,512]{4,3,2,1,0:T(8,128)(2,1)S(1)} %slice.26), channel_id=1, source_target_pairs={{0,32},{32,64},{64,96},{96,128},{128,160},{160,192},{192,224},{224... | collective-permute-start | bytes 786440 | tf_op jit(solution)/shard_map/ppermute | solution.py:27
  61.0 8.9 %collective-permute-start.10 = (bf16[1,2,2,64,512]{4,3,2,1,0:T(8,128)(2,1)S(1)}, bf16[1,2,2,64,512]{4,3,2,1,0:T(8,128)(2,1)S(1)}, u32[]{:S(2)}, u32[]{:S(2)}) collective-permute-start(bf16[1,2,2,64,512]{4,3,2,1,0:T(8,128)(2,1)S(1)} %slice.27), channel_id=1, source_target_pairs={{0,224},{32,0},{64,32},{96,64},{128,96},{160,128},{192,160},{224,1... | collective-permute-start | bytes 786440 | tf_op jit(solution)/shard_map/ppermute | solution.py:27
  65.4 4.5 %copy-start.5 = (bf16[2,2,2,64,512]{4,3,2,1,0:T(8,128)(2,1)S(1)}, bf16[2,2,2,64,512]{4,3,2,1,0:T(8,128)(2,1)}, u32[]{:S(2)}) copy-start(bf16[2,2,2,64,512]{4,3,2,1,0:T(8,128)(2,1)} %copy-done.4) | copy-start | bytes 1572868
  65.4 4.5 %copy-start.11 = (s32[32]{0:T(128)S(1)}, s32[32]{0:T(128)}, u32[]{:S(2)}) copy-start(s32[32]{0:T(128)} %rank.3) | copy-start | bytes 388
  72.8 15.4 %collective-permute-start.23 = (bf16[4,256,128]{2,1,0:T(8,128)(2,1)S(1)}, bf16[4,256,128]{2,1,0:T(8,128)(2,1)S(1)}, u32[]{:S(2)}, u32[]{:S(2)}) collective-permute-start(bf16[4,256,128]{2,1,0:T(8,128)(2,1)S(1)} %dynamic-slice_bitcast_fusion), channel_id=1, source_target_pairs={{0,2},{1,3},{16,18},{17,19},{34,32},{35,33},{50,48},{51,49},{68,70... | collective-permute-start | bytes 786440 | tf_op jit(solution)/shard_map/ppermute | solution.py:330
  73.5 1.0 copy-start.1
  74.6 1.0 copy-start.3
  87.6 4.6 %copy-start.6 = (f32[1024,128]{1,0:T(8,128)}, f32[1024,128]{1,0:T(8,128)S(1)}, u32[]{:S(2)}) copy-start(f32[1024,128]{1,0:T(8,128)S(1)} %get-tuple-element.20) | copy-start | bytes 1572868
  87.6 4.6 %copy-start.8 = (f32[1024,128]{1,0:T(8,128)}, f32[1024,128]{1,0:T(8,128)S(1)}, u32[]{:S(2)}) copy-start(f32[1024,128]{1,0:T(8,128)S(1)} %get-tuple-element.19) | copy-start | bytes 1572868
  87.6 20.5 %collective-permute-start.13 = (bf16[2,1024,128]{2,1,0:T(8,128)(2,1)}, bf16[2,1024,128]{2,1,0:T(8,128)(2,1)S(1)}, u32[]{:S(2)}, u32[]{:S(2)}) collective-permute-start(bf16[2,1024,128]{2,1,0:T(8,128)(2,1)} %get-tuple-element.17), channel_id=1, source_target_pairs={{0,4},{4,8},{8,12},{12,0},{1,5},{5,9},{9,13},{13,1},{2,6},{6,10},{... | collective-permute-start | bytes 1572872 | tf_op jit(solution)/shard_map/ppermute | solution.py:27
  88.9 5.6 %collective-permute-start.26 = (bf16[256,128]{1,0:T(8,128)(2,1)}, bf16[256,128]{1,0:T(8,128)(2,1)S(1)}, u32[]{:S(2)}, u32[]{:S(2)}) collective-permute-start(bf16[256,128]{1,0:T(8,128)(2,1)} %get-tuple-element.28), channel_id=1, source_target_pairs={{0,12},{2,14},{1,13},{3,15},{16,28},{18,30},{17,29},{19,31},{32,44... | collective-permute-start | bytes 196616 | tf_op jit(solution)/shard_map/ppermute | solution.py:339
  89.6 14.3 %collective-permute-start.25 = (bf16[256,128]{1,0:T(8,128)(2,1)}, bf16[256,128]{1,0:T(8,128)(2,1)S(1)}, u32[]{:S(2)}, u32[]{:S(2)}) collective-permute-start(bf16[256,128]{1,0:T(8,128)(2,1)} %get-tuple-element.29), channel_id=1, source_target_pairs={{0,8},{2,10},{1,9},{3,11},{16,24},{18,26},{17,25},{19,27},{32,40},... | collective-permute-start | bytes 196616 | tf_op jit(solution)/shard_map/ppermute | solution.py:339
  90.9 13.0 %collective-permute-start.24 = (bf16[256,128]{1,0:T(8,128)(2,1)}, bf16[256,128]{1,0:T(8,128)(2,1)}, u32[]{:S(2)}, u32[]{:S(2)}) collective-permute-start(bf16[256,128]{1,0:T(8,128)(2,1)} %get-tuple-element.27), channel_id=1, source_target_pairs={{0,4},{2,6},{1,5},{3,7},{16,20},{18,22},{17,21},{19,23},{32,36},{3... | collective-permute-start | bytes 196616 | tf_op jit(solution)/shard_map/ppermute | solution.py:339
  92.2 16.1 %collective-permute-start.14 = (bf16[2,1024,128]{2,1,0:T(8,128)(2,1)}, bf16[2,1024,128]{2,1,0:T(8,128)(2,1)S(1)}, u32[]{:S(2)}, u32[]{:S(2)}) collective-permute-start(bf16[2,1024,128]{2,1,0:T(8,128)(2,1)} %get-tuple-element.18), channel_id=1, source_target_pairs={{0,12},{4,0},{8,4},{12,8},{1,13},{5,1},{9,5},{13,9},{2,14},{6,2},{... | collective-permute-start | bytes 1572872 | tf_op jit(solution)/shard_map/ppermute | solution.py:27
  93.1 14.9 %copy-start.9 = (f32[1024,128]{1,0:T(8,128)S(1)}, f32[1024,128]{1,0:T(8,128)}, u32[]{:S(2)}) copy-start(f32[1024,128]{1,0:T(8,128)} %copy-done.8) | copy-start | bytes 1572868
  93.2 15.1 %copy-start.7 = (f32[1024,128]{1,0:T(8,128)S(1)}, f32[1024,128]{1,0:T(8,128)}, u32[]{:S(2)}) copy-start(f32[1024,128]{1,0:T(8,128)} %copy-done.6) | copy-start | bytes 1572868
  105.2 6.6 %collective-permute-start.27 = (bf16[512,128]{1,0:T(8,128)(2,1)S(1)}, bf16[512,128]{1,0:T(8,128)(2,1)S(1)}, u32[]{:S(2)}, u32[]{:S(2)}) collective-permute-start(bf16[512,128]{1,0:T(8,128)(2,1)S(1)} %sweep_part.1), channel_id=1, source_target_pairs={{0,16},{16,0},{1,17},{17,1},{2,18},{18,2},{3,19},{19,3},{4,20},{20... | collective-permute-start | bytes 393224 | tf_op jit(solution)/shard_map/ppermute | solution.py:32
  108.2 11.1 %collective-permute-start.15 = (bf16[1024,128]{1,0:T(8,128)(2,1)S(1)}, bf16[1024,128]{1,0:T(8,128)(2,1)S(1)}, u32[]{:S(2)}, u32[]{:S(2)}) collective-permute-start(bf16[1024,128]{1,0:T(8,128)(2,1)S(1)} %fusion.5), channel_id=1, source_target_pairs={{0,4},{4,8},{8,12},{12,0},{1,5},{5,9},{9,13},{13,1},{2,6},{6,10},{... | collective-permute-start | bytes 786440 | tf_op jit(solution)/shard_map/ppermute | solution.py:27
  108.3 10.9 %collective-permute-start.16 = (bf16[1024,128]{1,0:T(8,128)(2,1)S(1)}, bf16[1024,128]{1,0:T(8,128)(2,1)S(1)}, u32[]{:S(2)}, u32[]{:S(2)}) collective-permute-start(bf16[1024,128]{1,0:T(8,128)(2,1)S(1)} %fusion.4), channel_id=1, source_target_pairs={{0,12},{4,0},{8,4},{12,8},{1,13},{5,1},{9,5},{13,9},{2,14},{6,2},{... | collective-permute-start | bytes 786440 | tf_op jit(solution)/shard_map/ppermute | solution.py:27
  111.8 5.8 %collective-permute-start.28 = (bf16[512,128]{1,0:T(8,128)(2,1)S(1)}, bf16[512,128]{1,0:T(8,128)(2,1)S(1)}, u32[]{:S(2)}, u32[]{:S(2)}) collective-permute-start(bf16[512,128]{1,0:T(8,128)(2,1)S(1)} %add.84), channel_id=1, source_target_pairs={{0,32},{32,0},{64,96},{96,64},{128,160},{160,128},{192,224},{224,1... | collective-permute-start | bytes 393224 | tf_op jit(solution)/shard_map/ppermute | solution.py:32
  117.6 9.6 %collective-permute-start.29 = (bf16[512,128]{1,0:T(8,128)(2,1)S(1)}, bf16[512,128]{1,0:T(8,128)(2,1)S(1)}, u32[]{:S(2)}, u32[]{:S(2)}) collective-permute-start(bf16[512,128]{1,0:T(8,128)(2,1)S(1)} %add.85), channel_id=1, source_target_pairs={{0,64},{32,96},{64,0},{96,32},{128,192},{160,224},{192,128},{224,1... | collective-permute-start | bytes 393224 | tf_op jit(solution)/shard_map/ppermute | solution.py:32
  120.2 19.0 %collective-permute-start.17 = (bf16[1024,128]{1,0:T(8,128)(2,1)S(1)}, bf16[1024,128]{1,0:T(8,128)(2,1)S(1)}, u32[]{:S(2)}, u32[]{:S(2)}) collective-permute-start(bf16[1024,128]{1,0:T(8,128)(2,1)S(1)} %get-tuple-element.22), channel_id=1, source_target_pairs={{0,2},{2,0},{1,3},{3,1},{4,6},{6,4},{5,7},{7,5},{8,10},{10,8},{9,1... | collective-permute-start | bytes 786440 | tf_op jit(solution)/shard_map/ppermute | solution.py:32
  127.3 10.4 %collective-permute-start.30 = (bf16[512,128]{1,0:T(8,128)(2,1)S(1)}, bf16[512,128]{1,0:T(8,128)(2,1)S(1)}, u32[]{:S(2)}, u32[]{:S(2)}) collective-permute-start(bf16[512,128]{1,0:T(8,128)(2,1)S(1)} %add.86), channel_id=1, source_target_pairs={{0,128},{32,160},{64,192},{96,224},{128,0},{160,32},{192,64},{224,... | collective-permute-start | bytes 393224 | tf_op jit(solution)/shard_map/ppermute | solution.py:32

commit v2 on v1

v2 whole, which is shorter than its diff:
```python
import jax
import jax.numpy as jnp
from jax import lax
from jax.experimental import pallas as pl
from jax.experimental.pallas import tpu as pltpu
from jax.sharding import Mesh
from jax.sharding import PartitionSpec as P

ALL = ("z", "xh", "y", "xl", "co")
ROW = ("z", "xh")
COL = ("y", "xl", "co")
BF = jnp.bfloat16
F32 = jnp.float32
ANY = pl.BlockSpec(memory_space=pl.ANY)
SMEM = pl.BlockSpec(memory_space=pltpu.SMEM)
VMEM = pl.BlockSpec(memory_space=pltpu.VMEM)


def move(a, axis, k):
    n = lax.axis_size(axis)
    return lax.ppermute(a, axis, [(i, (i + k) % n) for i in range(n)])


def swap(a, axis, k=1):
    n = lax.axis_size(axis)
    return lax.ppermute(a, axis, [(i, i ^ k) for i in range(n)])


def split_kernel(at, x_ref, mine_ref, theirs_ref):
    first = at[4] == 0
    for y in range(4):
        a = x_ref[:, :, 256 * y : 256 * y + 128]
        b = x_ref[:, :, 256 * y + 128 : 256 * y + 256]
        low = jnp.concatenate([a[..., :64], b[..., :64]], axis=-1)
        high = jnp.concatenate([a[..., 64:], b[..., 64:]], axis=-1)
        mine_ref[:, :, 128 * y : 128 * y + 128] = jnp.where(first, low, high)
        theirs_ref[:, :, 128 * y : 128 * y + 128] = jnp.where(first, high, low)


def split_columns(at, x):
    half = jax.ShapeDtypeStruct((2, 64, 512), BF)
    return pl.pallas_call(
        split_kernel,
        out_shape=(half, half),
        in_specs=[SMEM, VMEM],
        out_specs=(VMEM, VMEM),
        compiler_params=pltpu.CompilerParams(vmem_limit_bytes=8 << 20),
        name="split_columns",
    )(at, x)


EARLY = (
    (0, ((0, 0), (2, 1))),
    (-1, ((0, 0), (2, 1))),
    (1, ((0, 0), (2, 1))),
    (-2, ((0, 0), (2, 1))),
    (2, ((0, 0), (2, 1))),
    (-3, ((0, 0), (2, 1))),
    (3, ((0, 0), (2, 1))),
    (4, ((0, 0),)),
    (4, ((0, 1),)),
)
LATER = (
    (0, ((1, 0),)),
    (-1, ((1, 0),)),
    (1, ((1, 0),)),
    (-2, ((1, 0),)),
    (2, ((1, 0),)),
    (-3, ((1, 0),)),
    (3, ((1, 0),)),
    (4, ((1, 0),)),
)
CROSS = (((0, 0), (1, -1), (2, 1)), ((0, -2), (1, 2)), ((0, -3), (1, 3)), ((0, 4),))


def row_of(at, step, other):
    rows = lax.rem(at[0] + step + 8, 8) * 128 + (1 - at[1] if other else at[1]) * 64
    return pl.multiple_of(rows, 64)


def copies_early(at, refs, x_s, sem):
    return [
        pltpu.make_async_copy(ref.at[n], x_s.at[:, pl.ds(row_of(at, step, other), 64), :], sem)
        for ref, (step, blocks) in zip(refs, EARLY)
        for n, other in blocks
    ]


def copies_later(at, refs, crossed, x_s, sem):
    found = [
        pltpu.make_async_copy(ref.at[n], x_s.at[:, pl.ds(row_of(at, step, other), 64), :], sem)
        for ref, (step, blocks) in zip(refs, LATER, strict=True)
        for n, other in blocks
    ]
    return found + [
        pltpu.make_async_copy(ref.at[n], x_s.at[:, pl.ds(row_of(at, step, 1), 64), :], sem)
        for ref, blocks in zip(crossed, CROSS, strict=True)
        for n, step in blocks
    ]


def early_kernel(at, *refs):
    u_ref, out_ref, x_s, sem = refs[7:]
    copies = copies_early(at, refs[:7], x_s, sem)
    for c in copies:
        c.start()
    x_s[:, pl.ds(pl.multiple_of(lax.rem(at[0] + 4, 8) * 128, 128), 128), :] = jnp.zeros((2, 128, 512), BF)
    for c in copies:
        c.wait()
    for j in range(2):
        out_ref[j] = lax.dot_general(u_ref[j], x_s[j], (((0,), (0,)), ((), ())), preferred_element_type=F32)


def project_early(at, messages, u):
    return pl.pallas_call(
        early_kernel,
        out_shape=jax.ShapeDtypeStruct((2, 256, 512), F32),
        in_specs=[SMEM] + [ANY] * 7 + [VMEM],
        out_specs=VMEM,
        scratch_shapes=[pltpu.VMEM((2, 1024, 512), BF), pltpu.SemaphoreType.DMA(())],
        compiler_params=pltpu.CompilerParams(vmem_limit_bytes=16 << 20),
        cost_estimate=pl.CostEstimate(flops=2 * 2 * 256 * 1024 * 512, bytes_accessed=4 << 20, transcendentals=0),
        name="project_early",
    )(at, *messages, u)


def proj_kernel(at, rank, a_ref, b_ref, u_ref, early_ref, mine_ref, other_ref, x_s, u_s, sem):
    rows = pl.multiple_of(lax.rem(at[0] + 4, 8) * 128, 128)
    copies = [
        pltpu.make_async_copy(a_ref.at[0], x_s.at[:, pl.ds(pl.multiple_of(64 * at[1], 64), 64), :], sem),
        pltpu.make_async_copy(b_ref.at[0], x_s.at[:, pl.ds(pl.multiple_of(64 - 64 * at[1], 64), 64), :], sem),
        pltpu.make_async_copy(u_ref.at[:, pl.ds(rows, 128), :], u_s, sem),
    ]
    for c in copies:
        c.start()
    for c in copies:
        c.wait()
    slot = lax.broadcasted_iota(jnp.int32, (256, 1), 0)
    both = []
    for j in range(2):
        p = lax.dot_general(u_s[j], x_s[j], (((0,), (0,)), ((), ())), preferred_element_type=F32) + early_ref[j]
        both.append(jnp.where(slot < rank[2 * (2 * at[0] + at[1]) + j], p, 0.0))
    for y in range(4):
        a, b = (p[:, 128 * y : 128 * y + 128] for p in both)
        low = jnp.concatenate([a[:, :64], b[:, :64]], axis=-1).astype(BF)
        high = jnp.concatenate([a[:, 64:], b[:, 64:]], axis=-1).astype(BF)
        mine_ref[y] = jnp.where(at[3] == 0, low, high)
        other_ref[y] = jnp.where(at[3] == 0, high, low)


def project(at, panel_rank, a, b, u, early):
    return pl.pallas_call(
        proj_kernel,
        out_shape=(jax.ShapeDtypeStruct((4, 256, 128), BF),) * 2,
        in_specs=[SMEM, SMEM, ANY, ANY, ANY, VMEM],
        out_specs=(VMEM, VMEM),
        scratch_shapes=[
            pltpu.VMEM((2, 128, 512), BF),
            pltpu.VMEM((2, 128, 256), BF),
            pltpu.SemaphoreType.DMA(()),
        ],
        compiler_params=pltpu.CompilerParams(vmem_limit_bytes=4 << 20),
        cost_estimate=pl.CostEstimate(flops=2 * 2 * 256 * 128 * 512, bytes_accessed=2 << 20, transcendentals=0),
        name="project",
    )(at, panel_rank, a, b, u, early)


def part_kernel(p_ref, v_ref, out_ref):
    lane = lax.broadcasted_iota(jnp.int32, (1, 128), 1)
    p = p_ref[...]
    zero = jnp.zeros_like(p)
    s = jnp.dot(v_ref[0], jnp.where(lane < 64, p, zero), preferred_element_type=F32)
    s += jnp.dot(v_ref[1], jnp.where(lane < 64, zero, p), preferred_element_type=F32)
    s += jnp.concatenate([s[:, 64:], s[:, :64]], axis=-1)
    out_ref[...] = jnp.where(lane < 64, s[:512], s[512:]).astype(BF)


def sweep_part(p, v):
    return pl.pallas_call(
        part_kernel,
        out_shape=jax.ShapeDtypeStruct((512, 128), BF),
        in_specs=[VMEM, VMEM],
        out_specs=VMEM,
        compiler_params=pltpu.CompilerParams(vmem_limit_bytes=8 << 20),
        cost_estimate=pl.CostEstimate(flops=2 * 2 * 256 * 1024 * 128, bytes_accessed=2 << 20, transcendentals=0),
        name="sweep_part",
    )(p, v)


def base_kernel(at, rank_a, rank_b, *refs):
    messages, crossed = refs[:9], refs[9:13]
    qa, qb, pa, pb = refs[13:17]
    plus_ref, minus_ref, own_ref, next_ref, prev_ref = refs[17:22]
    x_s, q_s, p_s, t_s, stage, sem, q_sem, p_sem, o_sem = refs[22:]
    same = at[4] == at[1]
    x_copies = (
        copies_early(at, messages, x_s.at[0], sem.at[0]),
        copies_later(at, messages[:8], crossed, x_s.at[1], sem.at[1]),
    )

    def tile(ref, to, sems, h, i):
        return pltpu.make_async_copy(ref.at[i], to.at[2 * h + i], sems.at[2 * h + i])

    def fetch(h, a, b, to, sems):
        mine = same == (h == 0)

        @pl.when(mine)
        def _():
            for i in range(2):
                tile(a, to, sems, h, i).start()

        @pl.when(jnp.logical_not(mine))
        def _():
            for i in range(2):
                tile(b, to, sems, h, i).start()

    for h in range(2):
        for c in x_copies[h]:
            c.start()
        fetch(h, qa, qb, q_s, q_sem)
    for h in range(2):
        fetch(h, pa, pb, p_s, p_sem)
    slot = lax.broadcasted_iota(jnp.int32, (256, 1), 0)
    for h in range(2):
        mine = same == (h == 0)
        for c in x_copies[h]:
            c.wait()
        for i in range(2):
            tile(qa, q_s, q_sem, h, i).wait()
            for j in range(2):
                t = lax.dot_general(
                    q_s[2 * h + i, j], x_s[h, j], (((0,), (0,)), ((), ())), preferred_element_type=F32
                )
                rank = jnp.where(mine, rank_a[i, j], rank_b[i, j])
                t = jnp.where(slot < rank, t, 0.0).astype(BF)
                for y in range(4):
                    lanes = pl.multiple_of(lax.rem(y + 4 - at[2], 4) * 128, 128)
                    t_s[i, 2 * h + j, :, pl.ds(lanes, 128)] = t[:, 128 * y : 128 * y + 128]
    outs = (
        ((plus_ref.at[0], 2), (minus_ref.at[1], 3), (own_ref.at[0], 0), (next_ref, 1)),
        ((plus_ref.at[1], 1), (minus_ref.at[0], 2), (own_ref.at[1], 0), (prev_ref, 3)),
    )
    leaving = []
    for i in range(2):
        for h in range(2):
            tile(pa, p_s, p_sem, h, i).wait()
        for k in range(4):
            rows = slice(256 * k, 256 * k + 256)
            u = sum(
                jnp.dot(p_s[2 * h + i, j, rows], t_s[i, 2 * h + j], preferred_element_type=F32)
                for h in range(2)
                for j in range(2)
            )
            for n, (ref, d) in enumerate(outs[i]):
                stage[i, n, rows] = u[:, 128 * d : 128 * d + 128].astype(BF)
                leaving.append(pltpu.make_async_copy(stage.at[i, n, rows], ref.at[rows], o_sem))
                leaving[-1].start()
    for c in leaving:
        c.wait()


def base(at, rank_a, rank_b, *operands):
    two, one = (jax.ShapeDtypeStruct(n, BF) for n in ((2, 1024, 128), (1024, 128)))
    return pl.pallas_call(
        base_kernel,
        out_shape=(two, two, two, one, one),
        in_specs=[SMEM, SMEM, SMEM] + [ANY] * 17,
        out_specs=(ANY,) * 5,
        scratch_shapes=[
            pltpu.VMEM((2, 2, 1024, 512), BF),
            pltpu.VMEM((4, 2, 1024, 256), BF),
            pltpu.VMEM((4, 2, 1024, 256), BF),
            pltpu.VMEM((2, 4, 256, 512), BF),
            pltpu.VMEM((2, 4, 1024, 128), BF),
            pltpu.SemaphoreType.DMA((2,)),
            pltpu.SemaphoreType.DMA((4,)),
            pltpu.SemaphoreType.DMA((4,)),
            pltpu.SemaphoreType.DMA(()),
        ],
        compiler_params=pltpu.CompilerParams(vmem_limit_bytes=60 << 20),
        cost_estimate=pl.CostEstimate(flops=8 * 2 * 2 * 256 * 1024 * 512, bytes_accessed=15 << 20, transcendentals=0),
        name="base",
    )(at, rank_a, rank_b, *operands)


def pack_kernel(at, own_ref, plus_ref, minus_ref, low_ref, high_ref, keep_ref, send_ref):
    lane = lax.broadcasted_iota(jnp.int32, (1, 128), 1)
    a = own_ref[0].astype(F32) + minus_ref[1].astype(F32) + low_ref[...].astype(F32)
    b = own_ref[1].astype(F32) + plus_ref[1].astype(F32) + high_ref[...].astype(F32)
    turn = lambda v: jnp.concatenate([v[:, 64:], v[:, :64]], axis=-1)
    low = jnp.where(lane < 64, a, turn(b))
    high = jnp.where(lane < 64, turn(a), b)
    first = at[3] == 0
    keep_ref[...] = jnp.where(first, low, high)
    send_ref[...] = jnp.where(first, high, low).astype(BF)


def pack(at, own, plus, minus, low, high):
    return pl.pallas_call(
        pack_kernel,
        out_shape=(jax.ShapeDtypeStruct((1024, 128), F32), jax.ShapeDtypeStruct((1024, 128), BF)),
        in_specs=[SMEM] + [VMEM] * 5,
        out_specs=(VMEM, VMEM),
        compiler_params=pltpu.CompilerParams(vmem_limit_bytes=12 << 20),
        name="pack",
    )(at, own, plus, minus, low, high)


def last_kernel(at, rank, s_ref, u_ref, v_ref, keep_ref, came_ref, out_ref):
    lane = lax.broadcasted_iota(jnp.int32, (1, 128), 1)
    slot = lax.broadcasted_iota(jnp.int32, (256, 1), 0)
    packed = s_ref[...].astype(F32)
    turned = jnp.concatenate([packed[:, 64:], packed[:, :64]], axis=-1)
    s = jnp.concatenate([jnp.where(lane < 64, packed, turned), jnp.where(lane < 64, turned, packed)], axis=0)
    s = s.astype(BF)
    v = keep_ref[...] + came_ref[...].astype(F32)
    for i in range(2):
        back = lax.dot_general(v_ref[i], s, (((0,), (0,)), ((), ())), preferred_element_type=F32)
        keep = jnp.logical_and(slot < rank[2 * (2 * at[0] + at[1]) + i], (lane < 64) == (i == 0))
        back = jnp.where(keep, back, 0.0).astype(BF)
        v -= jnp.dot(u_ref[i], back, preferred_element_type=F32)
    t = v.T.astype(BF)
    out_ref[0] = t[:64]
    out_ref[1] = t[64:]


def last(at, panel_rank, s, u, v, keep, came):
    return pl.pallas_call(
        last_kernel,
        out_shape=jax.ShapeDtypeStruct((2, 64, 1024), BF),
        in_specs=[SMEM, SMEM] + [VMEM] * 5,
        out_specs=VMEM,
        compiler_params=pltpu.CompilerParams(vmem_limit_bytes=12 << 20),
        name="last",
    )(at, panel_rank, s, u, v, keep, came)


def panel_kernel(at, *refs):
    held, (u_ref, v_ref, sem) = refs[:8], refs[8:]
    copies = []
    for n, ref in enumerate(held):
        y = lax.rem(at[2] + n % 4, 4)
        co = at[4] if n < 4 else 1 - at[4]
        for m in range(2):
            xl = at[3] if m == 0 else 1 - at[3]
            rows = pl.multiple_of(y * 256 + xl * 128 + co * 64, 64)
            for f, out in enumerate((u_ref, v_ref)):
                copies.append(pltpu.make_async_copy(ref.at[m, f], out.at[:, pl.ds(rows, 64), :], sem))
    for c in copies:
        c.start()
    for c in copies:
        c.wait()


def whole_panel(at, u, v):
    both = jnp.stack([u, v])
    pair = jnp.stack([both, swap(both, "xl")])
    before = move(pair, "y", 1)
    after = move(pair, "y", -1)
    far = move(before, "y", 1)
    held = [pair, after, far, before]
    held += [swap(a, "co") for a in held]
    whole = jax.ShapeDtypeStruct((2, 1024, 256), BF)
    return pl.pallas_call(
        panel_kernel,
        out_shape=(whole, whole),
        in_specs=[SMEM] + [ANY] * 8,
        out_specs=(VMEM, ANY),
        scratch_shapes=[pltpu.SemaphoreType.DMA(())],
        compiler_params=pltpu.CompilerParams(vmem_limit_bytes=4 << 20),
        cost_estimate=pl.CostEstimate(flops=0, bytes_accessed=4 << 20, transcendentals=0),
        name="whole_panel",
    )(at, *held)


def shards(x_rhs, panel_u, panel_v, panel_rank, tile_p, tile_q, tile_rank):
    z, xh, y, xl, co = (lax.axis_index(a) for a in ALL)
    at = jnp.stack([z, xh, y, xl, co]).astype(jnp.int32)

    mine, theirs = split_columns(at, x_rhs)
    came = swap(theirs, "co")
    same = co == xh
    first, second = jnp.where(same, mine, came), jnp.where(same, came, mine)
    own = jnp.stack([first, second, swap(second, "xh")])
    p1, m1 = move(own, "z", 1), move(own, "z", -1)
    p2, m2 = move(p1, "z", 1), move(m1, "z", -1)
    p3, m3 = move(p2, "z", 1), move(m2, "z", -1)
    p4, m4 = move(p3[:2], "z", 1), move(m3[2:], "z", -1)
    messages = (own, p1, m1, p2, m2, p3, m3, p4, m4)
    crossed = (
        swap(jnp.stack([own[0], p1[0], m1[0]]), "xh"),
        swap(jnp.stack([p2[0], m2[0]]), "xh"),
        swap(jnp.stack([p3[0], m3[0]]), "xh"),
        swap(p4[:1], "xh"),
    )
    qb = swap(tile_q, "co")
    pb = swap(tile_p, "co")
    rank_b = swap(tile_rank, "co")
    u, v = whole_panel(at, panel_u, panel_v)

    early = project_early(at, messages[:7], u)
    row, other = project(at, panel_rank, p4, m4, u, early)
    n_z, n_h, n_y, n_l, n_c = (lax.axis_size(a) for a in ALL)

    def device(a, b, c, d, e):
        return (((a * n_h + b) * n_y + c) * n_l + d) * n_c + e

    spread = [(a, b, e) for a in range(n_z) for b in range(n_h) for e in range(n_c)]
    pairs = [(device(a, b, a >> 1, a & 1, e), device(a, b, a >> 1, 1 - (a & 1), e)) for a, b, e in spread]
    got = lax.ppermute(other, ALL, pairs)
    row = jnp.where(xl == lax.rem(z, 2), row, got)
    high = y // 2
    pairs = [
        (device(a, b, a >> 1, f, e), device(a, b, (a >> 1) ^ 2, f, e)) for a, b, e in spread for f in range(n_l)
    ]
    got = lax.ppermute(lax.dynamic_slice_in_dim(row, 2 - 2 * high, 2, 0), ALL, pairs)
    two = jnp.where(y == z // 2, lax.dynamic_slice_in_dim(row, 2 * high, 2, 0), got)
    low = lax.rem(y, 2)
    pairs = [
        (device(a, b, (a >> 1) ^ g, f, e), device(a, b, (a >> 1) ^ g ^ 1, f, e))
        for a, b, e in spread
        for f in range(n_l)
        for g in (0, 2)
    ]
    got = lax.ppermute(lax.dynamic_index_in_dim(two, 1 - low, 0, False), ALL, pairs)
    block = jnp.where(low == lax.rem(z // 2, 2), lax.dynamic_index_in_dim(two, low, 0, False), got)
    s = sweep_part(block, v)
    s = s + swap(s, "xh")
    right = move(s, "z", -1)
    pair = s + right
    near = pair + move(s, "z", 1)
    s = near + move(near, "z", -3) + move(pair, "z", 3)

    tiles = (tile_q, qb, tile_p, pb)
    operands = (*messages, *crossed, *tiles)
    plus, minus, own_sum, after, before = base(at, tile_rank, rank_b, *operands)
    plus, minus = move(plus, "y", 1), move(minus, "y", -1)
    up = move(after + plus[0], "y", 1)
    down = move(before + minus[0], "y", -1)
    keep, away = pack(at, own_sum, plus, minus, up, down)
    out = last(at, panel_rank, s, u, v, keep, swap(away, "xl"))
    return out.swapaxes(1, 2)


def solution(mesh):
    finer = Mesh(mesh.devices.reshape(8, 2, 4, 2, 2), ALL)
    return jax.shard_map(
        shards,
        mesh=finer,
        in_specs=(
            P(COL, ROW, None),
            P(ROW, COL, None),
            P(ROW, COL, None),
            P(),
            P(ROW, COL, None, None),
            P(ROW, COL, None, None),
            P(ROW, COL),
        ),
        out_specs=P(ROW, None, COL),
        check_vma=False,
    )
```

time: 141 us -> 145 us (1.028)
  starting transfers between devices: 42.5 us -> 62.9 us
  waiting for transfers between devices: 64.7 us -> 52.1 us
  other arithmetic: 6.77 us -> 3.02 us
  local copies, waits for them, and re-layouts: 6.54 us -> 4.29 us
  Pallas kernels: 19.2 us -> 21 us
    ppermute x19 -> x22, starting transfers between devices: 27.1 us -> 43.9 us  [the longest x19 37.1 us: move(): return lax.ppermute(a, axis, [(i, (i + k) % n) for i in range(n)])]
    ppermute x19 -> x22, waiting for transfers between devices: 42.6 us -> 30.2 us  [the longest x19 28 us: move(): return lax.ppermute(a, axis, [(i, (i + k) % n) for i in range(n)])]
    ppermute x12 -> x16, starting transfers between devices: 15.3 us -> 19 us  [swap(): return lax.ppermute(a, axis, [(i, i ^ k) for i in range(n)])]
    another operation x7 -> x6, other arithmetic: 4.53 us -> 1.82 us  [the longest x2 0.92 us: whole_panel(): pair = jnp.stack([both, swap(both, 'xl')])]
    pallas_call x1, Pallas kernels: 0.87 us -> 2.63 us  [last(): pl.pallas_call(last_kernel, out_shape=jax.ShapeDtypeStruct((2, 64, 1024),...]
    unnamed x28 -> x40, local copies, waits for them, and re-layouts: 3.07 us -> 1.64 us
    ppermute x12 -> x16, waiting for transfers between devices: 22.1 us -> 21.9 us  [swap(): return lax.ppermute(a, axis, [(i, i ^ k) for i in range(n)])]
    pallas_call x3 -> x4, Pallas kernels: 16.2 us -> 16.3 us  [the longest x1 10.3 us: base(): pl.pallas_call(base_kernel, out_shape=(two, two, two, one, one), in_specs...]
  transfers between devices with their start and end apart: 31 -> 38, of which waited for: 12 -> 16; matrix products, arithmetic and copies ran while one was open for 7% -> 4% of each run, Pallas kernels for 13% -> 12%
where the time goes in v2:
time: 145 us; the launch traced here: 144 us
  starting transfers between devices  62.9 us (43%)
  waiting for transfers between devices  52.1 us (36%)
  Pallas kernels  21 us (14%)
  local copies, waits for them, and re-layouts  4.29 us (3%)
  other arithmetic  3.02 us (2%)
    ppermute x19, starting transfers between devices, move(): return lax.ppermute(a, axis, [(i, (i + k) % n) for i in range(n)])  37.1 us
    ppermute x19, waiting for transfers between devices, move(): return lax.ppermute(a, axis, [(i, (i + k) % n) for i in range(n)])  28 us
    ppermute x16, waiting for transfers between devices, swap(): return lax.ppermute(a, axis, [(i, i ^ k) for i in range(n)])  21.9 us
    ppermute x16, starting transfers between devices, swap(): return lax.ppermute(a, axis, [(i, i ^ k) for i in range(n)])  19 us
    pallas_call x1, Pallas kernels, base(): pl.pallas_call(base_kernel, out_shape=(two, two, two, one, one), in_specs...  10.3 us
    ppermute x1, starting transfers between devices, shards(): lax.ppermute(lax.dynamic_index_in_dim(two, 1 - low, 0, False), ALL, pairs)  4.11 us
  transfers between devices with their start and end apart: 38, of which 16 were waited for; matrix products, arithmetic and copies ran while one was open for 4% of the time, Pallas kernels for 12%

profile of v2, /device:TPU:16, one launch (start us, length us, event | category | flops | bytes accessed | tf_op | source)
XLA Modules:
  0.0 143.8 jit_solution(15988029550266444427)
XLA Ops:
  0.0 0.1 stack.62.at
  0.1 0.9 copy-done.9
  1.0 0.7 split_columns.1
  1.7 0.1 collective-permute-start
  1.8 0.9 fusion.4
  2.7 1.6 %collective-permute-start.10 = (bf16[2,2,64,256]{3,2,1,0:T(8,128)(2,1)S(1)}, bf16[2,2,64,256]{3,2,1,0:T(8,128)(2,1)S(1)}, u32[]{:S(2)}, u32[]{:S(2)}) collective-permute-start(bf16[2,2,64,256]{3,2,1,0:T(8,128)(2,1)S(1)} %get-tuple-element.38), channel_id=1, source_target_pairs={{0,2},{2,0},{1,3},{3,1},{4,6},{6,4},{5,7},{7,5},{8,10},{10,8},{9,1... | collective-permute-start | bytes 393224 | tf_op jit(solution)/shard_map/ppermute | solution.py:26
  4.3 2.8 %collective-permute-start.1 = (bf16[2,64,512]{2,1,0:T(8,128)(2,1)S(1)}, bf16[2,64,512]{2,1,0:T(8,128)(2,1)S(1)}, u32[]{:S(2)}, u32[]{:S(2)}) collective-permute-start(bf16[2,64,512]{2,1,0:T(8,128)(2,1)S(1)} %get-tuple-element.35), channel_id=1, source_target_pairs={{0,16},{16,0},{1,17},{17,1},{2,18},{18,2},{3,19},{19,3},{4,20},{20... | collective-permute-start | bytes 393224 | tf_op jit(solution)/shard_map/ppermute | solution.py:26
  7.2 2.0 %collective-permute-done.10 = bf16[2,2,64,256]{3,2,1,0:T(8,128)(2,1)S(1)} collective-permute-done((bf16[2,2,64,256]{3,2,1,0:T(8,128)(2,1)S(1)}, bf16[2,2,64,256]{3,2,1,0:T(8,128)(2,1)S(1)}, u32[]{:S(2)}, u32[]{:S(2)}) %collective-permute-start.10) | collective-permute-done | bytes 131104 | tf_op jit(solution)/shard_map/ppermute | solution.py:26
  9.2 1.4 collective-permute-start.12
  10.6 3.1 %collective-permute-done.1 = bf16[2,64,512]{2,1,0:T(8,128)(2,1)S(1)} collective-permute-done((bf16[2,64,512]{2,1,0:T(8,128)(2,1)S(1)}, bf16[2,64,512]{2,1,0:T(8,128)(2,1)S(1)}, u32[]{:S(2)}, u32[]{:S(2)}) %collective-permute-start.1) | collective-permute-done | bytes 131104 | tf_op jit(solution)/shard_map/ppermute | solution.py:26
  13.8 2.0 %collective-permute-start.2 = (bf16[3,2,64,512]{3,2,1,0:T(8,128)(2,1)S(1)}, bf16[3,2,64,512]{3,2,1,0:T(8,128)(2,1)S(1)}, u32[]{:S(2)}, u32[]{:S(2)}) collective-permute-start(bf16[3,2,64,512]{3,2,1,0:T(8,128)(2,1)S(1)} %fusion.refs_0_), channel_id=1, source_target_pairs={{0,32},{32,64},{64,96},{96,128},{128,160},{160,192},{192,224},{224... | collective-permute-start | bytes 1179656 | tf_op jit(solution)/shard_map/ppermute | solution.py:21
  15.8 4.0 %collective-permute-start.6 = (bf16[3,2,64,512]{3,2,1,0:T(8,128)(2,1)S(1)}, bf16[3,2,64,512]{3,2,1,0:T(8,128)(2,1)S(1)}, u32[]{:S(2)}, u32[]{:S(2)}) collective-permute-start(bf16[3,2,64,512]{3,2,1,0:T(8,128)(2,1)S(1)} %fusion.refs_0_), channel_id=1, source_target_pairs={{0,224},{32,0},{64,32},{96,64},{128,96},{160,128},{192,160},{224,1... | collective-permute-start | bytes 1179656 | tf_op jit(solution)/shard_map/ppermute | solution.py:21
  19.8 0.4 collective-permute-start.11
  20.2 0.5 collective-permute-start.32
  20.8 7.9 %collective-permute-done.2.refs_1_ = bf16[3,2,64,512]{3,2,1,0:T(8,128)(2,1)S(1)} collective-permute-done((bf16[3,2,64,512]{3,2,1,0:T(8,128)(2,1)S(1)}, bf16[3,2,64,512]{3,2,1,0:T(8,128)(2,1)S(1)}, u32[]{:S(2)}, u32[]{:S(2)}) %collective-permute-start.2) | collective-permute-done | bytes 393248 | tf_op jit(solution)/shard_map/ppermute | solution.py:21
  28.6 0.1 collective-permute-start.14
  28.7 3.2 %collective-permute-start.7 = (bf16[3,2,64,512]{3,2,1,0:T(8,128)(2,1)S(1)}, bf16[3,2,64,512]{3,2,1,0:T(8,128)(2,1)S(1)}, u32[]{:S(2)}, u32[]{:S(2)}) collective-permute-start(bf16[3,2,64,512]{3,2,1,0:T(8,128)(2,1)S(1)} %collective-permute-done.6.refs_2_), channel_id=1, source_target_pairs={{0,224},{32,0},{64,32},{96,64},{128,96},{160,128},{192,160},{224,1... | collective-permute-start | bytes 1179656 | tf_op jit(solution)/shard_map/ppermute | solution.py:21
  32.0 1.3 collective-permute-start.13
  33.2 6.7 %collective-permute-done.3.refs_3_ = bf16[3,2,64,512]{3,2,1,0:T(8,128)(2,1)S(1)} collective-permute-done((bf16[3,2,64,512]{3,2,1,0:T(8,128)(2,1)S(1)}, bf16[3,2,64,512]{3,2,1,0:T(8,128)(2,1)S(1)}, u32[]{:S(2)}, u32[]{:S(2)}) %collective-permute-start.3) | collective-permute-done | bytes 393248 | tf_op jit(solution)/shard_map/ppermute | solution.py:21
  39.9 1.0 collective-permute-done.7.refs_4_
  40.9 3.7 %collective-permute-start.8 = (bf16[3,2,64,512]{3,2,1,0:T(8,128)(2,1)S(1)}, bf16[3,2,64,512]{3,2,1,0:T(8,128)(2,1)S(1)}, u32[]{:S(2)}, u32[]{:S(2)}) collective-permute-start(bf16[3,2,64,512]{3,2,1,0:T(8,128)(2,1)S(1)} %collective-permute-done.7.refs_4_), channel_id=1, source_target_pairs={{0,224},{32,0},{64,32},{96,64},{128,96},{160,128},{192,160},{224,1... | collective-permute-start | bytes 1179656 | tf_op jit(solution)/shard_map/ppermute | solution.py:21
  44.6 5.7 %collective-permute-done.4.refs_5_ = bf16[3,2,64,512]{3,2,1,0:T(8,128)(2,1)S(1)} collective-permute-done((bf16[3,2,64,512]{3,2,1,0:T(8,128)(2,1)S(1)}, bf16[3,2,64,512]{3,2,1,0:T(8,128)(2,1)S(1)}, u32[]{:S(2)}, u32[]{:S(2)}) %collective-permute-start.4) | collective-permute-done | bytes 393248 | tf_op jit(solution)/shard_map/ppermute | solution.py:21
  50.4 0.8 collective-permute-start.16
  51.2 1.5 %collective-permute-done.8.refs_6_ = bf16[3,2,64,512]{3,2,1,0:T(8,128)(2,1)S(1)} collective-permute-done((bf16[3,2,64,512]{3,2,1,0:T(8,128)(2,1)S(1)}, bf16[3,2,64,512]{3,2,1,0:T(8,128)(2,1)S(1)}, u32[]{:S(2)}, u32[]{:S(2)}) %collective-permute-start.8) | collective-permute-done | bytes 393248 | tf_op jit(solution)/shard_map/ppermute | solution.py:21
  52.7 0.8 collective-permute-start.5
  53.5 3.0 %collective-permute-start.9 = (bf16[1,2,64,512]{3,2,1,0:T(8,128)(2,1)S(1)}, bf16[1,2,64,512]{3,2,1,0:T(8,128)(2,1)S(1)}, u32[]{:S(2)}, u32[]{:S(2)}) collective-permute-start(bf16[1,2,64,512]{3,2,1,0:T(8,128)(2,1)S(1)} %get-tuple-element.34), channel_id=1, source_target_pairs={{0,224},{32,0},{64,32},{96,64},{128,96},{160,128},{192,160},{224,1... | collective-permute-start | bytes 393224 | tf_op jit(solution)/shard_map/ppermute | solution.py:21
  56.5 0.8 fusion.1
  57.3 0.8 collective-permute-start.27
  58.1 2.1 %whole_panel.1 = (bf16[2,1024,256]{2,1,0:T(8,128)(2,1)S(1)}, bf16[2,1024,256]{2,1,0:T(8,128)(2,1)S(1)}) custom-call(s32[5]{0:T(128)S(1)} %stack.62.at, bf16[2,2,2,64,256]{4,3,2,1,0:T(8,128)(2,1)S(1)} %pad_maximum_fusion.2.refs_0_, bf16[2,2,2,64,256]{4,3,2,1,0:T(8,128)(2,1)S(1)} %collective-permute-done.11.refs_1_, ...), custom_call_target="tpu_custom_call" | custom-call | bytes 4194304 | tf_op jit(solution)/shard_map/whole_panel/pallas_call | solution.py:364
  60.3 2.6 %project_early.1.early_ref = f32[2,256,512]{2,1,0:T(8,128)S(1)} custom-call(s32[5]{0:T(128)S(1)} %stack.62.at, bf16[3,2,64,512]{3,2,1,0:T(8,128)(2,1)S(1)} %fusion.refs_0_, bf16[3,2,64,512]{3,2,1,0:T(8,128)(2,1)S(1)} %collective-permute-done.2.refs_1_, bf16[3,2,64,512]{3,2,1,0:T(8,128)(2,1)S(1)} %collective-permute-done.6.refs_2_, ...), custom_call_target="tpu_custom_call" | custom-call | flops 536870912 | bytes 4194304 | tf_op jit(solution)/shard_map/project_early/pallas_call | solution.py:115
  63.0 0.0 copy-start.7
  63.0 1.3 project.1
  64.3 1.4 collective-permute-start.18
  65.7 0.9 slice.48
  66.6 0.9 slice.49
  67.7 2.9 %collective-permute-start.28 = (bf16[2,2,64,512]{3,2,1,0:T(8,128)(2,1)S(1)}, bf16[2,2,64,512]{3,2,1,0:T(8,128)(2,1)S(1)}, u32[]{:S(2)}, u32[]{:S(2)}) collective-permute-start(bf16[2,2,64,512]{3,2,1,0:T(8,128)(2,1)S(1)} %pad_maximum_fusion.3), channel_id=1, source_target_pairs={{0,16},{16,0},{1,17},{17,1},{2,18},{18,2},{3,19},{19,3},{4,20},{20... | collective-permute-start | bytes 786440 | tf_op jit(solution)/shard_map/ppermute | solution.py:26
  70.5 0.8 collective-permute-start.29
  71.3 2.8 %collective-permute-start.30 = (bf16[1,2,64,512]{3,2,1,0:T(8,128)(2,1)S(1)}, bf16[1,2,64,512]{3,2,1,0:T(8,128)(2,1)S(1)}, u32[]{:S(2)}, u32[]{:S(2)}) collective-permute-start(bf16[1,2,64,512]{3,2,1,0:T(8,128)(2,1)S(1)} %slice.52), channel_id=1, source_target_pairs={{0,16},{16,0},{1,17},{17,1},{2,18},{18,2},{3,19},{19,3},{4,20},{20... | collective-permute-start | bytes 393224 | tf_op jit(solution)/shard_map/ppermute | solution.py:26
  74.1 4.3 %collective-permute-done.28.refs_10_ = bf16[2,2,64,512]{3,2,1,0:T(8,128)(2,1)S(1)} collective-permute-done((bf16[2,2,64,512]{3,2,1,0:T(8,128)(2,1)S(1)}, bf16[2,2,64,512]{3,2,1,0:T(8,128)(2,1)S(1)}, u32[]{:S(2)}, u32[]{:S(2)}) %collective-permute-start.28) | collective-permute-done | bytes 262176 | tf_op jit(solution)/shard_map/ppermute | solution.py:26
  78.4 1.3 collective-permute-start.19
  79.7 4.3 %collective-permute-done.29.refs_11_ = bf16[2,2,64,512]{3,2,1,0:T(8,128)(2,1)S(1)} collective-permute-done((bf16[2,2,64,512]{3,2,1,0:T(8,128)(2,1)S(1)}, bf16[2,2,64,512]{3,2,1,0:T(8,128)(2,1)S(1)}, u32[]{:S(2)}, u32[]{:S(2)}) %collective-permute-start.29) | collective-permute-done | bytes 262176 | tf_op jit(solution)/shard_map/ppermute | solution.py:26
  84.0 2.3 %collective-permute-done.30.refs_12_ = bf16[1,2,64,512]{3,2,1,0:T(8,128)(2,1)S(1)} collective-permute-done((bf16[1,2,64,512]{3,2,1,0:T(8,128)(2,1)S(1)}, bf16[1,2,64,512]{3,2,1,0:T(8,128)(2,1)S(1)}, u32[]{:S(2)}, u32[]{:S(2)}) %collective-permute-start.30) | collective-permute-done | bytes 131104 | tf_op jit(solution)/shard_map/ppermute | solution.py:26
  86.4 0.6 copy-done.17
  87.0 10.3 %base.1 = (bf16[2,1024,128]{2,1,0:T(8,128)(2,1)}, bf16[2,1024,128]{2,1,0:T(8,128)(2,1)}, bf16[2,1024,128]{2,1,0:T(8,128)(2,1)}, bf16[1024,128]{1,0:T(8,128)(2,1)}, bf16[1024,128]{1,0:T(8,128)(2,1)}) custom-call(s32[5]{0:T(128)} %copy-done.11, s32[2,2]{1,0:T(2,128)} %rank_a.1, s32[2,2]{1,0:T(2,128)} %copy-done.19, bf16[3,2,64,512]{3,2,1,0:T(8,128)(2,1)} %copy-done, ...), custom_call_target="tpu_custom_call" | custom-call | flops 4294967296 | bytes 15728640 | tf_op jit(solution)/shard_map/base/pallas_call | solution.py:264
  97.3 0.5 collective-permute-start.34
  97.9 0.6 dynamic-slice_bitcast_fusion
  98.6 4.1 %collective-permute-start.20 = (bf16[256,128]{1,0:T(8,128)(2,1)}, bf16[256,128]{1,0:T(8,128)(2,1)}, u32[]{:S(2)}, u32[]{:S(2)}) collective-permute-start(bf16[256,128]{1,0:T(8,128)(2,1)} %dynamic-slice_bitcast_fusion), channel_id=1, source_target_pairs={{0,4},{8,12},{2,6},{10,14},{1,5},{9,13},{3,7},{11,15},{16,20},{24,... | collective-permute-start | bytes 196616 | tf_op jit(solution)/shard_map/ppermute | solution.py:425
  102.7 2.1 %collective-permute-done.20 = bf16[256,128]{1,0:T(8,128)(2,1)} collective-permute-done((bf16[256,128]{1,0:T(8,128)(2,1)}, bf16[256,128]{1,0:T(8,128)(2,1)}, u32[]{:S(2)}, u32[]{:S(2)}) %collective-permute-start.20) | collective-permute-done | bytes 65568 | tf_op jit(solution)/shard_map/ppermute | solution.py:425
  104.8 0.5 sweep_part.1
  105.3 3.1 %collective-permute-start.21 = (bf16[512,128]{1,0:T(8,128)(2,1)S(1)}, bf16[512,128]{1,0:T(8,128)(2,1)S(1)}, u32[]{:S(2)}, u32[]{:S(2)}) collective-permute-start(bf16[512,128]{1,0:T(8,128)(2,1)S(1)} %sweep_part.1), channel_id=1, source_target_pairs={{0,16},{16,0},{1,17},{17,1},{2,18},{18,2},{3,19},{19,3},{4,20},{20... | collective-permute-start | bytes 393224 | tf_op jit(solution)/shard_map/ppermute | solution.py:26
  108.4 3.7 %collective-permute-done.21 = bf16[512,128]{1,0:T(8,128)(2,1)S(1)} collective-permute-done((bf16[512,128]{1,0:T(8,128)(2,1)S(1)}, bf16[512,128]{1,0:T(8,128)(2,1)S(1)}, u32[]{:S(2)}, u32[]{:S(2)}) %collective-permute-start.21) | collective-permute-done | bytes 131104 | tf_op jit(solution)/shard_map/ppermute | solution.py:26
  112.2 10.7 %collective-permute-start.22 = (bf16[512,128]{1,0:T(8,128)(2,1)S(1)}, bf16[512,128]{1,0:T(8,128)(2,1)S(1)}, u32[]{:S(2)}, u32[]{:S(2)}) collective-permute-start(bf16[512,128]{1,0:T(8,128)(2,1)S(1)} %add.42), channel_id=1, source_target_pairs={{0,224},{32,0},{64,32},{96,64},{128,96},{160,128},{192,160},{224,1... | collective-permute-start | bytes 393224 | tf_op jit(solution)/shard_map/ppermute | solution.py:21
  122.9 1.0 fusion.2
  123.9 0.1 collective-permute-start.36
  124.0 2.1 %collective-permute-start.35 = (bf16[1024,128]{1,0:T(8,128)(2,1)S(1)}, bf16[1024,128]{1,0:T(8,128)(2,1)S(1)}, u32[]{:S(2)}, u32[]{:S(2)}) collective-permute-start(bf16[1024,128]{1,0:T(8,128)(2,1)S(1)} %fusion.3), channel_id=1, source_target_pairs={{0,4},{4,8},{8,12},{12,0},{1,5},{5,9},{9,13},{13,1},{2,6},{6,10},{... | collective-permute-start | bytes 786440 | tf_op jit(solution)/shard_map/ppermute | solution.py:21
  126.1 3.0 %collective-permute-done.23 = bf16[512,128]{1,0:T(8,128)(2,1)S(1)} collective-permute-done((bf16[512,128]{1,0:T(8,128)(2,1)S(1)}, bf16[512,128]{1,0:T(8,128)(2,1)S(1)}, u32[]{:S(2)}, u32[]{:S(2)}) %collective-permute-start.23) | collective-permute-done | bytes 131104 | tf_op jit(solution)/shard_map/ppermute | solution.py:21
  129.1 1.7 %collective-permute-start.24 = (bf16[512,128]{1,0:T(8,128)(2,1)S(1)}, bf16[512,128]{1,0:T(8,128)(2,1)S(1)}, u32[]{:S(2)}, u32[]{:S(2)}) collective-permute-start(bf16[512,128]{1,0:T(8,128)(2,1)S(1)} %get-tuple-element.31), channel_id=1, source_target_pairs={{0,160},{32,192},{64,224},{96,0},{128,32},{160,64},{192,96},{224,1... | collective-permute-start | bytes 393224 | tf_op jit(solution)/shard_map/ppermute | solution.py:21
  130.8 2.2 %collective-permute-start.25 = (bf16[512,128]{1,0:T(8,128)(2,1)S(1)}, bf16[512,128]{1,0:T(8,128)(2,1)S(1)}, u32[]{:S(2)}, u32[]{:S(2)}) collective-permute-start(bf16[512,128]{1,0:T(8,128)(2,1)S(1)} %get-tuple-element.32), channel_id=1, source_target_pairs={{0,96},{32,128},{64,160},{96,192},{128,224},{160,0},{192,32},{224,... | collective-permute-start | bytes 393224 | tf_op jit(solution)/shard_map/ppermute | solution.py:21
  133.0 0.9 pack.1
  133.9 2.9 %collective-permute-start.37 = (bf16[1024,128]{1,0:T(8,128)(2,1)S(1)}, bf16[1024,128]{1,0:T(8,128)(2,1)S(1)}, u32[]{:S(2)}, u32[]{:S(2)}) collective-permute-start(bf16[1024,128]{1,0:T(8,128)(2,1)S(1)} %get-tuple-element.30), channel_id=1, source_target_pairs={{0,2},{2,0},{1,3},{3,1},{4,6},{6,4},{5,7},{7,5},{8,10},{10,8},{9,1... | collective-permute-start | bytes 786440 | tf_op jit(solution)/shard_map/ppermute | solution.py:26
  136.8 1.9 %collective-permute-done.24 = bf16[512,128]{1,0:T(8,128)(2,1)S(1)} collective-permute-done((bf16[512,128]{1,0:T(8,128)(2,1)S(1)}, bf16[512,128]{1,0:T(8,128)(2,1)S(1)}, u32[]{:S(2)}, u32[]{:S(2)}) %collective-permute-start.24) | collective-permute-done | bytes 131104 | tf_op jit(solution)/shard_map/ppermute | solution.py:21
  138.7 0.4 collective-permute-done.25
  139.1 2.1 %collective-permute-done.37.came_ref = bf16[1024,128]{1,0:T(8,128)(2,1)S(1)} collective-permute-done((bf16[1024,128]{1,0:T(8,128)(2,1)S(1)}, bf16[1024,128]{1,0:T(8,128)(2,1)S(1)}, u32[]{:S(2)}, u32[]{:S(2)}) %collective-permute-start.37) | collective-permute-done | bytes 262176 | tf_op jit(solution)/shard_map/ppermute | solution.py:26
  141.2 2.6 %last.1 = bf16[2,64,1024]{2,1,0:T(8,128)(2,1)} custom-call(s32[5]{0:T(128)S(1)} %copy-done.12, s32[32]{0:T(128)S(1)} %copy-done.13, bf16[512,128]{1,0:T(8,128)(2,1)S(1)} %add_add_fusion.s_ref, bf16[2,1024,256]{2,1,0:T(8,128)(2,1)S(1)} %get-tuple-element.20.refs_7_.u_ref, bf16[2,1024,256]{2,1,0:T(8,128)(2,1)S(1)} %get-tuple-element.23.v_ref, ...), custom_call_target="tpu_custom_call" | custom-call | tf_op jit(solution)/shard_map/last/pallas_call | solution.py:328
  (86 shorter events, 0.6 us)
Async XLA Ops:
  0.1 1.0 copy-start.9
  1.0 61.9 %copy-start.11 = (s32[5]{0:T(128)}, s32[5]{0:T(128)S(1)}, u32[]{:S(2)}) copy-start(s32[5]{0:T(128)S(1)} %stack.62.at) | copy-start | bytes 64
  1.7 2.6 %collective-permute-start = (bf16[2,64,512]{2,1,0:T(8,128)(2,1)S(1)}, bf16[2,64,512]{2,1,0:T(8,128)(2,1)S(1)}, u32[]{:S(2)}, u32[]{:S(2)}) collective-permute-start(bf16[2,64,512]{2,1,0:T(8,128)(2,1)S(1)} %get-tuple-element.19), channel_id=1, source_target_pairs={{0,1},{1,0},{2,3},{3,2},{4,5},{5,4},{6,7},{7,6},{8,9},{9,8},{10,11... | collective-permute-start | bytes 393224 | tf_op jit(solution)/shard_map/ppermute | solution.py:26
  2.7 6.5 %collective-permute-start.10 = (bf16[2,2,64,256]{3,2,1,0:T(8,128)(2,1)S(1)}, bf16[2,2,64,256]{3,2,1,0:T(8,128)(2,1)S(1)}, u32[]{:S(2)}, u32[]{:S(2)}) collective-permute-start(bf16[2,2,64,256]{3,2,1,0:T(8,128)(2,1)S(1)} %get-tuple-element.38), channel_id=1, source_target_pairs={{0,2},{2,0},{1,3},{3,1},{4,6},{6,4},{5,7},{7,5},{8,10},{10,8},{9,1... | collective-permute-start | bytes 393224 | tf_op jit(solution)/shard_map/ppermute | solution.py:26
  4.3 9.4 %collective-permute-start.1 = (bf16[2,64,512]{2,1,0:T(8,128)(2,1)S(1)}, bf16[2,64,512]{2,1,0:T(8,128)(2,1)S(1)}, u32[]{:S(2)}, u32[]{:S(2)}) collective-permute-start(bf16[2,64,512]{2,1,0:T(8,128)(2,1)S(1)} %get-tuple-element.35), channel_id=1, source_target_pairs={{0,16},{16,0},{1,17},{17,1},{2,18},{18,2},{3,19},{19,3},{4,20},{20... | collective-permute-start | bytes 393224 | tf_op jit(solution)/shard_map/ppermute | solution.py:26
  9.2 11.0 %collective-permute-start.12 = (bf16[2,2,2,64,256]{4,3,2,1,0:T(8,128)(2,1)S(1)}, bf16[2,2,2,64,256]{4,3,2,1,0:T(8,128)(2,1)S(1)}, u32[]{:S(2)}, u32[]{:S(2)}) collective-permute-start(bf16[2,2,2,64,256]{4,3,2,1,0:T(8,128)(2,1)S(1)} %pad_maximum_fusion.2.refs_0_), channel_id=1, source_target_pairs={{0,4},{4,8},{8,12},{12,0},{1,5},{5,9},{9,13},{13,1},{2,6},{6,10},{... | collective-permute-start | bytes 786440 | tf_op jit(solution)/shard_map/ppermute | solution.py:21
  13.8 46.5 %copy-start = (bf16[3,2,64,512]{3,2,1,0:T(8,128)(2,1)}, bf16[3,2,64,512]{3,2,1,0:T(8,128)(2,1)S(1)}, u32[]{:S(2)}) copy-start(bf16[3,2,64,512]{3,2,1,0:T(8,128)(2,1)S(1)} %fusion.refs_0_) | copy-start | bytes 1179652
  13.8 14.8 %collective-permute-start.2 = (bf16[3,2,64,512]{3,2,1,0:T(8,128)(2,1)S(1)}, bf16[3,2,64,512]{3,2,1,0:T(8,128)(2,1)S(1)}, u32[]{:S(2)}, u32[]{:S(2)}) collective-permute-start(bf16[3,2,64,512]{3,2,1,0:T(8,128)(2,1)S(1)} %fusion.refs_0_), channel_id=1, source_target_pairs={{0,32},{32,64},{64,96},{96,128},{128,160},{160,192},{192,224},{224... | collective-permute-start | bytes 1179656 | tf_op jit(solution)/shard_map/ppermute | solution.py:21
  15.8 13.0 %collective-permute-start.6 = (bf16[3,2,64,512]{3,2,1,0:T(8,128)(2,1)S(1)}, bf16[3,2,64,512]{3,2,1,0:T(8,128)(2,1)S(1)}, u32[]{:S(2)}, u32[]{:S(2)}) collective-permute-start(bf16[3,2,64,512]{3,2,1,0:T(8,128)(2,1)S(1)} %fusion.refs_0_), channel_id=1, source_target_pairs={{0,224},{32,0},{64,32},{96,64},{128,96},{160,128},{192,160},{224,1... | collective-permute-start | bytes 1179656 | tf_op jit(solution)/shard_map/ppermute | solution.py:21
  19.8 8.8 %collective-permute-start.11 = (bf16[2,2,2,64,256]{4,3,2,1,0:T(8,128)(2,1)S(1)}, bf16[2,2,2,64,256]{4,3,2,1,0:T(8,128)(2,1)S(1)}, u32[]{:S(2)}, u32[]{:S(2)}) collective-permute-start(bf16[2,2,2,64,256]{4,3,2,1,0:T(8,128)(2,1)S(1)} %pad_maximum_fusion.2.refs_0_), channel_id=1, source_target_pairs={{0,12},{4,0},{8,4},{12,8},{1,13},{5,1},{9,5},{13,9},{2,14},{6,2},{... | collective-permute-start | bytes 786440 | tf_op jit(solution)/shard_map/ppermute | solution.py:21
  20.2 66.2 %collective-permute-start.31 = (bf16[2,2,1024,256]{3,2,1,0:T(8,128)(2,1)}, bf16[2,2,1024,256]{3,2,1,0:T(8,128)(2,1)}, u32[]{:S(2)}, u32[]{:S(2)}) collective-permute-start(bf16[2,2,1024,256]{3,2,1,0:T(8,128)(2,1)} %refs_13_.1), channel_id=1, source_target_pairs={{0,1},{1,0},{2,3},{3,2},{4,5},{5,4},{6,7},{7,6},{8,9},{9,8},{10,11... | collective-permute-start | bytes 6291464 | tf_op jit(solution)/shard_map/ppermute | solution.py:26
  20.2 66.2 %collective-permute-start.32 = (bf16[2,2,1024,256]{3,2,1,0:T(8,128)(2,1)}, bf16[2,2,1024,256]{3,2,1,0:T(8,128)(2,1)}, u32[]{:S(2)}, u32[]{:S(2)}) collective-permute-start(bf16[2,2,1024,256]{3,2,1,0:T(8,128)(2,1)} %refs_15_.1), channel_id=1, source_target_pairs={{0,1},{1,0},{2,3},{3,2},{4,5},{5,4},{6,7},{7,6},{8,9},{9,8},{10,11... | collective-permute-start | bytes 6291464 | tf_op jit(solution)/shard_map/ppermute | solution.py:26
  28.6 31.6 %copy-start.3 = (bf16[3,2,64,512]{3,2,1,0:T(8,128)(2,1)}, bf16[3,2,64,512]{3,2,1,0:T(8,128)(2,1)S(1)}, u32[]{:S(2)}) copy-start(bf16[3,2,64,512]{3,2,1,0:T(8,128)(2,1)S(1)} %collective-permute-done.2.refs_1_) | copy-start | bytes 1179652
  28.6 11.3 %collective-permute-start.3 = (bf16[3,2,64,512]{3,2,1,0:T(8,128)(2,1)S(1)}, bf16[3,2,64,512]{3,2,1,0:T(8,128)(2,1)S(1)}, u32[]{:S(2)}, u32[]{:S(2)}) collective-permute-start(bf16[3,2,64,512]{3,2,1,0:T(8,128)(2,1)S(1)} %collective-permute-done.2.refs_1_), channel_id=1, source_target_pairs={{0,32},{32,64},{64,96},{96,128},{128,160},{160,192},{192,224},{224... | collective-permute-start | bytes 1179656 | tf_op jit(solution)/shard_map/ppermute | solution.py:21
  28.6 3.3 %collective-permute-start.14 = (bf16[2,2,2,64,256]{4,3,2,1,0:T(8,128)(2,1)S(1)}, bf16[2,2,2,64,256]{4,3,2,1,0:T(8,128)(2,1)S(1)}, u32[]{:S(2)}, u32[]{:S(2)}) collective-permute-start(bf16[2,2,2,64,256]{4,3,2,1,0:T(8,128)(2,1)S(1)} %pad_maximum_fusion.2.refs_0_), channel_id=1, source_target_pairs={{0,1},{1,0},{2,3},{3,2},{4,5},{5,4},{6,7},{7,6},{8,9},{9,8},{10,11... | collective-permute-start | bytes 786440 | tf_op jit(solution)/shard_map/ppermute | solution.py:26
  28.7 31.5 %copy-start.4 = (bf16[3,2,64,512]{3,2,1,0:T(8,128)(2,1)}, bf16[3,2,64,512]{3,2,1,0:T(8,128)(2,1)S(1)}, u32[]{:S(2)}) copy-start(bf16[3,2,64,512]{3,2,1,0:T(8,128)(2,1)S(1)} %collective-permute-done.6.refs_2_) | copy-start | bytes 1179652
  28.7 12.2 %collective-permute-start.7 = (bf16[3,2,64,512]{3,2,1,0:T(8,128)(2,1)S(1)}, bf16[3,2,64,512]{3,2,1,0:T(8,128)(2,1)S(1)}, u32[]{:S(2)}, u32[]{:S(2)}) collective-permute-start(bf16[3,2,64,512]{3,2,1,0:T(8,128)(2,1)S(1)} %collective-permute-done.6.refs_2_), channel_id=1, source_target_pairs={{0,224},{32,0},{64,32},{96,64},{128,96},{160,128},{192,160},{224,1... | collective-permute-start | bytes 1179656 | tf_op jit(solution)/shard_map/ppermute | solution.py:21
  32.0 12.7 %collective-permute-start.13 = (bf16[2,2,2,64,256]{4,3,2,1,0:T(8,128)(2,1)S(1)}, bf16[2,2,2,64,256]{4,3,2,1,0:T(8,128)(2,1)S(1)}, u32[]{:S(2)}, u32[]{:S(2)}) collective-permute-start(bf16[2,2,2,64,256]{4,3,2,1,0:T(8,128)(2,1)S(1)} %collective-permute-done.12.refs_3_), channel_id=1, source_target_pairs={{0,4},{4,8},{8,12},{12,0},{1,5},{5,9},{9,13},{13,1},{2,6},{6,10},{... | collective-permute-start | bytes 786440 | tf_op jit(solution)/shard_map/ppermute | solution.py:21
  39.9 20.3 %copy-start.5 = (bf16[3,2,64,512]{3,2,1,0:T(8,128)(2,1)}, bf16[3,2,64,512]{3,2,1,0:T(8,128)(2,1)S(1)}, u32[]{:S(2)}) copy-start(bf16[3,2,64,512]{3,2,1,0:T(8,128)(2,1)S(1)} %collective-permute-done.3.refs_3_) | copy-start | bytes 1179652
  39.9 10.4 %collective-permute-start.4 = (bf16[3,2,64,512]{3,2,1,0:T(8,128)(2,1)S(1)}, bf16[3,2,64,512]{3,2,1,0:T(8,128)(2,1)S(1)}, u32[]{:S(2)}, u32[]{:S(2)}) collective-permute-start(bf16[3,2,64,512]{3,2,1,0:T(8,128)(2,1)S(1)} %collective-permute-done.3.refs_3_), channel_id=1, source_target_pairs={{0,32},{32,64},{64,96},{96,128},{128,160},{160,192},{192,224},{224... | collective-permute-start | bytes 1179656 | tf_op jit(solution)/shard_map/ppermute | solution.py:21
  40.9 19.3 %copy-start.6 = (bf16[3,2,64,512]{3,2,1,0:T(8,128)(2,1)}, bf16[3,2,64,512]{3,2,1,0:T(8,128)(2,1)S(1)}, u32[]{:S(2)}) copy-start(bf16[3,2,64,512]{3,2,1,0:T(8,128)(2,1)S(1)} %collective-permute-done.7.refs_4_) | copy-start | bytes 1179652
  40.9 11.8 %collective-permute-start.8 = (bf16[3,2,64,512]{3,2,1,0:T(8,128)(2,1)S(1)}, bf16[3,2,64,512]{3,2,1,0:T(8,128)(2,1)S(1)}, u32[]{:S(2)}, u32[]{:S(2)}) collective-permute-start(bf16[3,2,64,512]{3,2,1,0:T(8,128)(2,1)S(1)} %collective-permute-done.7.refs_4_), channel_id=1, source_target_pairs={{0,224},{32,0},{64,32},{96,64},{128,96},{160,128},{192,160},{224,1... | collective-permute-start | bytes 1179656 | tf_op jit(solution)/shard_map/ppermute | solution.py:21
  44.6 5.8 %collective-permute-start.17 = (bf16[2,2,2,64,256]{4,3,2,1,0:T(8,128)(2,1)S(1)}, bf16[2,2,2,64,256]{4,3,2,1,0:T(8,128)(2,1)S(1)}, u32[]{:S(2)}, u32[]{:S(2)}) collective-permute-start(bf16[2,2,2,64,256]{4,3,2,1,0:T(8,128)(2,1)S(1)} %collective-permute-done.12.refs_3_), channel_id=1, source_target_pairs={{0,1},{1,0},{2,3},{3,2},{4,5},{5,4},{6,7},{7,6},{8,9},{9,8},{10,11... | collective-permute-start | bytes 786440 | tf_op jit(solution)/shard_map/ppermute | solution.py:26
  50.3 17.2 %copy-start.1 = (bf16[3,2,64,512]{3,2,1,0:T(8,128)(2,1)}, bf16[3,2,64,512]{3,2,1,0:T(8,128)(2,1)S(1)}, u32[]{:S(2)}) copy-start(bf16[3,2,64,512]{3,2,1,0:T(8,128)(2,1)S(1)} %collective-permute-done.4.refs_5_) | copy-start | bytes 1179652
  50.4 3.2 %collective-permute-start.15 = (bf16[2,2,2,64,256]{4,3,2,1,0:T(8,128)(2,1)S(1)}, bf16[2,2,2,64,256]{4,3,2,1,0:T(8,128)(2,1)S(1)}, u32[]{:S(2)}, u32[]{:S(2)}) collective-permute-start(bf16[2,2,2,64,256]{4,3,2,1,0:T(8,128)(2,1)S(1)} %collective-permute-done.11.refs_1_), channel_id=1, source_target_pairs={{0,1},{1,0},{2,3},{3,2},{4,5},{5,4},{6,7},{7,6},{8,9},{9,8},{10,11... | collective-permute-start | bytes 786440 | tf_op jit(solution)/shard_map/ppermute | solution.py:26
  50.4 6.9 %collective-permute-start.16 = (bf16[2,2,2,64,256]{4,3,2,1,0:T(8,128)(2,1)S(1)}, bf16[2,2,2,64,256]{4,3,2,1,0:T(8,128)(2,1)S(1)}, u32[]{:S(2)}, u32[]{:S(2)}) collective-permute-start(bf16[2,2,2,64,256]{4,3,2,1,0:T(8,128)(2,1)S(1)} %collective-permute-done.13.refs_2_), channel_id=1, source_target_pairs={{0,1},{1,0},{2,3},{3,2},{4,5},{5,4},{6,7},{7,6},{8,9},{9,8},{10,11... | collective-permute-start | bytes 786440 | tf_op jit(solution)/shard_map/ppermute | solution.py:26
  52.7 10.2 %copy-start.2 = (bf16[3,2,64,512]{3,2,1,0:T(8,128)(2,1)}, bf16[3,2,64,512]{3,2,1,0:T(8,128)(2,1)S(1)}, u32[]{:S(2)}) copy-start(bf16[3,2,64,512]{3,2,1,0:T(8,128)(2,1)S(1)} %collective-permute-done.8.refs_6_) | copy-start | bytes 1179652
  52.7 10.2 %collective-permute-start.5 = (bf16[2,2,64,512]{3,2,1,0:T(8,128)(2,1)S(1)}, bf16[2,2,64,512]{3,2,1,0:T(8,128)(2,1)S(1)}, u32[]{:S(2)}, u32[]{:S(2)}) collective-permute-start(bf16[2,2,64,512]{3,2,1,0:T(8,128)(2,1)S(1)} %slice.44), channel_id=1, source_target_pairs={{0,32},{32,64},{64,96},{96,128},{128,160},{160,192},{192,224},{224... | collective-permute-start | bytes 786440 | tf_op jit(solution)/shard_map/ppermute | solution.py:21
  53.5 9.4 %collective-permute-start.9 = (bf16[1,2,64,512]{3,2,1,0:T(8,128)(2,1)S(1)}, bf16[1,2,64,512]{3,2,1,0:T(8,128)(2,1)S(1)}, u32[]{:S(2)}, u32[]{:S(2)}) collective-permute-start(bf16[1,2,64,512]{3,2,1,0:T(8,128)(2,1)S(1)} %get-tuple-element.34), channel_id=1, source_target_pairs={{0,224},{32,0},{64,32},{96,64},{128,96},{160,128},{192,160},{224,1... | collective-permute-start | bytes 393224 | tf_op jit(solution)/shard_map/ppermute | solution.py:21
  57.3 13.2 %collective-permute-start.27 = (bf16[3,2,64,512]{3,2,1,0:T(8,128)(2,1)}, bf16[3,2,64,512]{3,2,1,0:T(8,128)(2,1)}, u32[]{:S(2)}, u32[]{:S(2)}) collective-permute-start(bf16[3,2,64,512]{3,2,1,0:T(8,128)(2,1)} %fusion.1), channel_id=1, source_target_pairs={{0,16},{16,0},{1,17},{17,1},{2,18},{18,2},{3,19},{19,3},{4,20},{20... | collective-permute-start | bytes 1179656 | tf_op jit(solution)/shard_map/ppermute | solution.py:26
  60.3 2.7 %copy-start.13 = (s32[32]{0:T(128)S(1)}, s32[32]{0:T(128)}, u32[]{:S(2)}) copy-start(s32[32]{0:T(128)} %rank.3) | copy-start | bytes 388
  62.9 2.7 %copy-start.18 = (s32[2,2]{1,0:T(2,128)S(1)}, s32[2,2]{1,0:T(2,128)}, u32[]{:S(2)}) copy-start(s32[2,2]{1,0:T(2,128)} %rank_a.1) | copy-start | bytes 52
  63.0 1.3 copy-start.10
  63.0 4.6 %copy-start.7 = (bf16[2,2,64,512]{3,2,1,0:T(8,128)(2,1)}, bf16[2,2,64,512]{3,2,1,0:T(8,128)(2,1)S(1)}, u32[]{:S(2)}) copy-start(bf16[2,2,64,512]{3,2,1,0:T(8,128)(2,1)S(1)} %collective-permute-done.5.a_ref.refs_7_) | copy-start | bytes 786436
  64.3 7.0 %collective-permute-start.18 = (bf16[4,256,128]{2,1,0:T(8,128)(2,1)S(1)}, bf16[4,256,128]{2,1,0:T(8,128)(2,1)}, u32[]{:S(2)}, u32[]{:S(2)}) collective-permute-start(bf16[4,256,128]{2,1,0:T(8,128)(2,1)S(1)} %get-tuple-element.22), channel_id=1, source_target_pairs={{0,2},{1,3},{16,18},{17,19},{34,32},{35,33},{50,48},{51,49},{68,70... | collective-permute-start | bytes 786440 | tf_op jit(solution)/shard_map/ppermute | solution.py:410
  65.7 2.0 %collective-permute-start.26 = (s32[2,2]{1,0:T(2,128)S(1)}, s32[2,2]{1,0:T(2,128)S(1)}, u32[]{:S(2)}, u32[]{:S(2)}) collective-permute-start(s32[2,2]{1,0:T(2,128)S(1)} %copy-done.18), channel_id=1, source_target_pairs={{0,1},{1,0},{2,3},{3,2},{4,5},{5,4},{6,7},{7,6},{8,9},{9,8},{10,11... | collective-permute-start | bytes 56 | tf_op jit(solution)/shard_map/ppermute | solution.py:26
  67.6 18.8 %copy-start.19 = (s32[2,2]{1,0:T(2,128)}, s32[2,2]{1,0:T(2,128)S(1)}, u32[]{:S(2)}) copy-start(s32[2,2]{1,0:T(2,128)S(1)} %collective-permute-done.26.rank_b) | copy-start | bytes 52
  67.7 10.8 %collective-permute-start.28 = (bf16[2,2,64,512]{3,2,1,0:T(8,128)(2,1)S(1)}, bf16[2,2,64,512]{3,2,1,0:T(8,128)(2,1)S(1)}, u32[]{:S(2)}, u32[]{:S(2)}) collective-permute-start(bf16[2,2,64,512]{3,2,1,0:T(8,128)(2,1)S(1)} %pad_maximum_fusion.3), channel_id=1, source_target_pairs={{0,16},{16,0},{1,17},{17,1},{2,18},{18,2},{3,19},{19,3},{4,20},{20... | collective-permute-start | bytes 786440 | tf_op jit(solution)/shard_map/ppermute | solution.py:26
  70.5 13.5 %collective-permute-start.29 = (bf16[2,2,64,512]{3,2,1,0:T(8,128)(2,1)S(1)}, bf16[2,2,64,512]{3,2,1,0:T(8,128)(2,1)S(1)}, u32[]{:S(2)}, u32[]{:S(2)}) collective-permute-start(bf16[2,2,64,512]{3,2,1,0:T(8,128)(2,1)S(1)} %pad_maximum_fusion.4), channel_id=1, source_target_pairs={{0,16},{16,0},{1,17},{17,1},{2,18},{18,2},{3,19},{19,3},{4,20},{20... | collective-permute-start | bytes 786440 | tf_op jit(solution)/shard_map/ppermute | solution.py:26
  71.3 15.1 %collective-permute-start.30 = (bf16[1,2,64,512]{3,2,1,0:T(8,128)(2,1)S(1)}, bf16[1,2,64,512]{3,2,1,0:T(8,128)(2,1)S(1)}, u32[]{:S(2)}, u32[]{:S(2)}) collective-permute-start(bf16[1,2,64,512]{3,2,1,0:T(8,128)(2,1)S(1)} %slice.52), channel_id=1, source_target_pairs={{0,16},{16,0},{1,17},{17,1},{2,18},{18,2},{3,19},{19,3},{4,20},{20... | collective-permute-start | bytes 393224 | tf_op jit(solution)/shard_map/ppermute | solution.py:26
  78.4 8.0 %copy-start.15 = (bf16[2,2,64,512]{3,2,1,0:T(8,128)(2,1)}, bf16[2,2,64,512]{3,2,1,0:T(8,128)(2,1)S(1)}, u32[]{:S(2)}) copy-start(bf16[2,2,64,512]{3,2,1,0:T(8,128)(2,1)S(1)} %collective-permute-done.28.refs_10_) | copy-start | bytes 786436
  78.4 19.5 %collective-permute-start.19 = (bf16[2,256,128]{2,1,0:T(8,128)(2,1)S(1)}, bf16[2,256,128]{2,1,0:T(8,128)(2,1)S(1)}, u32[]{:S(2)}, u32[]{:S(2)}) collective-permute-start(bf16[2,256,128]{2,1,0:T(8,128)(2,1)S(1)} %constant_dynamic-slice_fusion), channel_id=1, source_target_pairs={{0,8},{2,10},{1,9},{3,11},{16,24},{18,26},{17,25},{19,27},{32,40},... | collective-permute-start | bytes 393224 | tf_op jit(solution)/shard_map/ppermute | solution.py:416
  84.0 2.4 %copy-start.16 = (bf16[2,2,64,512]{3,2,1,0:T(8,128)(2,1)}, bf16[2,2,64,512]{3,2,1,0:T(8,128)(2,1)S(1)}, u32[]{:S(2)}) copy-start(bf16[2,2,64,512]{3,2,1,0:T(8,128)(2,1)S(1)} %collective-permute-done.29.refs_11_) | copy-start | bytes 786436
  86.4 0.7 copy-start.17
  97.3 26.7 %copy-start.14 = (bf16[1024,128]{1,0:T(8,128)(2,1)S(1)}, bf16[1024,128]{1,0:T(8,128)(2,1)}, u32[]{:S(2)}) copy-start(bf16[1024,128]{1,0:T(8,128)(2,1)} %get-tuple-element.27) | copy-start | bytes 786436
  97.3 25.6 %collective-permute-start.34 = (bf16[2,1024,128]{2,1,0:T(8,128)(2,1)}, bf16[2,1024,128]{2,1,0:T(8,128)(2,1)S(1)}, u32[]{:S(2)}, u32[]{:S(2)}) collective-permute-start(bf16[2,1024,128]{2,1,0:T(8,128)(2,1)} %get-tuple-element.26), channel_id=1, source_target_pairs={{0,12},{4,0},{8,4},{12,8},{1,13},{5,1},{9,5},{13,9},{2,14},{6,2},{... | collective-permute-start | bytes 1572872 | tf_op jit(solution)/shard_map/ppermute | solution.py:21
  97.9 35.1 %copy-start.8 = (bf16[2,1024,128]{2,1,0:T(8,128)(2,1)S(1)}, bf16[2,1024,128]{2,1,0:T(8,128)(2,1)}, u32[]{:S(2)}) copy-start(bf16[2,1024,128]{2,1,0:T(8,128)(2,1)} %get-tuple-element.24.own_ref) | copy-start | bytes 1572868
  97.9 35.1 %copy-start.12 = (s32[5]{0:T(128)S(1)}, s32[5]{0:T(128)}, u32[]{:S(2)}) copy-start(s32[5]{0:T(128)} %copy-done.11) | copy-start | bytes 64
  98.6 6.3 %collective-permute-start.20 = (bf16[256,128]{1,0:T(8,128)(2,1)}, bf16[256,128]{1,0:T(8,128)(2,1)}, u32[]{:S(2)}, u32[]{:S(2)}) collective-permute-start(bf16[256,128]{1,0:T(8,128)(2,1)} %dynamic-slice_bitcast_fusion), channel_id=1, source_target_pairs={{0,4},{8,12},{2,6},{10,14},{1,5},{9,13},{3,7},{11,15},{16,20},{24,... | collective-permute-start | bytes 196616 | tf_op jit(solution)/shard_map/ppermute | solution.py:425
  102.7 21.3 %collective-permute-start.33 = (bf16[2,1024,128]{2,1,0:T(8,128)(2,1)}, bf16[2,1024,128]{2,1,0:T(8,128)(2,1)S(1)}, u32[]{:S(2)}, u32[]{:S(2)}) collective-permute-start(bf16[2,1024,128]{2,1,0:T(8,128)(2,1)} %get-tuple-element.25), channel_id=1, source_target_pairs={{0,4},{4,8},{8,12},{12,0},{1,5},{5,9},{9,13},{13,1},{2,6},{6,10},{... | collective-permute-start | bytes 1572872 | tf_op jit(solution)/shard_map/ppermute | solution.py:21
  105.3 6.8 %collective-permute-start.21 = (bf16[512,128]{1,0:T(8,128)(2,1)S(1)}, bf16[512,128]{1,0:T(8,128)(2,1)S(1)}, u32[]{:S(2)}, u32[]{:S(2)}) collective-permute-start(bf16[512,128]{1,0:T(8,128)(2,1)S(1)} %sweep_part.1), channel_id=1, source_target_pairs={{0,16},{16,0},{1,17},{17,1},{2,18},{18,2},{3,19},{19,3},{4,20},{20... | collective-permute-start | bytes 393224 | tf_op jit(solution)/shard_map/ppermute | solution.py:26
  112.2 13.9 %collective-permute-start.22 = (bf16[512,128]{1,0:T(8,128)(2,1)S(1)}, bf16[512,128]{1,0:T(8,128)(2,1)S(1)}, u32[]{:S(2)}, u32[]{:S(2)}) collective-permute-start(bf16[512,128]{1,0:T(8,128)(2,1)S(1)} %add.42), channel_id=1, source_target_pairs={{0,224},{32,0},{64,32},{96,64},{128,96},{160,128},{192,160},{224,1... | collective-permute-start | bytes 393224 | tf_op jit(solution)/shard_map/ppermute | solution.py:21
  122.9 6.2 %collective-permute-start.23 = (bf16[512,128]{1,0:T(8,128)(2,1)S(1)}, bf16[512,128]{1,0:T(8,128)(2,1)S(1)}, u32[]{:S(2)}, u32[]{:S(2)}) collective-permute-start(bf16[512,128]{1,0:T(8,128)(2,1)S(1)} %add.42), channel_id=1, source_target_pairs={{0,32},{32,64},{64,96},{96,128},{128,160},{160,192},{192,224},{224... | collective-permute-start | bytes 393224 | tf_op jit(solution)/shard_map/ppermute | solution.py:21
  123.9 9.1 %collective-permute-start.36 = (bf16[1024,128]{1,0:T(8,128)(2,1)S(1)}, bf16[1024,128]{1,0:T(8,128)(2,1)S(1)}, u32[]{:S(2)}, u32[]{:S(2)}) collective-permute-start(bf16[1024,128]{1,0:T(8,128)(2,1)S(1)} %fusion.2), channel_id=1, source_target_pairs={{0,12},{4,0},{8,4},{12,8},{1,13},{5,1},{9,5},{13,9},{2,14},{6,2},{... | collective-permute-start | bytes 786440 | tf_op jit(solution)/shard_map/ppermute | solution.py:21
  124.0 9.0 %collective-permute-start.35 = (bf16[1024,128]{1,0:T(8,128)(2,1)S(1)}, bf16[1024,128]{1,0:T(8,128)(2,1)S(1)}, u32[]{:S(2)}, u32[]{:S(2)}) collective-permute-start(bf16[1024,128]{1,0:T(8,128)(2,1)S(1)} %fusion.3), channel_id=1, source_target_pairs={{0,4},{4,8},{8,12},{12,0},{1,5},{5,9},{9,13},{13,1},{2,6},{6,10},{... | collective-permute-start | bytes 786440 | tf_op jit(solution)/shard_map/ppermute | solution.py:21
  129.1 9.6 %collective-permute-start.24 = (bf16[512,128]{1,0:T(8,128)(2,1)S(1)}, bf16[512,128]{1,0:T(8,128)(2,1)S(1)}, u32[]{:S(2)}, u32[]{:S(2)}) collective-permute-start(bf16[512,128]{1,0:T(8,128)(2,1)S(1)} %get-tuple-element.31), channel_id=1, source_target_pairs={{0,160},{32,192},{64,224},{96,0},{128,32},{160,64},{192,96},{224,1... | collective-permute-start | bytes 393224 | tf_op jit(solution)/shard_map/ppermute | solution.py:21
  130.8 8.3 %collective-permute-start.25 = (bf16[512,128]{1,0:T(8,128)(2,1)S(1)}, bf16[512,128]{1,0:T(8,128)(2,1)S(1)}, u32[]{:S(2)}, u32[]{:S(2)}) collective-permute-start(bf16[512,128]{1,0:T(8,128)(2,1)S(1)} %get-tuple-element.32), channel_id=1, source_target_pairs={{0,96},{32,128},{64,160},{96,192},{128,224},{160,0},{192,32},{224,... | collective-permute-start | bytes 393224 | tf_op jit(solution)/shard_map/ppermute | solution.py:21
  133.9 7.3 %collective-permute-start.37 = (bf16[1024,128]{1,0:T(8,128)(2,1)S(1)}, bf16[1024,128]{1,0:T(8,128)(2,1)S(1)}, u32[]{:S(2)}, u32[]{:S(2)}) collective-permute-start(bf16[1024,128]{1,0:T(8,128)(2,1)S(1)} %get-tuple-element.30), channel_id=1, source_target_pairs={{0,2},{2,0},{1,3},{3,1},{4,6},{6,4},{5,7},{7,5},{8,10},{10,8},{9,1... | collective-permute-start | bytes 786440 | tf_op jit(solution)/shard_map/ppermute | solution.py:26

commit v3 on v2

--- a/solution.py
+++ b/solution.py
@@ -1,3 +1,5 @@
+import functools
+
 import jax
 import jax.numpy as jnp
 from jax import lax
@@ -49,27 +51,8 @@
     )(at, x)
 
 
-EARLY = (
-    (0, ((0, 0), (2, 1))),
-    (-1, ((0, 0), (2, 1))),
-    (1, ((0, 0), (2, 1))),
-    (-2, ((0, 0), (2, 1))),
-    (2, ((0, 0), (2, 1))),
-    (-3, ((0, 0), (2, 1))),
-    (3, ((0, 0), (2, 1))),
-    (4, ((0, 0),)),
-    (4, ((0, 1),)),
-)
-LATER = (
-    (0, ((1, 0),)),
-    (-1, ((1, 0),)),
-    (1, ((1, 0),)),
-    (-2, ((1, 0),)),
-    (2, ((1, 0),)),
-    (-3, ((1, 0),)),
-    (3, ((1, 0),)),
-    (4, ((1, 0),)),
-)
+EARLY = tuple((step, ((0, 0), (2, 1))) for step in (0, -1, 1, -2, 2, -3, 3))
+LATER = (0, -1, 1, -2, 2, -3, 3)
 CROSS = (((0, 0), (1, -1), (2, 1)), ((0, -2), (1, 2)), ((0, -3), (1, 3)), ((0, 4),))
 
 
@@ -79,18 +62,27 @@
 
 
 def copies_early(at, refs, x_s, sem):
-    return [
+    found = [
         pltpu.make_async_copy(ref.at[n], x_s.at[:, pl.ds(row_of(at, step, other), 64), :], sem)
-        for ref, (step, blocks) in zip(refs, EARLY)
+        for ref, (step, blocks) in zip(refs[:7], EARLY, strict=True)
         for n, other in blocks
     ]
+    if len(refs) == 9:
+        found += [
+            pltpu.make_async_copy(ref.at[n : n + 2], x_s.at[:, pl.ds(row_of(at, 4, other), 64), :], sem)
+            for ref, n, other in ((refs[7], 0, 0), (refs[8], 1, 1))
+        ]
+    return found
 
 
 def copies_later(at, refs, crossed, x_s, sem):
     found = [
-        pltpu.make_async_copy(ref.at[n], x_s.at[:, pl.ds(row_of(at, step, other), 64), :], sem)
-        for ref, (step, blocks) in zip(refs, LATER, strict=True)
-        for n, other in blocks
+        pltpu.make_async_copy(ref.at[1], x_s.at[:, pl.ds(row_of(at, step, 0), 64), :], sem)
+        for ref, step in zip(refs[:7], LATER, strict=True)
+    ]
+    found += [
+        pltpu.make_async_copy(ref.at[n], x_s.at[j, pl.ds(row_of(at, 4, 0), 64), :], sem)
+        for j, (ref, n) in enumerate(((refs[7], 2), (refs[8], 0)))
     ]
     return found + [
         pltpu.make_async_copy(ref.at[n], x_s.at[:, pl.ds(row_of(at, step, 1), 64), :], sem)
@@ -127,8 +119,8 @@
 def proj_kernel(at, rank, a_ref, b_ref, u_ref, early_ref, mine_ref, other_ref, x_s, u_s, sem):
     rows = pl.multiple_of(lax.rem(at[0] + 4, 8) * 128, 128)
     copies = [
-        pltpu.make_async_copy(a_ref.at[0], x_s.at[:, pl.ds(pl.multiple_of(64 * at[1], 64), 64), :], sem),
-        pltpu.make_async_copy(b_ref.at[0], x_s.at[:, pl.ds(pl.multiple_of(64 - 64 * at[1], 64), 64), :], sem),
+        pltpu.make_async_copy(a_ref.at[0:2], x_s.at[:, pl.ds(pl.multiple_of(64 * at[1], 64), 64), :], sem),
+        pltpu.make_async_copy(b_ref.at[1:3], x_s.at[:, pl.ds(pl.multiple_of(64 - 64 * at[1], 64), 64), :], sem),
         pltpu.make_async_copy(u_ref.at[:, pl.ds(rows, 128), :], u_s, sem),
     ]
     for c in copies:
@@ -187,32 +179,30 @@
     )(p, v)
 
 
-def base_kernel(at, rank_a, rank_b, *refs):
+def base_kernel(i, at, rank_a, rank_b, *refs):
     messages, crossed = refs[:9], refs[9:13]
     qa, qb, pa, pb = refs[13:17]
-    plus_ref, minus_ref, own_ref, next_ref, prev_ref = refs[17:22]
-    x_s, q_s, p_s, t_s, stage, sem, q_sem, p_sem, o_sem = refs[22:]
+    refs = refs[17:] if i == 0 else refs[20:]
+    plus_ref, minus_ref, own_ref, side_ref, x_s, q_s, p_s, t_s, stage, sem, q_sem, p_sem, o_sem = refs
     same = at[4] == at[1]
     x_copies = (
         copies_early(at, messages, x_s.at[0], sem.at[0]),
-        copies_later(at, messages[:8], crossed, x_s.at[1], sem.at[1]),
+        copies_later(at, messages, crossed, x_s.at[1], sem.at[1]),
     )
 
-    def tile(ref, to, sems, h, i):
-        return pltpu.make_async_copy(ref.at[i], to.at[2 * h + i], sems.at[2 * h + i])
+    def tile(ref, to, sems, h):
+        return pltpu.make_async_copy(ref.at[i], to.at[h], sems.at[h])
 
     def fetch(h, a, b, to, sems):
         mine = same == (h == 0)
 
         @pl.when(mine)
         def _():
-            for i in range(2):
-                tile(a, to, sems, h, i).start()
+            tile(a, to, sems, h).start()
 
         @pl.when(jnp.logical_not(mine))
         def _():
-            for i in range(2):
-                tile(b, to, sems, h, i).start()
+            tile(b, to, sems, h).start()
 
     for h in range(2):
         for c in x_copies[h]:
@@ -225,61 +215,56 @@
         mine = same == (h == 0)
         for c in x_copies[h]:
             c.wait()
-        for i in range(2):
-            tile(qa, q_s, q_sem, h, i).wait()
-            for j in range(2):
-                t = lax.dot_general(
-                    q_s[2 * h + i, j], x_s[h, j], (((0,), (0,)), ((), ())), preferred_element_type=F32
-                )
-                rank = jnp.where(mine, rank_a[i, j], rank_b[i, j])
-                t = jnp.where(slot < rank, t, 0.0).astype(BF)
-                for y in range(4):
-                    lanes = pl.multiple_of(lax.rem(y + 4 - at[2], 4) * 128, 128)
-                    t_s[i, 2 * h + j, :, pl.ds(lanes, 128)] = t[:, 128 * y : 128 * y + 128]
+        tile(qa, q_s, q_sem, h).wait()
+        for j in range(2):
+            t = lax.dot_general(q_s[h, j], x_s[h, j], (((0,), (0,)), ((), ())), preferred_element_type=F32)
+            rank = jnp.where(mine, rank_a[i, j], rank_b[i, j])
+            t = jnp.where(slot < rank, t, 0.0).astype(BF)
+            for y in range(4):
+                lanes = pl.multiple_of(lax.rem(y + 4 - at[2], 4) * 128, 128)
+                t_s[2 * h + j, :, pl.ds(lanes, 128)] = t[:, 128 * y : 128 * y + 128]
     outs = (
-        ((plus_ref.at[0], 2), (minus_ref.at[1], 3), (own_ref.at[0], 0), (next_ref, 1)),
-        ((plus_ref.at[1], 1), (minus_ref.at[0], 2), (own_ref.at[1], 0), (prev_ref, 3)),
+        ((plus_ref.at[0], 2), (minus_ref.at[1], 3), (own_ref.at[0], 0), (side_ref, 1))
+        if i == 0
+        else ((plus_ref.at[1], 1), (minus_ref.at[0], 2), (own_ref.at[1], 0), (side_ref, 3))
     )
     leaving = []
-    for i in range(2):
-        for h in range(2):
-            tile(pa, p_s, p_sem, h, i).wait()
-        for k in range(4):
-            rows = slice(256 * k, 256 * k + 256)
-            u = sum(
-                jnp.dot(p_s[2 * h + i, j, rows], t_s[i, 2 * h + j], preferred_element_type=F32)
-                for h in range(2)
-                for j in range(2)
-            )
-            for n, (ref, d) in enumerate(outs[i]):
-                stage[i, n, rows] = u[:, 128 * d : 128 * d + 128].astype(BF)
-                leaving.append(pltpu.make_async_copy(stage.at[i, n, rows], ref.at[rows], o_sem))
-                leaving[-1].start()
+    for h in range(2):
+        tile(pa, p_s, p_sem, h).wait()
+    for k in range(4):
+        rows = slice(256 * k, 256 * k + 256)
+        u = sum(
+            jnp.dot(p_s[h, j, rows], t_s[2 * h + j], preferred_element_type=F32) for h in range(2) for j in range(2)
+        )
+        for n, (ref, d) in enumerate(outs):
+            stage[n, rows] = u[:, 128 * d : 128 * d + 128].astype(BF)
+            leaving.append(pltpu.make_async_copy(stage.at[n, rows], ref.at[rows], o_sem))
+            leaving[-1].start()
     for c in leaving:
         c.wait()
 
 
-def base(at, rank_a, rank_b, *operands):
+def base(i, at, rank_a, rank_b, *operands):
     two, one = (jax.ShapeDtypeStruct(n, BF) for n in ((2, 1024, 128), (1024, 128)))
     return pl.pallas_call(
-        base_kernel,
-        out_shape=(two, two, two, one, one),
-        in_specs=[SMEM, SMEM, SMEM] + [ANY] * 17,
-        out_specs=(ANY,) * 5,
+        functools.partial(base_kernel, i),
+        out_shape=(two, two, two, one),
+        in_specs=[SMEM, SMEM, SMEM] + [ANY] * len(operands),
+        out_specs=(ANY,) * 4,
         scratch_shapes=[
             pltpu.VMEM((2, 2, 1024, 512), BF),
-            pltpu.VMEM((4, 2, 1024, 256), BF),
-            pltpu.VMEM((4, 2, 1024, 256), BF),
-            pltpu.VMEM((2, 4, 256, 512), BF),
-            pltpu.VMEM((2, 4, 1024, 128), BF),
+            pltpu.VMEM((2, 2, 1024, 256), BF),
+            pltpu.VMEM((2, 2, 1024, 256), BF),
+            pltpu.VMEM((4, 256, 512), BF),
+            pltpu.VMEM((4, 1024, 128), BF),
             pltpu.SemaphoreType.DMA((2,)),
-            pltpu.SemaphoreType.DMA((4,)),
-            pltpu.SemaphoreType.DMA((4,)),
+            pltpu.SemaphoreType.DMA((2,)),
+            pltpu.SemaphoreType.DMA((2,)),
             pltpu.SemaphoreType.DMA(()),
         ],
+        input_output_aliases={20: 0, 21: 1, 22: 2} if i == 1 else {},
         compiler_params=pltpu.CompilerParams(vmem_limit_bytes=60 << 20),
-        cost_estimate=pl.CostEstimate(flops=8 * 2 * 2 * 256 * 1024 * 512, bytes_accessed=15 << 20, transcendentals=0),
-        name="base",
+        cost_estimate=pl.CostEstimate(flops=4 * 2 * 2 * 256 * 1024 * 512, bytes_accessed=9 << 20, transcendentals=0),
     )(at, rank_a, rank_b, *operands)
 
 
@@ -306,33 +291,50 @@
     )(at, own, plus, minus, low, high)
 
 
-def last_kernel(at, rank, s_ref, u_ref, v_ref, keep_ref, came_ref, out_ref):
+def late_kernel(at, rank, s_ref, u_ref, v_ref, out_ref):
     lane = lax.broadcasted_iota(jnp.int32, (1, 128), 1)
     slot = lax.broadcasted_iota(jnp.int32, (256, 1), 0)
     packed = s_ref[...].astype(F32)
     turned = jnp.concatenate([packed[:, 64:], packed[:, :64]], axis=-1)
     s = jnp.concatenate([jnp.where(lane < 64, packed, turned), jnp.where(lane < 64, turned, packed)], axis=0)
     s = s.astype(BF)
-    v = keep_ref[...] + came_ref[...].astype(F32)
+    total = []
     for i in range(2):
         back = lax.dot_general(v_ref[i], s, (((0,), (0,)), ((), ())), preferred_element_type=F32)
         keep = jnp.logical_and(slot < rank[2 * (2 * at[0] + at[1]) + i], (lane < 64) == (i == 0))
         back = jnp.where(keep, back, 0.0).astype(BF)
-        v -= jnp.dot(u_ref[i], back, preferred_element_type=F32)
+        total.append(jnp.dot(u_ref[i], back, preferred_element_type=F32))
+    out_ref[...] = total[0] + total[1]
+
+
+def late(at, panel_rank, s, u, v):
+    return pl.pallas_call(
+        late_kernel,
+        out_shape=jax.ShapeDtypeStruct((1024, 128), F32),
+        in_specs=[SMEM, SMEM, VMEM, VMEM, VMEM],
+        out_specs=VMEM,
+        compiler_params=pltpu.CompilerParams(vmem_limit_bytes=12 << 20),
+        cost_estimate=pl.CostEstimate(flops=4 * 2 * 256 * 1024 * 128, bytes_accessed=3 << 20, transcendentals=0),
+        name="late",
+    )(at, panel_rank, s, u, v)
+
+
+def last_kernel(keep_ref, came_ref, late_ref, out_ref):
+    v = keep_ref[...] + came_ref[...].astype(F32) - late_ref[...]
     t = v.T.astype(BF)
     out_ref[0] = t[:64]
     out_ref[1] = t[64:]
 
 
-def last(at, panel_rank, s, u, v, keep, came):
+def last(keep, came, correction):
     return pl.pallas_call(
         last_kernel,
         out_shape=jax.ShapeDtypeStruct((2, 64, 1024), BF),
-        in_specs=[SMEM, SMEM] + [VMEM] * 5,
+        in_specs=[VMEM] * 3,
         out_specs=VMEM,
-        compiler_params=pltpu.CompilerParams(vmem_limit_bytes=12 << 20),
+        compiler_params=pltpu.CompilerParams(vmem_limit_bytes=8 << 20),
         name="last",
-    )(at, panel_rank, s, u, v, keep, came)
+    )(keep, came, correction)
 
 
 def panel_kernel(at, *refs):
@@ -385,13 +387,13 @@
     p1, m1 = move(own, "z", 1), move(own, "z", -1)
     p2, m2 = move(p1, "z", 1), move(m1, "z", -1)
     p3, m3 = move(p2, "z", 1), move(m2, "z", -1)
-    p4, m4 = move(p3[:2], "z", 1), move(m3[2:], "z", -1)
+    p4, m4 = move(p3.reshape(6, 64, 512)[:3], "z", 1), move(m3.reshape(6, 64, 512)[3:], "z", -1)
     messages = (own, p1, m1, p2, m2, p3, m3, p4, m4)
     crossed = (
         swap(jnp.stack([own[0], p1[0], m1[0]]), "xh"),
         swap(jnp.stack([p2[0], m2[0]]), "xh"),
         swap(jnp.stack([p3[0], m3[0]]), "xh"),
-        swap(p4[:1], "xh"),
+        swap(p4[None, :2], "xh"),
     )
     qb = swap(tile_q, "co")
     pb = swap(tile_p, "co")
@@ -400,29 +402,13 @@
 
     early = project_early(at, messages[:7], u)
     row, other = project(at, panel_rank, p4, m4, u, early)
-    n_z, n_h, n_y, n_l, n_c = (lax.axis_size(a) for a in ALL)
-
-    def device(a, b, c, d, e):
-        return (((a * n_h + b) * n_y + c) * n_l + d) * n_c + e
-
-    spread = [(a, b, e) for a in range(n_z) for b in range(n_h) for e in range(n_c)]
-    pairs = [(device(a, b, a >> 1, a & 1, e), device(a, b, a >> 1, 1 - (a & 1), e)) for a, b, e in spread]
-    got = lax.ppermute(other, ALL, pairs)
+    got = swap(other, "xl")
     row = jnp.where(xl == lax.rem(z, 2), row, got)
     high = y // 2
-    pairs = [
-        (device(a, b, a >> 1, f, e), device(a, b, (a >> 1) ^ 2, f, e)) for a, b, e in spread for f in range(n_l)
-    ]
-    got = lax.ppermute(lax.dynamic_slice_in_dim(row, 2 - 2 * high, 2, 0), ALL, pairs)
+    got = swap(lax.dynamic_slice_in_dim(row, 2 - 2 * high, 2, 0), "y", 2)
     two = jnp.where(y == z // 2, lax.dynamic_slice_in_dim(row, 2 * high, 2, 0), got)
     low = lax.rem(y, 2)
-    pairs = [
-        (device(a, b, (a >> 1) ^ g, f, e), device(a, b, (a >> 1) ^ g ^ 1, f, e))
-        for a, b, e in spread
-        for f in range(n_l)
-        for g in (0, 2)
-    ]
-    got = lax.ppermute(lax.dynamic_index_in_dim(two, 1 - low, 0, False), ALL, pairs)
+    got = swap(lax.dynamic_index_in_dim(two, 1 - low, 0, False), "y", 1)
     block = jnp.where(low == lax.rem(z // 2, 2), lax.dynamic_index_in_dim(two, low, 0, False), got)
     s = sweep_part(block, v)
     s = s + swap(s, "xh")
@@ -433,12 +419,15 @@
 
     tiles = (tile_q, qb, tile_p, pb)
     operands = (*messages, *crossed, *tiles)
-    plus, minus, own_sum, after, before = base(at, tile_rank, rank_b, *operands)
+    plus, minus, own_sum, after = base(0, at, tile_rank, rank_b, *operands)
+    plus, minus, own_sum, before = base(1, at, tile_rank, rank_b, *operands, plus, minus, own_sum)
     plus, minus = move(plus, "y", 1), move(minus, "y", -1)
     up = move(after + plus[0], "y", 1)
     down = move(before + minus[0], "y", -1)
     keep, away = pack(at, own_sum, plus, minus, up, down)
-    out = last(at, panel_rank, s, u, v, keep, swap(away, "xl"))
+    came = swap(away, "xl")
+    correction = late(at, panel_rank, s, u, v)
+    out = last(keep, came, correction)
     return out.swapaxes(1, 2)
 
 

time: 145 us -> 168 us (1.16)
  the two profiles are of different devices: /device:TPU:16 before, /device:TPU:56 now
where the time goes in v3:
time: 168 us; the launch traced here: 167 us
  waiting for transfers between devices  74.2 us (44%)
  starting transfers between devices  45.4 us (27%)
  Pallas kernels  25.2 us (15%)
  local copies, waits for them, and re-layouts  19.8 us (12%)
  other arithmetic  2.12 us (1%)
    ppermute x19, waiting for transfers between devices, swap(): return lax.ppermute(a, axis, [(i, i ^ k) for i in range(n)])  46.2 us
    ppermute x19, waiting for transfers between devices, move(): return lax.ppermute(a, axis, [(i, (i + k) % n) for i in range(n)])  28 us
    ppermute x19, starting transfers between devices, move(): return lax.ppermute(a, axis, [(i, (i + k) % n) for i in range(n)])  27.9 us
    ppermute x19, starting transfers between devices, swap(): return lax.ppermute(a, axis, [(i, i ^ k) for i in range(n)])  17.4 us
    unnamed x78, local copies, waits for them, and re-layouts  16.6 us
    pallas_call x2, Pallas kernels, base(): pl.pallas_call(functools.partial(base_kernel, i), out_shape=(two, two, tw...  14 us
  transfers between devices with their start and end apart: 38, of which 18 were waited for; matrix products, arithmetic and copies ran while one was open for 3% of the time, Pallas kernels for 6%

profile of v3, /device:TPU:56, one launch (start us, length us, event | category | flops | bytes accessed | tf_op | source)
XLA Modules:
  0.0 167.2 jit_solution(3024156396460101698)
XLA Ops:
  0.1 0.9 copy-done.27
  1.8 1.3 collective-permute-done.1
  3.2 3.1 %collective-permute-start.2 = (bf16[2,64,512]{2,1,0:T(8,128)(2,1)S(1)}, bf16[2,64,512]{2,1,0:T(8,128)(2,1)S(1)}, u32[]{:S(2)}, u32[]{:S(2)}) collective-permute-start(bf16[2,64,512]{2,1,0:T(8,128)(2,1)S(1)} %get-tuple-element.39), channel_id=1, source_target_pairs={{0,16},{16,0},{1,17},{17,1},{2,18},{18,2},{3,19},{19,3},{4,20},{20... | collective-permute-start | bytes 393224 | tf_op jit(solution)/shard_map/ppermute | solution.py:28
  6.3 4.0 %collective-permute-done.2 = bf16[2,64,512]{2,1,0:T(8,128)(2,1)S(1)} collective-permute-done((bf16[2,64,512]{2,1,0:T(8,128)(2,1)S(1)}, bf16[2,64,512]{2,1,0:T(8,128)(2,1)S(1)}, u32[]{:S(2)}, u32[]{:S(2)}) %collective-permute-start.2) | collective-permute-done | bytes 131104 | tf_op jit(solution)/shard_map/ppermute | solution.py:28
  10.4 2.0 %collective-permute-start.3 = (bf16[3,2,64,512]{3,2,1,0:T(8,128)(2,1)S(1)}, bf16[3,2,64,512]{3,2,1,0:T(8,128)(2,1)S(1)}, u32[]{:S(2)}, u32[]{:S(2)}) collective-permute-start(bf16[3,2,64,512]{3,2,1,0:T(8,128)(2,1)S(1)} %fusion.refs_0_), channel_id=1, source_target_pairs={{0,32},{32,64},{64,96},{96,128},{128,160},{160,192},{192,224},{224... | collective-permute-start | bytes 1179656 | tf_op jit(solution)/shard_map/ppermute | solution.py:23
  12.5 0.9 fusion.4
  13.4 1.6 collective-permute-start.22
  15.0 5.8 %collective-permute-done.3.refs_1_ = bf16[3,2,64,512]{3,2,1,0:T(8,128)(2,1)S(1)} collective-permute-done((bf16[3,2,64,512]{3,2,1,0:T(8,128)(2,1)S(1)}, bf16[3,2,64,512]{3,2,1,0:T(8,128)(2,1)S(1)}, u32[]{:S(2)}, u32[]{:S(2)}) %collective-permute-start.3) | collective-permute-done | bytes 393248 | tf_op jit(solution)/shard_map/ppermute | solution.py:23
  20.8 1.9 %collective-permute-start.5 = (bf16[3,2,64,512]{3,2,1,0:T(8,128)(2,1)S(1)}, bf16[3,2,64,512]{3,2,1,0:T(8,128)(2,1)S(1)}, u32[]{:S(2)}, u32[]{:S(2)}) collective-permute-start(bf16[3,2,64,512]{3,2,1,0:T(8,128)(2,1)S(1)} %collective-permute-done.3.refs_1_), channel_id=1, source_target_pairs={{0,32},{32,64},{64,96},{96,128},{128,160},{160,192},{192,224},{224... | collective-permute-start | bytes 1179656 | tf_op jit(solution)/shard_map/ppermute | solution.py:23
  22.7 0.8 collective-permute-start.23
  23.5 2.5 %collective-permute-start.24 = (bf16[2,2,2,64,256]{4,3,2,1,0:T(8,128)(2,1)S(1)}, bf16[2,2,2,64,256]{4,3,2,1,0:T(8,128)(2,1)S(1)}, u32[]{:S(2)}, u32[]{:S(2)}) collective-permute-start(bf16[2,2,2,64,256]{4,3,2,1,0:T(8,128)(2,1)S(1)} %pad_maximum_fusion.4.refs_0_), channel_id=1, source_target_pairs={{0,4},{4,8},{8,12},{12,0},{1,5},{5,9},{9,13},{13,1},{2,6},{6,10},{... | collective-permute-start | bytes 786440 | tf_op jit(solution)/shard_map/ppermute | solution.py:23
  26.0 2.3 %collective-permute-start.6 = (bf16[3,2,64,512]{3,2,1,0:T(8,128)(2,1)S(1)}, bf16[3,2,64,512]{3,2,1,0:T(8,128)(2,1)S(1)}, u32[]{:S(2)}, u32[]{:S(2)}) collective-permute-start(bf16[3,2,64,512]{3,2,1,0:T(8,128)(2,1)S(1)} %collective-permute-done.4.refs_2_), channel_id=1, source_target_pairs={{0,224},{32,0},{64,32},{96,64},{128,96},{160,128},{192,160},{224,1... | collective-permute-start | bytes 1179656 | tf_op jit(solution)/shard_map/ppermute | solution.py:23
  28.4 0.7 copy-done.11
  29.1 1.3 collective-permute-done.23.refs_1_
  30.9 2.1 %collective-permute-done.5.refs_3_ = bf16[3,2,64,512]{3,2,1,0:T(8,128)(2,1)S(1)} collective-permute-done((bf16[3,2,64,512]{3,2,1,0:T(8,128)(2,1)S(1)}, bf16[3,2,64,512]{3,2,1,0:T(8,128)(2,1)S(1)}, u32[]{:S(2)}, u32[]{:S(2)}) %collective-permute-start.5) | collective-permute-done | bytes 393248 | tf_op jit(solution)/shard_map/ppermute | solution.py:23
  33.5 0.7 copy-done.17
  34.2 2.8 %collective-permute-start.25 = (bf16[2,2,2,64,256]{4,3,2,1,0:T(8,128)(2,1)S(1)}, bf16[2,2,2,64,256]{4,3,2,1,0:T(8,128)(2,1)S(1)}, u32[]{:S(2)}, u32[]{:S(2)}) collective-permute-start(bf16[2,2,2,64,256]{4,3,2,1,0:T(8,128)(2,1)S(1)} %collective-permute-done.24.refs_3_), channel_id=1, source_target_pairs={{0,4},{4,8},{8,12},{12,0},{1,5},{5,9},{9,13},{13,1},{2,6},{6,10},{... | collective-permute-start | bytes 786440 | tf_op jit(solution)/shard_map/ppermute | solution.py:23
  37.0 1.0 collective-permute-start.8
  38.0 0.8 copy-done.6
  38.8 4.1 %collective-permute-done.25.refs_2_ = bf16[2,2,2,64,256]{4,3,2,1,0:T(8,128)(2,1)S(1)} collective-permute-done((bf16[2,2,2,64,256]{4,3,2,1,0:T(8,128)(2,1)S(1)}, bf16[2,2,2,64,256]{4,3,2,1,0:T(8,128)(2,1)S(1)}, u32[]{:S(2)}, u32[]{:S(2)}) %collective-permute-start.25) | collective-permute-done | bytes 262176 | tf_op jit(solution)/shard_map/ppermute | solution.py:23
  44.8 5.1 %collective-permute-done.8.refs_6_ = bf16[3,2,64,512]{3,2,1,0:T(8,128)(2,1)S(1)} collective-permute-done((bf16[3,2,64,512]{3,2,1,0:T(8,128)(2,1)S(1)}, bf16[3,2,64,512]{3,2,1,0:T(8,128)(2,1)S(1)}, u32[]{:S(2)}, u32[]{:S(2)}) %collective-permute-start.8) | collective-permute-done | bytes 393248 | tf_op jit(solution)/shard_map/ppermute | solution.py:23
  49.8 0.7 copy-done.19
  51.9 0.7 copy-done.21
  52.6 1.7 %collective-permute-start.9 = (bf16[3,64,512]{2,1,0:T(8,128)(2,1)}, bf16[3,64,512]{2,1,0:T(8,128)(2,1)}, u32[]{:S(2)}, u32[]{:S(2)}) collective-permute-start(bf16[3,64,512]{2,1,0:T(8,128)(2,1)} %slice.44), channel_id=1, source_target_pairs={{0,32},{32,64},{64,96},{96,128},{128,160},{160,192},{192,224},{224... | collective-permute-start | bytes 589832 | tf_op jit(solution)/shard_map/ppermute | solution.py:23
  54.4 0.7 copy-done.23
  56.1 0.9 copy-done.12
  57.1 0.9 copy-done.14
  58.0 0.9 copy-done.16
  59.0 0.9 copy-done.18
  59.9 0.9 copy-done.20
  60.9 0.9 copy-done.22
  61.8 0.9 copy-done.24
  62.8 0.9 copy-done.26
  63.7 2.1 %whole_panel.1 = (bf16[2,1024,256]{2,1,0:T(8,128)(2,1)S(1)}, bf16[2,1024,256]{2,1,0:T(8,128)(2,1)S(1)}) custom-call(s32[5]{0:T(128)S(1)} %stack.62.at, bf16[2,2,2,64,256]{4,3,2,1,0:T(8,128)(2,1)S(1)} %copy-done.12, bf16[2,2,2,64,256]{4,3,2,1,0:T(8,128)(2,1)S(1)} %copy-done.14, bf16[2,2,2,64,256]{4,3,2,1,0:T(8,128)(2,1)S(1)} %copy-done.20, ...), custom_call_target="tpu_custom_call" | custom-call | bytes 4194304 | tf_op jit(solution)/shard_map/whole_panel/pallas_call | solution.py:366
  65.9 1.0 copy-done.8
  66.8 2.6 %project_early.1.early_ref = f32[2,256,512]{2,1,0:T(8,128)S(1)} custom-call(s32[5]{0:T(128)S(1)} %stack.62.at, bf16[3,2,64,512]{3,2,1,0:T(8,128)(2,1)S(1)} %fusion.refs_0_, bf16[3,2,64,512]{3,2,1,0:T(8,128)(2,1)S(1)} %collective-permute-done.3.refs_1_, bf16[3,2,64,512]{3,2,1,0:T(8,128)(2,1)S(1)} %collective-permute-done.4.refs_2_, ...), custom_call_target="tpu_custom_call" | custom-call | flops 536870912 | bytes 4194304 | tf_op jit(solution)/shard_map/project_early/pallas_call | solution.py:107
  69.6 2.0 %project.1 = (bf16[4,256,128]{2,1,0:T(8,128)(2,1)S(1)}, bf16[4,256,128]{2,1,0:T(8,128)(2,1)S(1)}) custom-call(s32[5]{0:T(128)S(1)} %stack.62.at, s32[32]{0:T(128)S(1)} %copy-done.30, bf16[3,64,512]{2,1,0:T(8,128)(2,1)} %collective-permute-done.9.refs_7_.a_ref, bf16[3,64,512]{2,1,0:T(8,128)(2,1)} %collective-permute-done.10.refs_8_.b_ref, ...), custom_call_target="tpu_custom_call" | custom-call | flops 67108864 | bytes 2097152 | tf_op jit(solution)/shard_map/project/pallas_call | solution.py:144
  71.5 1.6 collective-permute-start.30
  73.2 2.8 %collective-permute-start.11 = (bf16[3,2,64,512]{3,2,1,0:T(8,128)(2,1)S(1)}, bf16[3,2,64,512]{3,2,1,0:T(8,128)(2,1)S(1)}, u32[]{:S(2)}, u32[]{:S(2)}) collective-permute-start(bf16[3,2,64,512]{3,2,1,0:T(8,128)(2,1)S(1)} %fusion.1), channel_id=1, source_target_pairs={{0,16},{16,0},{1,17},{17,1},{2,18},{18,2},{3,19},{19,3},{4,20},{20... | collective-permute-start | bytes 1179656 | tf_op jit(solution)/shard_map/ppermute | solution.py:28
  76.1 4.7 %collective-permute-done.30 = bf16[4,256,128]{2,1,0:T(8,128)(2,1)S(1)} collective-permute-done((bf16[4,256,128]{2,1,0:T(8,128)(2,1)S(1)}, bf16[4,256,128]{2,1,0:T(8,128)(2,1)S(1)}, u32[]{:S(2)}, u32[]{:S(2)}) %collective-permute-start.30) | collective-permute-done | bytes 262176 | tf_op jit(solution)/shard_map/ppermute | solution.py:28
  80.8 3.0 %collective-permute-start.12 = (bf16[2,2,64,512]{3,2,1,0:T(8,128)(2,1)S(1)}, bf16[2,2,64,512]{3,2,1,0:T(8,128)(2,1)S(1)}, u32[]{:S(2)}, u32[]{:S(2)}) collective-permute-start(bf16[2,2,64,512]{3,2,1,0:T(8,128)(2,1)S(1)} %pad_maximum_fusion.2), channel_id=1, source_target_pairs={{0,16},{16,0},{1,17},{17,1},{2,18},{18,2},{3,19},{19,3},{4,20},{20... | collective-permute-start | bytes 786440 | tf_op jit(solution)/shard_map/ppermute | solution.py:28
  84.5 6.9 %collective-permute-done.11.refs_9_ = bf16[3,2,64,512]{3,2,1,0:T(8,128)(2,1)S(1)} collective-permute-done((bf16[3,2,64,512]{3,2,1,0:T(8,128)(2,1)S(1)}, bf16[3,2,64,512]{3,2,1,0:T(8,128)(2,1)S(1)}, u32[]{:S(2)}, u32[]{:S(2)}) %collective-permute-start.11) | collective-permute-done | bytes 393248 | tf_op jit(solution)/shard_map/ppermute | solution.py:28
  91.4 1.0 slice_bitcast_fusion.2
  92.5 5.4 %collective-permute-done.31 = bf16[2,256,128]{2,1,0:T(8,128)(2,1)S(1)} collective-permute-done((bf16[2,256,128]{2,1,0:T(8,128)(2,1)S(1)}, bf16[2,256,128]{2,1,0:T(8,128)(2,1)S(1)}, u32[]{:S(2)}, u32[]{:S(2)}) %collective-permute-start.31) | collective-permute-done | bytes 131104 | tf_op jit(solution)/shard_map/ppermute | solution.py:28
  97.9 0.8 collective-permute-start.14
  98.7 3.9 %collective-permute-done.13.refs_11_ = bf16[2,2,64,512]{3,2,1,0:T(8,128)(2,1)S(1)} collective-permute-done((bf16[2,2,64,512]{3,2,1,0:T(8,128)(2,1)S(1)}, bf16[2,2,64,512]{3,2,1,0:T(8,128)(2,1)S(1)}, u32[]{:S(2)}, u32[]{:S(2)}) %collective-permute-start.13) | collective-permute-done | bytes 262176 | tf_op jit(solution)/shard_map/ppermute | solution.py:28
  102.7 2.4 %collective-permute-done.14.refs_12_ = bf16[1,2,64,512]{3,2,1,0:T(8,128)(2,1)S(1)} collective-permute-done((bf16[1,2,64,512]{3,2,1,0:T(8,128)(2,1)S(1)}, bf16[1,2,64,512]{3,2,1,0:T(8,128)(2,1)S(1)}, u32[]{:S(2)}, u32[]{:S(2)}) %collective-permute-start.14) | collective-permute-done | bytes 131104 | tf_op jit(solution)/shard_map/ppermute | solution.py:28
  105.7 6.9 %shard_map.73 = (bf16[2,1024,128]{2,1,0:T(8,128)(2,1)}, bf16[2,1024,128]{2,1,0:T(8,128)(2,1)}, bf16[2,1024,128]{2,1,0:T(8,128)(2,1)}, bf16[1024,128]{1,0:T(8,128)(2,1)}) custom-call(s32[5]{0:T(128)} %copy-done.28, s32[2,2]{1,0:T(2,128)} %rank_a.3, s32[2,2]{1,0:T(2,128)} %copy-done.38, bf16[3,2,64,512]{3,2,1,0:T(8,128)(2,1)} %copy-done, ...), custom_call_target="tpu_custom_call" | custom-call | flops 2147483648 | bytes 9437184 | tf_op jit(solution)/shard_map/pallas_call | solution.py:249
  112.6 7.1 %shard_map.74 = (bf16[2,1024,128]{2,1,0:T(8,128)(2,1)}, bf16[2,1024,128]{2,1,0:T(8,128)(2,1)}, bf16[2,1024,128]{2,1,0:T(8,128)(2,1)}, bf16[1024,128]{1,0:T(8,128)(2,1)}) custom-call(s32[5]{0:T(128)} %copy-done.28, s32[2,2]{1,0:T(2,128)} %rank_a.3, s32[2,2]{1,0:T(2,128)} %copy-done.38, ...), custom_call_target="tpu_custom_call", output_to_operand_aliasing={{0}: (20, {}), {1}: (21, {}), {2}: (22, {})} | custom-call | flops 2147483648 | bytes 9437184 | tf_op jit(solution)/shard_map/pallas_call | solution.py:249
  120.8 1.6 collective-permute-start.32
  122.9 11.8 %collective-permute-done.32 = bf16[256,128]{1,0:T(8,128)(2,1)} collective-permute-done((bf16[256,128]{1,0:T(8,128)(2,1)}, bf16[256,128]{1,0:T(8,128)(2,1)}, u32[]{:S(2)}, u32[]{:S(2)}) %collective-permute-start.32) | collective-permute-done | bytes 65568 | tf_op jit(solution)/shard_map/ppermute | solution.py:28
  134.7 0.8 bitcast_select_fusion.p_ref
  136.1 0.9 collective-permute-start.33
  137.0 5.7 %collective-permute-done.33 = bf16[512,128]{1,0:T(8,128)(2,1)S(1)} collective-permute-done((bf16[512,128]{1,0:T(8,128)(2,1)S(1)}, bf16[512,128]{1,0:T(8,128)(2,1)S(1)}, u32[]{:S(2)}, u32[]{:S(2)}) %collective-permute-start.33) | collective-permute-done | bytes 131104 | tf_op jit(solution)/shard_map/ppermute | solution.py:28
  142.7 1.0 collective-permute-start.35
  143.7 1.1 collective-permute-start.34
  145.0 2.1 %collective-permute-start.20 = (bf16[1024,128]{1,0:T(8,128)(2,1)S(1)}, bf16[1024,128]{1,0:T(8,128)(2,1)S(1)}, u32[]{:S(2)}, u32[]{:S(2)}) collective-permute-start(bf16[1024,128]{1,0:T(8,128)(2,1)S(1)} %fusion.2), channel_id=1, source_target_pairs={{0,12},{4,0},{8,4},{12,8},{1,13},{5,1},{9,5},{13,9},{2,14},{6,2},{... | collective-permute-start | bytes 786440 | tf_op jit(solution)/shard_map/ppermute | solution.py:23
  147.7 0.9 collective-permute-done.34
  148.7 6.9 %collective-permute-start.37 = (bf16[512,128]{1,0:T(8,128)(2,1)S(1)}, bf16[512,128]{1,0:T(8,128)(2,1)S(1)}, u32[]{:S(2)}, u32[]{:S(2)}) collective-permute-start(bf16[512,128]{1,0:T(8,128)(2,1)S(1)} %get-tuple-element.38), channel_id=1, source_target_pairs={{0,96},{32,128},{64,160},{96,192},{128,224},{160,0},{192,32},{224,... | collective-permute-start | bytes 393224 | tf_op jit(solution)/shard_map/ppermute | solution.py:23
  155.6 0.9 pack.1
  156.8 3.7 %collective-permute-done.37 = bf16[512,128]{1,0:T(8,128)(2,1)S(1)} collective-permute-done((bf16[512,128]{1,0:T(8,128)(2,1)S(1)}, bf16[512,128]{1,0:T(8,128)(2,1)S(1)}, u32[]{:S(2)}, u32[]{:S(2)}) %collective-permute-start.37) | collective-permute-done | bytes 131104 | tf_op jit(solution)/shard_map/ppermute | solution.py:23
  160.5 4.3 %collective-permute-done.36 = bf16[512,128]{1,0:T(8,128)(2,1)S(1)} collective-permute-done((bf16[512,128]{1,0:T(8,128)(2,1)S(1)}, bf16[512,128]{1,0:T(8,128)(2,1)S(1)}, u32[]{:S(2)}, u32[]{:S(2)}) %collective-permute-start.36) | collective-permute-done | bytes 131104 | tf_op jit(solution)/shard_map/ppermute | solution.py:23
  164.8 1.5 late.1.late_ref
  166.3 0.9 last.1
  (127 shorter events, 11.1 us)
Async XLA Ops:
  0.0 56.1 %copy-start.37 = (s32[2,2]{1,0:T(2,128)S(1)}, s32[2,2]{1,0:T(2,128)}, u32[]{:S(2)}) copy-start(s32[2,2]{1,0:T(2,128)} %rank_a.3) | copy-start | bytes 52
  0.1 1.0 copy-start.27
  1.0 68.5 %copy-start.28 = (s32[5]{0:T(128)}, s32[5]{0:T(128)S(1)}, u32[]{:S(2)}) copy-start(s32[5]{0:T(128)S(1)} %stack.62.at) | copy-start | bytes 64
  1.7 1.4 collective-permute-start.1
  3.2 7.1 %collective-permute-start.2 = (bf16[2,64,512]{2,1,0:T(8,128)(2,1)S(1)}, bf16[2,64,512]{2,1,0:T(8,128)(2,1)S(1)}, u32[]{:S(2)}, u32[]{:S(2)}) collective-permute-start(bf16[2,64,512]{2,1,0:T(8,128)(2,1)S(1)} %get-tuple-element.39), channel_id=1, source_target_pairs={{0,16},{16,0},{1,17},{17,1},{2,18},{18,2},{3,19},{19,3},{4,20},{20... | collective-permute-start | bytes 393224 | tf_op jit(solution)/shard_map/ppermute | solution.py:28
  10.4 56.5 %copy-start = (bf16[3,2,64,512]{3,2,1,0:T(8,128)(2,1)}, bf16[3,2,64,512]{3,2,1,0:T(8,128)(2,1)S(1)}, u32[]{:S(2)}) copy-start(bf16[3,2,64,512]{3,2,1,0:T(8,128)(2,1)S(1)} %fusion.refs_0_) | copy-start | bytes 1179652
  10.4 10.4 %collective-permute-start.3 = (bf16[3,2,64,512]{3,2,1,0:T(8,128)(2,1)S(1)}, bf16[3,2,64,512]{3,2,1,0:T(8,128)(2,1)S(1)}, u32[]{:S(2)}, u32[]{:S(2)}) collective-permute-start(bf16[3,2,64,512]{3,2,1,0:T(8,128)(2,1)S(1)} %fusion.refs_0_), channel_id=1, source_target_pairs={{0,32},{32,64},{64,96},{96,128},{128,160},{160,192},{192,224},{224... | collective-permute-start | bytes 1179656 | tf_op jit(solution)/shard_map/ppermute | solution.py:23
  12.4 13.7 %collective-permute-start.4 = (bf16[3,2,64,512]{3,2,1,0:T(8,128)(2,1)S(1)}, bf16[3,2,64,512]{3,2,1,0:T(8,128)(2,1)S(1)}, u32[]{:S(2)}, u32[]{:S(2)}) collective-permute-start(bf16[3,2,64,512]{3,2,1,0:T(8,128)(2,1)S(1)} %fusion.refs_0_), channel_id=1, source_target_pairs={{0,224},{32,0},{64,32},{96,64},{128,96},{160,128},{192,160},{224,1... | collective-permute-start | bytes 1179656 | tf_op jit(solution)/shard_map/ppermute | solution.py:23
  13.4 9.3 %collective-permute-start.22 = (bf16[2,2,64,256]{3,2,1,0:T(8,128)(2,1)S(1)}, bf16[2,2,64,256]{3,2,1,0:T(8,128)(2,1)S(1)}, u32[]{:S(2)}, u32[]{:S(2)}) collective-permute-start(bf16[2,2,64,256]{3,2,1,0:T(8,128)(2,1)S(1)} %get-tuple-element.42), channel_id=1, source_target_pairs={{0,2},{2,0},{1,3},{3,1},{4,6},{6,4},{5,7},{7,5},{8,10},{10,8},{9,1... | collective-permute-start | bytes 393224 | tf_op jit(solution)/shard_map/ppermute | solution.py:28
  20.8 48.7 %copy-start.3 = (bf16[3,2,64,512]{3,2,1,0:T(8,128)(2,1)}, bf16[3,2,64,512]{3,2,1,0:T(8,128)(2,1)S(1)}, u32[]{:S(2)}) copy-start(bf16[3,2,64,512]{3,2,1,0:T(8,128)(2,1)S(1)} %collective-permute-done.3.refs_1_) | copy-start | bytes 1179652
  20.8 12.2 %collective-permute-start.5 = (bf16[3,2,64,512]{3,2,1,0:T(8,128)(2,1)S(1)}, bf16[3,2,64,512]{3,2,1,0:T(8,128)(2,1)S(1)}, u32[]{:S(2)}, u32[]{:S(2)}) collective-permute-start(bf16[3,2,64,512]{3,2,1,0:T(8,128)(2,1)S(1)} %collective-permute-done.3.refs_1_), channel_id=1, source_target_pairs={{0,32},{32,64},{64,96},{96,128},{128,160},{160,192},{192,224},{224... | collective-permute-start | bytes 1179656 | tf_op jit(solution)/shard_map/ppermute | solution.py:23
  22.7 7.7 %collective-permute-start.23 = (bf16[2,2,2,64,256]{4,3,2,1,0:T(8,128)(2,1)S(1)}, bf16[2,2,2,64,256]{4,3,2,1,0:T(8,128)(2,1)S(1)}, u32[]{:S(2)}, u32[]{:S(2)}) collective-permute-start(bf16[2,2,2,64,256]{4,3,2,1,0:T(8,128)(2,1)S(1)} %pad_maximum_fusion.4.refs_0_), channel_id=1, source_target_pairs={{0,12},{4,0},{8,4},{12,8},{1,13},{5,1},{9,5},{13,9},{2,14},{6,2},{... | collective-permute-start | bytes 786440 | tf_op jit(solution)/shard_map/ppermute | solution.py:23
  23.5 6.8 %collective-permute-start.24 = (bf16[2,2,2,64,256]{4,3,2,1,0:T(8,128)(2,1)S(1)}, bf16[2,2,2,64,256]{4,3,2,1,0:T(8,128)(2,1)S(1)}, u32[]{:S(2)}, u32[]{:S(2)}) collective-permute-start(bf16[2,2,2,64,256]{4,3,2,1,0:T(8,128)(2,1)S(1)} %pad_maximum_fusion.4.refs_0_), channel_id=1, source_target_pairs={{0,4},{4,8},{8,12},{12,0},{1,5},{5,9},{9,13},{13,1},{2,6},{6,10},{... | collective-permute-start | bytes 786440 | tf_op jit(solution)/shard_map/ppermute | solution.py:23
  26.0 43.5 %copy-start.4 = (bf16[3,2,64,512]{3,2,1,0:T(8,128)(2,1)}, bf16[3,2,64,512]{3,2,1,0:T(8,128)(2,1)S(1)}, u32[]{:S(2)}) copy-start(bf16[3,2,64,512]{3,2,1,0:T(8,128)(2,1)S(1)} %collective-permute-done.4.refs_2_) | copy-start | bytes 1179652
  26.0 10.9 %collective-permute-start.6 = (bf16[3,2,64,512]{3,2,1,0:T(8,128)(2,1)S(1)}, bf16[3,2,64,512]{3,2,1,0:T(8,128)(2,1)S(1)}, u32[]{:S(2)}, u32[]{:S(2)}) collective-permute-start(bf16[3,2,64,512]{3,2,1,0:T(8,128)(2,1)S(1)} %collective-permute-done.4.refs_2_), channel_id=1, source_target_pairs={{0,224},{32,0},{64,32},{96,64},{128,96},{160,128},{192,160},{224,1... | collective-permute-start | bytes 1179656 | tf_op jit(solution)/shard_map/ppermute | solution.py:23
  28.4 5.1 %collective-permute-start.26 = (bf16[2,2,2,64,256]{4,3,2,1,0:T(8,128)(2,1)S(1)}, bf16[2,2,2,64,256]{4,3,2,1,0:T(8,128)(2,1)S(1)}, u32[]{:S(2)}, u32[]{:S(2)}) collective-permute-start(bf16[2,2,2,64,256]{4,3,2,1,0:T(8,128)(2,1)S(1)} %pad_maximum_fusion.4.refs_0_), channel_id=1, source_target_pairs={{0,1},{1,0},{2,3},{3,2},{4,5},{5,4},{6,7},{7,6},{8,9},{9,8},{10,11... | collective-permute-start | bytes 786440 | tf_op jit(solution)/shard_map/ppermute | solution.py:28
  30.4 74.6 %collective-permute-start.15 = (bf16[2,2,1024,256]{3,2,1,0:T(8,128)(2,1)}, bf16[2,2,1024,256]{3,2,1,0:T(8,128)(2,1)}, u32[]{:S(2)}, u32[]{:S(2)}) collective-permute-start(bf16[2,2,1024,256]{3,2,1,0:T(8,128)(2,1)} %refs_13_.3), channel_id=1, source_target_pairs={{0,1},{1,0},{2,3},{3,2},{4,5},{5,4},{6,7},{7,6},{8,9},{9,8},{10,11... | collective-permute-start | bytes 6291464 | tf_op jit(solution)/shard_map/ppermute | solution.py:28
  30.4 74.6 %collective-permute-start.16 = (bf16[2,2,1024,256]{3,2,1,0:T(8,128)(2,1)}, bf16[2,2,1024,256]{3,2,1,0:T(8,128)(2,1)}, u32[]{:S(2)}, u32[]{:S(2)}) collective-permute-start(bf16[2,2,1024,256]{3,2,1,0:T(8,128)(2,1)} %refs_15_.3), channel_id=1, source_target_pairs={{0,1},{1,0},{2,3},{3,2},{4,5},{5,4},{6,7},{7,6},{8,9},{9,8},{10,11... | collective-permute-start | bytes 6291464 | tf_op jit(solution)/shard_map/ppermute | solution.py:28
  33.0 43.0 %copy-start.5 = (bf16[3,2,64,512]{3,2,1,0:T(8,128)(2,1)}, bf16[3,2,64,512]{3,2,1,0:T(8,128)(2,1)S(1)}, u32[]{:S(2)}) copy-start(bf16[3,2,64,512]{3,2,1,0:T(8,128)(2,1)S(1)} %collective-permute-done.5.refs_3_) | copy-start | bytes 1179652
  33.0 10.6 %collective-permute-start.7 = (bf16[3,2,64,512]{3,2,1,0:T(8,128)(2,1)S(1)}, bf16[3,2,64,512]{3,2,1,0:T(8,128)(2,1)S(1)}, u32[]{:S(2)}, u32[]{:S(2)}) collective-permute-start(bf16[3,2,64,512]{3,2,1,0:T(8,128)(2,1)S(1)} %collective-permute-done.5.refs_3_), channel_id=1, source_target_pairs={{0,32},{32,64},{64,96},{96,128},{128,160},{160,192},{192,224},{224... | collective-permute-start | bytes 1179656 | tf_op jit(solution)/shard_map/ppermute | solution.py:23
  34.2 8.7 %collective-permute-start.25 = (bf16[2,2,2,64,256]{4,3,2,1,0:T(8,128)(2,1)S(1)}, bf16[2,2,2,64,256]{4,3,2,1,0:T(8,128)(2,1)S(1)}, u32[]{:S(2)}, u32[]{:S(2)}) collective-permute-start(bf16[2,2,2,64,256]{4,3,2,1,0:T(8,128)(2,1)S(1)} %collective-permute-done.24.refs_3_), channel_id=1, source_target_pairs={{0,4},{4,8},{8,12},{12,0},{1,5},{5,9},{9,13},{13,1},{2,6},{6,10},{... | collective-permute-start | bytes 786440 | tf_op jit(solution)/shard_map/ppermute | solution.py:23
  37.0 12.8 %collective-permute-start.8 = (bf16[3,2,64,512]{3,2,1,0:T(8,128)(2,1)S(1)}, bf16[3,2,64,512]{3,2,1,0:T(8,128)(2,1)S(1)}, u32[]{:S(2)}, u32[]{:S(2)}) collective-permute-start(bf16[3,2,64,512]{3,2,1,0:T(8,128)(2,1)S(1)} %collective-permute-done.6.refs_4_), channel_id=1, source_target_pairs={{0,224},{32,0},{64,32},{96,64},{128,96},{160,128},{192,160},{224,1... | collective-permute-start | bytes 1179656 | tf_op jit(solution)/shard_map/ppermute | solution.py:23
  42.9 9.1 %collective-permute-start.27 = (bf16[2,2,2,64,256]{4,3,2,1,0:T(8,128)(2,1)S(1)}, bf16[2,2,2,64,256]{4,3,2,1,0:T(8,128)(2,1)S(1)}, u32[]{:S(2)}, u32[]{:S(2)}) collective-permute-start(bf16[2,2,2,64,256]{4,3,2,1,0:T(8,128)(2,1)S(1)} %collective-permute-done.23.refs_1_), channel_id=1, source_target_pairs={{0,1},{1,0},{2,3},{3,2},{4,5},{5,4},{6,7},{7,6},{8,9},{9,8},{10,11... | collective-permute-start | bytes 786440 | tf_op jit(solution)/shard_map/ppermute | solution.py:28
  43.6 32.5 %copy-start.1 = (bf16[3,2,64,512]{3,2,1,0:T(8,128)(2,1)}, bf16[3,2,64,512]{3,2,1,0:T(8,128)(2,1)S(1)}, u32[]{:S(2)}) copy-start(bf16[3,2,64,512]{3,2,1,0:T(8,128)(2,1)S(1)} %collective-permute-done.7.refs_5_) | copy-start | bytes 1179652
  43.6 10.8 %collective-permute-start.29 = (bf16[2,2,2,64,256]{4,3,2,1,0:T(8,128)(2,1)S(1)}, bf16[2,2,2,64,256]{4,3,2,1,0:T(8,128)(2,1)S(1)}, u32[]{:S(2)}, u32[]{:S(2)}) collective-permute-start(bf16[2,2,2,64,256]{4,3,2,1,0:T(8,128)(2,1)S(1)} %collective-permute-done.24.refs_3_), channel_id=1, source_target_pairs={{0,1},{1,0},{2,3},{3,2},{4,5},{5,4},{6,7},{7,6},{8,9},{9,8},{10,11... | collective-permute-start | bytes 786440 | tf_op jit(solution)/shard_map/ppermute | solution.py:28
  49.8 26.2 %copy-start.2 = (bf16[3,2,64,512]{3,2,1,0:T(8,128)(2,1)}, bf16[3,2,64,512]{3,2,1,0:T(8,128)(2,1)S(1)}, u32[]{:S(2)}) copy-start(bf16[3,2,64,512]{3,2,1,0:T(8,128)(2,1)S(1)} %collective-permute-done.8.refs_6_) | copy-start | bytes 1179652
  49.8 5.6 %collective-permute-start.28 = (bf16[2,2,2,64,256]{4,3,2,1,0:T(8,128)(2,1)S(1)}, bf16[2,2,2,64,256]{4,3,2,1,0:T(8,128)(2,1)S(1)}, u32[]{:S(2)}, u32[]{:S(2)}) collective-permute-start(bf16[2,2,2,64,256]{4,3,2,1,0:T(8,128)(2,1)S(1)} %collective-permute-done.25.refs_2_), channel_id=1, source_target_pairs={{0,1},{1,0},{2,3},{3,2},{4,5},{5,4},{6,7},{7,6},{8,9},{9,8},{10,11... | collective-permute-start | bytes 786440 | tf_op jit(solution)/shard_map/ppermute | solution.py:28
  52.6 16.9 %collective-permute-start.9 = (bf16[3,64,512]{2,1,0:T(8,128)(2,1)}, bf16[3,64,512]{2,1,0:T(8,128)(2,1)}, u32[]{:S(2)}, u32[]{:S(2)}) collective-permute-start(bf16[3,64,512]{2,1,0:T(8,128)(2,1)} %slice.44), channel_id=1, source_target_pairs={{0,32},{32,64},{64,96},{96,128},{128,160},{160,192},{192,224},{224... | collective-permute-start | bytes 589832 | tf_op jit(solution)/shard_map/ppermute | solution.py:23
  55.1 14.4 %collective-permute-start.10 = (bf16[3,64,512]{2,1,0:T(8,128)(2,1)}, bf16[3,64,512]{2,1,0:T(8,128)(2,1)}, u32[]{:S(2)}, u32[]{:S(2)}) collective-permute-start(bf16[3,64,512]{2,1,0:T(8,128)(2,1)} %slice.45), channel_id=1, source_target_pairs={{0,224},{32,0},{64,32},{96,64},{128,96},{160,128},{192,160},{224,1... | collective-permute-start | bytes 589832 | tf_op jit(solution)/shard_map/ppermute | solution.py:23
  55.4 11.5 %copy-start.7 = (bf16[3,2,64,512]{3,2,1,0:T(8,128)(2,1)S(1)}, bf16[3,2,64,512]{3,2,1,0:T(8,128)(2,1)}, u32[]{:S(2)}) copy-start(bf16[3,2,64,512]{3,2,1,0:T(8,128)(2,1)} %copy-done.6) | copy-start | bytes 1179652
  56.1 27.8 %collective-permute-start = (s32[2,2]{1,0:T(2,128)S(1)}, s32[2,2]{1,0:T(2,128)S(1)}, u32[]{:S(2)}, u32[]{:S(2)}) collective-permute-start(s32[2,2]{1,0:T(2,128)S(1)} %copy-done.37), channel_id=1, source_target_pairs={{0,1},{1,0},{2,3},{3,2},{4,5},{5,4},{6,7},{7,6},{8,9},{9,8},{10,11... | collective-permute-start | bytes 56 | tf_op jit(solution)/shard_map/ppermute | solution.py:28
  56.1 1.0 copy-start.12
  57.1 0.9 copy-start.14
  58.0 0.9 copy-start.16
  59.0 0.9 copy-start.18
  59.9 0.9 copy-start.20
  65.9 1.0 copy-start.8
  66.8 2.7 %copy-start.30 = (s32[32]{0:T(128)S(1)}, s32[32]{0:T(128)}, u32[]{:S(2)}) copy-start(s32[32]{0:T(128)} %rank.3) | copy-start | bytes 388
  71.5 9.3 %collective-permute-start.30 = (bf16[4,256,128]{2,1,0:T(8,128)(2,1)S(1)}, bf16[4,256,128]{2,1,0:T(8,128)(2,1)S(1)}, u32[]{:S(2)}, u32[]{:S(2)}) collective-permute-start(bf16[4,256,128]{2,1,0:T(8,128)(2,1)S(1)} %get-tuple-element.35), channel_id=1, source_target_pairs={{0,2},{2,0},{1,3},{3,1},{4,6},{6,4},{5,7},{7,5},{8,10},{10,8},{9,1... | collective-permute-start | bytes 786440 | tf_op jit(solution)/shard_map/ppermute | solution.py:28
  73.2 18.3 %collective-permute-start.11 = (bf16[3,2,64,512]{3,2,1,0:T(8,128)(2,1)S(1)}, bf16[3,2,64,512]{3,2,1,0:T(8,128)(2,1)S(1)}, u32[]{:S(2)}, u32[]{:S(2)}) collective-permute-start(bf16[3,2,64,512]{3,2,1,0:T(8,128)(2,1)S(1)} %fusion.1), channel_id=1, source_target_pairs={{0,16},{16,0},{1,17},{17,1},{2,18},{18,2},{3,19},{19,3},{4,20},{20... | collective-permute-start | bytes 1179656 | tf_op jit(solution)/shard_map/ppermute | solution.py:28
  80.8 17.9 %collective-permute-start.12 = (bf16[2,2,64,512]{3,2,1,0:T(8,128)(2,1)S(1)}, bf16[2,2,64,512]{3,2,1,0:T(8,128)(2,1)S(1)}, u32[]{:S(2)}, u32[]{:S(2)}) collective-permute-start(bf16[2,2,64,512]{3,2,1,0:T(8,128)(2,1)S(1)} %pad_maximum_fusion.2), channel_id=1, source_target_pairs={{0,16},{16,0},{1,17},{17,1},{2,18},{18,2},{3,19},{19,3},{4,20},{20... | collective-permute-start | bytes 786440 | tf_op jit(solution)/shard_map/ppermute | solution.py:28
  83.9 21.1 %copy-start.38 = (s32[2,2]{1,0:T(2,128)}, s32[2,2]{1,0:T(2,128)S(1)}, u32[]{:S(2)}) copy-start(s32[2,2]{1,0:T(2,128)S(1)} %collective-permute-done.rank_b) | copy-start | bytes 52
  83.9 18.7 %collective-permute-start.13 = (bf16[2,2,64,512]{3,2,1,0:T(8,128)(2,1)S(1)}, bf16[2,2,64,512]{3,2,1,0:T(8,128)(2,1)S(1)}, u32[]{:S(2)}, u32[]{:S(2)}) collective-permute-start(bf16[2,2,64,512]{3,2,1,0:T(8,128)(2,1)S(1)} %pad_maximum_fusion.3), channel_id=1, source_target_pairs={{0,16},{16,0},{1,17},{17,1},{2,18},{18,2},{3,19},{19,3},{4,20},{20... | collective-permute-start | bytes 786440 | tf_op jit(solution)/shard_map/ppermute | solution.py:28
  91.4 13.6 %copy-start.31 = (bf16[3,2,64,512]{3,2,1,0:T(8,128)(2,1)}, bf16[3,2,64,512]{3,2,1,0:T(8,128)(2,1)S(1)}, u32[]{:S(2)}) copy-start(bf16[3,2,64,512]{3,2,1,0:T(8,128)(2,1)S(1)} %collective-permute-done.11.refs_9_) | copy-start | bytes 1179652
  91.4 6.5 %collective-permute-start.31 = (bf16[2,256,128]{2,1,0:T(8,128)(2,1)S(1)}, bf16[2,256,128]{2,1,0:T(8,128)(2,1)S(1)}, u32[]{:S(2)}, u32[]{:S(2)}) collective-permute-start(bf16[2,256,128]{2,1,0:T(8,128)(2,1)S(1)} %constant_dynamic-slice_fusion), channel_id=1, source_target_pairs={{0,8},{4,12},{8,0},{12,4},{1,9},{5,13},{9,1},{13,5},{2,10},{6,14},... | collective-permute-start | bytes 393224 | tf_op jit(solution)/shard_map/ppermute | solution.py:28
  97.9 7.1 %collective-permute-start.14 = (bf16[1,2,64,512]{3,2,1,0:T(8,128)(2,1)S(1)}, bf16[1,2,64,512]{3,2,1,0:T(8,128)(2,1)S(1)}, u32[]{:S(2)}, u32[]{:S(2)}) collective-permute-start(bf16[1,2,64,512]{3,2,1,0:T(8,128)(2,1)S(1)} %slice_bitcast_fusion.2), channel_id=1, source_target_pairs={{0,16},{16,0},{1,17},{17,1},{2,18},{18,2},{3,19},{19,3},{4,20},{20... | collective-permute-start | bytes 393224 | tf_op jit(solution)/shard_map/ppermute | solution.py:28
  98.7 6.3 %copy-start.32 = (bf16[2,2,64,512]{3,2,1,0:T(8,128)(2,1)}, bf16[2,2,64,512]{3,2,1,0:T(8,128)(2,1)S(1)}, u32[]{:S(2)}) copy-start(bf16[2,2,64,512]{3,2,1,0:T(8,128)(2,1)S(1)} %collective-permute-done.12.refs_10_) | copy-start | bytes 786436
  102.7 2.4 %copy-start.33 = (bf16[2,2,64,512]{3,2,1,0:T(8,128)(2,1)}, bf16[2,2,64,512]{3,2,1,0:T(8,128)(2,1)S(1)}, u32[]{:S(2)}) copy-start(bf16[2,2,64,512]{3,2,1,0:T(8,128)(2,1)S(1)} %collective-permute-done.13.refs_11_) | copy-start | bytes 786436
  112.6 23.0 %copy-start.9 = (bf16[2,1024,256]{2,1,0:T(8,128)(2,1)S(1)}, bf16[2,1024,256]{2,1,0:T(8,128)(2,1)}, u32[]{:S(2)}) copy-start(bf16[2,1024,256]{2,1,0:T(8,128)(2,1)} %copy-done.8) | copy-start | bytes 3145732
  119.7 25.1 %copy-start.36 = (bf16[1024,128]{1,0:T(8,128)(2,1)S(1)}, bf16[1024,128]{1,0:T(8,128)(2,1)}, u32[]{:S(2)}) copy-start(bf16[1024,128]{1,0:T(8,128)(2,1)} %get-tuple-element.29) | copy-start | bytes 786436
  119.7 35.8 %copy-start.10 = (bf16[2,1024,128]{2,1,0:T(8,128)(2,1)S(1)}, bf16[2,1024,128]{2,1,0:T(8,128)(2,1)}, u32[]{:S(2)}) copy-start(bf16[2,1024,128]{2,1,0:T(8,128)(2,1)} %get-tuple-element.26.own_ref) | copy-start | bytes 1572868
  119.7 35.8 %copy-start.29 = (s32[5]{0:T(128)S(1)}, s32[5]{0:T(128)}, u32[]{:S(2)}) copy-start(s32[5]{0:T(128)} %copy-done.28) | copy-start | bytes 64
  119.7 25.0 %collective-permute-start.17 = (bf16[2,1024,128]{2,1,0:T(8,128)(2,1)}, bf16[2,1024,128]{2,1,0:T(8,128)(2,1)S(1)}, u32[]{:S(2)}, u32[]{:S(2)}) collective-permute-start(bf16[2,1024,128]{2,1,0:T(8,128)(2,1)} %get-tuple-element.27), channel_id=1, source_target_pairs={{0,4},{4,8},{8,12},{12,0},{1,5},{5,9},{9,13},{13,1},{2,6},{6,10},{... | collective-permute-start | bytes 1572872 | tf_op jit(solution)/shard_map/ppermute | solution.py:23
  120.8 13.9 %collective-permute-start.32 = (bf16[256,128]{1,0:T(8,128)(2,1)}, bf16[256,128]{1,0:T(8,128)(2,1)}, u32[]{:S(2)}, u32[]{:S(2)}) collective-permute-start(bf16[256,128]{1,0:T(8,128)(2,1)} %dynamic-slice_bitcast_fusion), channel_id=1, source_target_pairs={{0,4},{4,0},{8,12},{12,8},{1,5},{5,1},{9,13},{13,9},{2,6},{6,2},{1... | collective-permute-start | bytes 196616 | tf_op jit(solution)/shard_map/ppermute | solution.py:28
  122.5 22.4 %copy-start.35 = (bf16[1024,128]{1,0:T(8,128)(2,1)S(1)}, bf16[1024,128]{1,0:T(8,128)(2,1)}, u32[]{:S(2)}) copy-start(bf16[1024,128]{1,0:T(8,128)(2,1)} %get-tuple-element.30) | copy-start | bytes 786436
  122.5 22.4 %collective-permute-start.18 = (bf16[2,1024,128]{2,1,0:T(8,128)(2,1)}, bf16[2,1024,128]{2,1,0:T(8,128)(2,1)S(1)}, u32[]{:S(2)}, u32[]{:S(2)}) collective-permute-start(bf16[2,1024,128]{2,1,0:T(8,128)(2,1)} %get-tuple-element.28), channel_id=1, source_target_pairs={{0,12},{4,0},{8,4},{12,8},{1,13},{5,1},{9,5},{13,9},{2,14},{6,2},{... | collective-permute-start | bytes 1572872 | tf_op jit(solution)/shard_map/ppermute | solution.py:23
  136.1 6.6 %collective-permute-start.33 = (bf16[512,128]{1,0:T(8,128)(2,1)S(1)}, bf16[512,128]{1,0:T(8,128)(2,1)S(1)}, u32[]{:S(2)}, u32[]{:S(2)}) collective-permute-start(bf16[512,128]{1,0:T(8,128)(2,1)S(1)} %sweep_part.1), channel_id=1, source_target_pairs={{0,16},{16,0},{1,17},{17,1},{2,18},{18,2},{3,19},{19,3},{4,20},{20... | collective-permute-start | bytes 393224 | tf_op jit(solution)/shard_map/ppermute | solution.py:28
  142.7 5.0 %collective-permute-start.35 = (bf16[512,128]{1,0:T(8,128)(2,1)S(1)}, bf16[512,128]{1,0:T(8,128)(2,1)S(1)}, u32[]{:S(2)}, u32[]{:S(2)}) collective-permute-start(bf16[512,128]{1,0:T(8,128)(2,1)S(1)} %add.44), channel_id=1, source_target_pairs={{0,32},{32,64},{64,96},{96,128},{128,160},{160,192},{192,224},{224... | collective-permute-start | bytes 393224 | tf_op jit(solution)/shard_map/ppermute | solution.py:23
  143.7 5.0 %collective-permute-start.34 = (bf16[512,128]{1,0:T(8,128)(2,1)S(1)}, bf16[512,128]{1,0:T(8,128)(2,1)S(1)}, u32[]{:S(2)}, u32[]{:S(2)}) collective-permute-start(bf16[512,128]{1,0:T(8,128)(2,1)S(1)} %add.44), channel_id=1, source_target_pairs={{0,224},{32,0},{64,32},{96,64},{128,96},{160,128},{192,160},{224,1... | collective-permute-start | bytes 393224 | tf_op jit(solution)/shard_map/ppermute | solution.py:23
  144.8 10.7 %collective-permute-start.19 = (bf16[1024,128]{1,0:T(8,128)(2,1)S(1)}, bf16[1024,128]{1,0:T(8,128)(2,1)S(1)}, u32[]{:S(2)}, u32[]{:S(2)}) collective-permute-start(bf16[1024,128]{1,0:T(8,128)(2,1)S(1)} %fusion.3), channel_id=1, source_target_pairs={{0,4},{4,8},{8,12},{12,0},{1,5},{5,9},{9,13},{13,1},{2,6},{6,10},{... | collective-permute-start | bytes 786440 | tf_op jit(solution)/shard_map/ppermute | solution.py:23
  145.0 10.5 %collective-permute-start.20 = (bf16[1024,128]{1,0:T(8,128)(2,1)S(1)}, bf16[1024,128]{1,0:T(8,128)(2,1)S(1)}, u32[]{:S(2)}, u32[]{:S(2)}) collective-permute-start(bf16[1024,128]{1,0:T(8,128)(2,1)S(1)} %fusion.2), channel_id=1, source_target_pairs={{0,12},{4,0},{8,4},{12,8},{1,13},{5,1},{9,5},{13,9},{2,14},{6,2},{... | collective-permute-start | bytes 786440 | tf_op jit(solution)/shard_map/ppermute | solution.py:23
  148.7 11.8 %collective-permute-start.37 = (bf16[512,128]{1,0:T(8,128)(2,1)S(1)}, bf16[512,128]{1,0:T(8,128)(2,1)S(1)}, u32[]{:S(2)}, u32[]{:S(2)}) collective-permute-start(bf16[512,128]{1,0:T(8,128)(2,1)S(1)} %get-tuple-element.38), channel_id=1, source_target_pairs={{0,96},{32,128},{64,160},{96,192},{128,224},{160,0},{192,32},{224,... | collective-permute-start | bytes 393224 | tf_op jit(solution)/shard_map/ppermute | solution.py:23
  155.5 9.3 %collective-permute-start.36 = (bf16[512,128]{1,0:T(8,128)(2,1)S(1)}, bf16[512,128]{1,0:T(8,128)(2,1)S(1)}, u32[]{:S(2)}, u32[]{:S(2)}) collective-permute-start(bf16[512,128]{1,0:T(8,128)(2,1)S(1)} %get-tuple-element.37), channel_id=1, source_target_pairs={{0,160},{32,192},{64,224},{96,0},{128,32},{160,64},{192,96},{224,1... | collective-permute-start | bytes 393224 | tf_op jit(solution)/shard_map/ppermute | solution.py:23
  156.5 9.8 %collective-permute-start.21 = (bf16[1024,128]{1,0:T(8,128)(2,1)S(1)}, bf16[1024,128]{1,0:T(8,128)(2,1)S(1)}, u32[]{:S(2)}, u32[]{:S(2)}) collective-permute-start(bf16[1024,128]{1,0:T(8,128)(2,1)S(1)} %get-tuple-element.32), channel_id=1, source_target_pairs={{0,2},{2,0},{1,3},{3,1},{4,6},{6,4},{5,7},{7,5},{8,10},{10,8},{9,1... | collective-permute-start | bytes 786440 | tf_op jit(solution)/shard_map/ppermute | solution.py:28
  (13 other events, 9.9 us)

commit v4 on v3

--- a/solution.py
+++ b/solution.py
@@ -157,9 +157,9 @@
     )(at, panel_rank, a, b, u, early)
 
 
-def part_kernel(p_ref, v_ref, out_ref):
+def part_kernel(at, held_ref, got_ref, v_ref, out_ref):
     lane = lax.broadcasted_iota(jnp.int32, (1, 128), 1)
-    p = p_ref[...]
+    p = jnp.where(lax.rem(at[2], 2) == lax.rem(at[0] // 2, 2), held_ref[...], got_ref[...])
     zero = jnp.zeros_like(p)
     s = jnp.dot(v_ref[0], jnp.where(lane < 64, p, zero), preferred_element_type=F32)
     s += jnp.dot(v_ref[1], jnp.where(lane < 64, zero, p), preferred_element_type=F32)
@@ -167,16 +167,16 @@
     out_ref[...] = jnp.where(lane < 64, s[:512], s[512:]).astype(BF)
 
 
-def sweep_part(p, v):
+def sweep_part(at, held, got, v):
     return pl.pallas_call(
         part_kernel,
         out_shape=jax.ShapeDtypeStruct((512, 128), BF),
-        in_specs=[VMEM, VMEM],
+        in_specs=[SMEM, VMEM, VMEM, VMEM],
         out_specs=VMEM,
         compiler_params=pltpu.CompilerParams(vmem_limit_bytes=8 << 20),
         cost_estimate=pl.CostEstimate(flops=2 * 2 * 256 * 1024 * 128, bytes_accessed=2 << 20, transcendentals=0),
         name="sweep_part",
-    )(p, v)
+    )(at, held, got, v)
 
 
 def base_kernel(i, at, rank_a, rank_b, *refs):
@@ -409,8 +409,7 @@
     two = jnp.where(y == z // 2, lax.dynamic_slice_in_dim(row, 2 * high, 2, 0), got)
     low = lax.rem(y, 2)
     got = swap(lax.dynamic_index_in_dim(two, 1 - low, 0, False), "y", 1)
-    block = jnp.where(low == lax.rem(z // 2, 2), lax.dynamic_index_in_dim(two, low, 0, False), got)
-    s = sweep_part(block, v)
+    s = sweep_part(at, lax.dynamic_index_in_dim(two, low, 0, False), got, v)
     s = s + swap(s, "xh")
     right = move(s, "z", -1)
     pair = s + right

time: 168 us -> 148 us (0.88)
  the two profiles are of different devices: /device:TPU:56 before, /device:TPU:16 now
where the time goes in v4:
time: 148 us; the launch traced here: 147 us
  waiting for transfers between devices  65.7 us (44%)
  starting transfers between devices  47.5 us (32%)
  Pallas kernels  25.2 us (17%)
  local copies, waits for them, and re-layouts  6.68 us (5%)
    ppermute x19, waiting for transfers between devices, swap(): return lax.ppermute(a, axis, [(i, i ^ k) for i in range(n)])  40 us
    ppermute x19, starting transfers between devices, move(): return lax.ppermute(a, axis, [(i, (i + k) % n) for i in range(n)])  31.7 us
    ppermute x19, waiting for transfers between devices, move(): return lax.ppermute(a, axis, [(i, (i + k) % n) for i in range(n)])  25.6 us
    ppermute x19, starting transfers between devices, swap(): return lax.ppermute(a, axis, [(i, i ^ k) for i in range(n)])  15.8 us
    pallas_call x2, Pallas kernels, base(): pl.pallas_call(functools.partial(base_kernel, i), out_shape=(two, two, tw...  14 us
    unnamed x64, local copies, waits for them, and re-layouts  6.46 us
  transfers between devices with their start and end apart: 38, of which 17 were waited for; matrix products, arithmetic and copies ran while one was open for 1% of the time, Pallas kernels for 16%

profile of v4, /device:TPU:16, one launch (start us, length us, event | category | flops | bytes accessed | tf_op | source)
XLA Modules:
  0.0 146.9 jit_solution(4880881427996873529)
XLA Ops:
  0.1 0.9 copy-done.20
  1.0 0.7 split_columns.1
  1.7 0.1 collective-permute-start.1
  1.8 1.3 collective-permute-done.1
  3.2 3.1 %collective-permute-start.2 = (bf16[2,64,512]{2,1,0:T(8,128)(2,1)S(1)}, bf16[2,64,512]{2,1,0:T(8,128)(2,1)S(1)}, u32[]{:S(2)}, u32[]{:S(2)}) collective-permute-start(bf16[2,64,512]{2,1,0:T(8,128)(2,1)S(1)} %get-tuple-element.39), channel_id=1, source_target_pairs={{0,16},{16,0},{1,17},{17,1},{2,18},{18,2},{3,19},{19,3},{4,20},{20... | collective-permute-start | bytes 393224 | tf_op jit(solution)/shard_map/ppermute | solution.py:28
  6.3 0.9 fusion.4
  7.2 0.7 collective-permute-start.22
  7.9 2.5 %collective-permute-done.2 = bf16[2,64,512]{2,1,0:T(8,128)(2,1)S(1)} collective-permute-done((bf16[2,64,512]{2,1,0:T(8,128)(2,1)S(1)}, bf16[2,64,512]{2,1,0:T(8,128)(2,1)S(1)}, u32[]{:S(2)}, u32[]{:S(2)}) %collective-permute-start.2) | collective-permute-done | bytes 131104 | tf_op jit(solution)/shard_map/ppermute | solution.py:28
  10.4 2.0 %collective-permute-start.3 = (bf16[3,2,64,512]{3,2,1,0:T(8,128)(2,1)S(1)}, bf16[3,2,64,512]{3,2,1,0:T(8,128)(2,1)S(1)}, u32[]{:S(2)}, u32[]{:S(2)}) collective-permute-start(bf16[3,2,64,512]{3,2,1,0:T(8,128)(2,1)S(1)} %fusion.refs_0_), channel_id=1, source_target_pairs={{0,32},{32,64},{64,96},{96,128},{128,160},{160,192},{192,224},{224... | collective-permute-start | bytes 1179656 | tf_op jit(solution)/shard_map/ppermute | solution.py:23
  12.4 4.0 %collective-permute-start.4 = (bf16[3,2,64,512]{3,2,1,0:T(8,128)(2,1)S(1)}, bf16[3,2,64,512]{3,2,1,0:T(8,128)(2,1)S(1)}, u32[]{:S(2)}, u32[]{:S(2)}) collective-permute-start(bf16[3,2,64,512]{3,2,1,0:T(8,128)(2,1)S(1)} %fusion.refs_0_), channel_id=1, source_target_pairs={{0,224},{32,0},{64,32},{96,64},{128,96},{160,128},{192,160},{224,1... | collective-permute-start | bytes 1179656 | tf_op jit(solution)/shard_map/ppermute | solution.py:23
  16.4 0.5 collective-permute-start.23
  17.0 0.5 collective-permute-start.16
  17.5 6.3 %collective-permute-done.23.refs_1_ = bf16[2,2,2,64,256]{4,3,2,1,0:T(8,128)(2,1)S(1)} collective-permute-done((bf16[2,2,2,64,256]{4,3,2,1,0:T(8,128)(2,1)S(1)}, bf16[2,2,2,64,256]{4,3,2,1,0:T(8,128)(2,1)S(1)}, u32[]{:S(2)}, u32[]{:S(2)}) %collective-permute-start.23) | collective-permute-done | bytes 262176 | tf_op jit(solution)/shard_map/ppermute | solution.py:23
  23.7 2.5 %collective-permute-start.24 = (bf16[2,2,2,64,256]{4,3,2,1,0:T(8,128)(2,1)S(1)}, bf16[2,2,2,64,256]{4,3,2,1,0:T(8,128)(2,1)}, u32[]{:S(2)}, u32[]{:S(2)}) collective-permute-start(bf16[2,2,2,64,256]{4,3,2,1,0:T(8,128)(2,1)S(1)} %pad_maximum_fusion.4.refs_0_), channel_id=1, source_target_pairs={{0,4},{4,8},{8,12},{12,0},{1,5},{5,9},{9,13},{13,1},{2,6},{6,10},{... | collective-permute-start | bytes 786440 | tf_op jit(solution)/shard_map/ppermute | solution.py:23
  26.3 3.2 %collective-permute-start.6 = (bf16[3,2,64,512]{3,2,1,0:T(8,128)(2,1)S(1)}, bf16[3,2,64,512]{3,2,1,0:T(8,128)(2,1)S(1)}, u32[]{:S(2)}, u32[]{:S(2)}) collective-permute-start(bf16[3,2,64,512]{3,2,1,0:T(8,128)(2,1)S(1)} %collective-permute-done.4.refs_2_), channel_id=1, source_target_pairs={{0,224},{32,0},{64,32},{96,64},{128,96},{160,128},{192,160},{224,1... | collective-permute-start | bytes 1179656 | tf_op jit(solution)/shard_map/ppermute | solution.py:23
  29.5 0.7 collective-permute-done.24.refs_3_
  30.2 0.7 copy-done.12
  30.9 6.0 %collective-permute-done.5.refs_3_ = bf16[3,2,64,512]{3,2,1,0:T(8,128)(2,1)S(1)} collective-permute-done((bf16[3,2,64,512]{3,2,1,0:T(8,128)(2,1)S(1)}, bf16[3,2,64,512]{3,2,1,0:T(8,128)(2,1)S(1)}, u32[]{:S(2)}, u32[]{:S(2)}) %collective-permute-start.5) | collective-permute-done | bytes 393248 | tf_op jit(solution)/shard_map/ppermute | solution.py:23
  36.9 3.2 %collective-permute-start.8 = (bf16[3,2,64,512]{3,2,1,0:T(8,128)(2,1)S(1)}, bf16[3,2,64,512]{3,2,1,0:T(8,128)(2,1)S(1)}, u32[]{:S(2)}, u32[]{:S(2)}) collective-permute-start(bf16[3,2,64,512]{3,2,1,0:T(8,128)(2,1)S(1)} %collective-permute-done.6.refs_4_), channel_id=1, source_target_pairs={{0,224},{32,0},{64,32},{96,64},{128,96},{160,128},{192,160},{224,1... | collective-permute-start | bytes 1179656 | tf_op jit(solution)/shard_map/ppermute | solution.py:23
  40.2 0.7 copy-done.16
  40.9 0.4 collective-permute-start.25
  41.2 6.3 %collective-permute-done.25.refs_2_ = bf16[2,2,2,64,256]{4,3,2,1,0:T(8,128)(2,1)} collective-permute-done((bf16[2,2,2,64,256]{4,3,2,1,0:T(8,128)(2,1)}, bf16[2,2,2,64,256]{4,3,2,1,0:T(8,128)(2,1)}, u32[]{:S(2)}, u32[]{:S(2)}) %collective-permute-start.25) | collective-permute-done | bytes 262176 | tf_op jit(solution)/shard_map/ppermute | solution.py:23
  47.6 0.7 copy-done.14
  48.3 0.5 collective-permute-start.29
  48.8 0.3 collective-permute-start.28
  49.2 0.7 copy-done.18
  49.9 0.4 collective-permute-done.29.refs_7_
  50.3 2.8 %collective-permute-start.10 = (bf16[3,64,512]{2,1,0:T(8,128)(2,1)S(1)}, bf16[3,64,512]{2,1,0:T(8,128)(2,1)S(1)}, u32[]{:S(2)}, u32[]{:S(2)}) collective-permute-start(bf16[3,64,512]{2,1,0:T(8,128)(2,1)S(1)} %slice.45), channel_id=1, source_target_pairs={{0,224},{32,0},{64,32},{96,64},{128,96},{160,128},{192,160},{224,1... | collective-permute-start | bytes 589832 | tf_op jit(solution)/shard_map/ppermute | solution.py:23
  53.2 1.7 %collective-permute-start.11 = (bf16[3,2,64,512]{3,2,1,0:T(8,128)(2,1)S(1)}, bf16[3,2,64,512]{3,2,1,0:T(8,128)(2,1)S(1)}, u32[]{:S(2)}, u32[]{:S(2)}) collective-permute-start(bf16[3,2,64,512]{3,2,1,0:T(8,128)(2,1)S(1)} %fusion.1), channel_id=1, source_target_pairs={{0,16},{16,0},{1,17},{17,1},{2,18},{18,2},{3,19},{19,3},{4,20},{20... | collective-permute-start | bytes 1179656 | tf_op jit(solution)/shard_map/ppermute | solution.py:28
  54.9 0.9 copy-done.19
  55.9 2.4 %whole_panel.1 = (bf16[2,1024,256]{2,1,0:T(8,128)(2,1)S(1)}, bf16[2,1024,256]{2,1,0:T(8,128)(2,1)S(1)}) custom-call(s32[5]{0:T(128)S(1)} %stack.62.at, bf16[2,2,2,64,256]{4,3,2,1,0:T(8,128)(2,1)S(1)} %copy-done.13, bf16[2,2,2,64,256]{4,3,2,1,0:T(8,128)(2,1)S(1)} %copy-done.15, bf16[2,2,2,64,256]{4,3,2,1,0:T(8,128)(2,1)} %collective-permute-done.25.refs_2_, ...), custom_call_target="tpu_custom_call" | custom-call | bytes 4194304 | tf_op jit(solution)/shard_map/whole_panel/pallas_call | solution.py:366
  58.3 1.0 copy-done.7
  59.5 2.6 %project_early.1.early_ref = f32[2,256,512]{2,1,0:T(8,128)S(1)} custom-call(s32[5]{0:T(128)S(1)} %stack.62.at, bf16[3,2,64,512]{3,2,1,0:T(8,128)(2,1)S(1)} %fusion.refs_0_, bf16[3,2,64,512]{3,2,1,0:T(8,128)(2,1)S(1)} %collective-permute-done.3.refs_1_, bf16[3,2,64,512]{3,2,1,0:T(8,128)(2,1)S(1)} %collective-permute-done.4.refs_2_, ...), custom_call_target="tpu_custom_call" | custom-call | flops 536870912 | bytes 4194304 | tf_op jit(solution)/shard_map/project_early/pallas_call | solution.py:107
  62.3 1.3 project.1
  63.6 0.8 collective-permute-start.30
  64.5 2.8 %collective-permute-start.12 = (bf16[2,2,64,512]{3,2,1,0:T(8,128)(2,1)S(1)}, bf16[2,2,64,512]{3,2,1,0:T(8,128)(2,1)S(1)}, u32[]{:S(2)}, u32[]{:S(2)}) collective-permute-start(bf16[2,2,64,512]{3,2,1,0:T(8,128)(2,1)S(1)} %pad_maximum_fusion.2), channel_id=1, source_target_pairs={{0,16},{16,0},{1,17},{17,1},{2,18},{18,2},{3,19},{19,3},{4,20},{20... | collective-permute-start | bytes 786440 | tf_op jit(solution)/shard_map/ppermute | solution.py:28
  67.3 0.8 collective-permute-start.13
  68.1 4.7 %collective-permute-done.30 = bf16[4,256,128]{2,1,0:T(8,128)(2,1)S(1)} collective-permute-done((bf16[4,256,128]{2,1,0:T(8,128)(2,1)S(1)}, bf16[4,256,128]{2,1,0:T(8,128)(2,1)S(1)}, u32[]{:S(2)}, u32[]{:S(2)}) %collective-permute-start.30) | collective-permute-done | bytes 262176 | tf_op jit(solution)/shard_map/ppermute | solution.py:28
  72.8 1.9 %collective-permute-start.14 = (bf16[1,2,64,512]{3,2,1,0:T(8,128)(2,1)S(1)}, bf16[1,2,64,512]{3,2,1,0:T(8,128)(2,1)S(1)}, u32[]{:S(2)}, u32[]{:S(2)}) collective-permute-start(bf16[1,2,64,512]{3,2,1,0:T(8,128)(2,1)S(1)} %slice_bitcast_fusion.2), channel_id=1, source_target_pairs={{0,16},{16,0},{1,17},{17,1},{2,18},{18,2},{3,19},{19,3},{4,20},{20... | collective-permute-start | bytes 393224 | tf_op jit(solution)/shard_map/ppermute | solution.py:28
  74.8 5.1 %collective-permute-done.12.refs_10_ = bf16[2,2,64,512]{3,2,1,0:T(8,128)(2,1)S(1)} collective-permute-done((bf16[2,2,64,512]{3,2,1,0:T(8,128)(2,1)S(1)}, bf16[2,2,64,512]{3,2,1,0:T(8,128)(2,1)S(1)}, u32[]{:S(2)}, u32[]{:S(2)}) %collective-permute-start.12) | collective-permute-done | bytes 262176 | tf_op jit(solution)/shard_map/ppermute | solution.py:28
  79.9 0.6 collective-permute-start.31
  80.6 5.0 %collective-permute-done.13.refs_11_ = bf16[2,2,64,512]{3,2,1,0:T(8,128)(2,1)S(1)} collective-permute-done((bf16[2,2,64,512]{3,2,1,0:T(8,128)(2,1)S(1)}, bf16[2,2,64,512]{3,2,1,0:T(8,128)(2,1)S(1)}, u32[]{:S(2)}, u32[]{:S(2)}) %collective-permute-start.13) | collective-permute-done | bytes 262176 | tf_op jit(solution)/shard_map/ppermute | solution.py:28
  85.5 2.3 %collective-permute-done.14.refs_12_ = bf16[1,2,64,512]{3,2,1,0:T(8,128)(2,1)S(1)} collective-permute-done((bf16[1,2,64,512]{3,2,1,0:T(8,128)(2,1)S(1)}, bf16[1,2,64,512]{3,2,1,0:T(8,128)(2,1)S(1)}, u32[]{:S(2)}, u32[]{:S(2)}) %collective-permute-start.14) | collective-permute-done | bytes 131104 | tf_op jit(solution)/shard_map/ppermute | solution.py:28
  87.9 0.6 copy-done.27
  88.5 6.9 %shard_map.73 = (bf16[2,1024,128]{2,1,0:T(8,128)(2,1)}, bf16[2,1024,128]{2,1,0:T(8,128)(2,1)}, bf16[2,1024,128]{2,1,0:T(8,128)(2,1)}, bf16[1024,128]{1,0:T(8,128)(2,1)}) custom-call(s32[5]{0:T(128)} %copy-done.21, s32[2,2]{1,0:T(2,128)} %rank_a.3, s32[2,2]{1,0:T(2,128)} %copy-done.31, bf16[3,2,64,512]{3,2,1,0:T(8,128)(2,1)} %copy-done, ...), custom_call_target="tpu_custom_call" | custom-call | flops 2147483648 | bytes 9437184 | tf_op jit(solution)/shard_map/pallas_call | solution.py:249
  95.5 7.1 %shard_map.74 = (bf16[2,1024,128]{2,1,0:T(8,128)(2,1)}, bf16[2,1024,128]{2,1,0:T(8,128)(2,1)}, bf16[2,1024,128]{2,1,0:T(8,128)(2,1)}, bf16[1024,128]{1,0:T(8,128)(2,1)}) custom-call(s32[5]{0:T(128)} %copy-done.21, s32[2,2]{1,0:T(2,128)} %rank_a.3, s32[2,2]{1,0:T(2,128)} %copy-done.31, ...), custom_call_target="tpu_custom_call", output_to_operand_aliasing={{0}: (20, {}), {1}: (21, {}), {2}: (22, {})} | custom-call | flops 2147483648 | bytes 9437184 | tf_op jit(solution)/shard_map/pallas_call | solution.py:249
  102.6 0.4 collective-permute-start.17
  103.1 2.0 %collective-permute-start.18 = (bf16[2,1024,128]{2,1,0:T(8,128)(2,1)}, bf16[2,1024,128]{2,1,0:T(8,128)(2,1)S(1)}, u32[]{:S(2)}, u32[]{:S(2)}) collective-permute-start(bf16[2,1024,128]{2,1,0:T(8,128)(2,1)} %get-tuple-element.28), channel_id=1, source_target_pairs={{0,12},{4,0},{8,4},{12,8},{1,13},{5,1},{9,5},{13,9},{2,14},{6,2},{... | collective-permute-start | bytes 1572872 | tf_op jit(solution)/shard_map/ppermute | solution.py:23
  105.0 0.4 collective-permute-start.32
  105.5 12.7 %collective-permute-done.32.got_ref = bf16[256,128]{1,0:T(8,128)(2,1)S(1)} collective-permute-done((bf16[256,128]{1,0:T(8,128)(2,1)S(1)}, bf16[256,128]{1,0:T(8,128)(2,1)S(1)}, u32[]{:S(2)}, u32[]{:S(2)}) %collective-permute-start.32) | collective-permute-done | bytes 65568 | tf_op jit(solution)/shard_map/ppermute | solution.py:28
  118.2 1.1 sweep_part.1
  119.2 1.3 collective-permute-start.33
  120.5 5.3 %collective-permute-done.33 = bf16[512,128]{1,0:T(8,128)(2,1)S(1)} collective-permute-done((bf16[512,128]{1,0:T(8,128)(2,1)S(1)}, bf16[512,128]{1,0:T(8,128)(2,1)S(1)}, u32[]{:S(2)}, u32[]{:S(2)}) %collective-permute-start.33) | collective-permute-done | bytes 131104 | tf_op jit(solution)/shard_map/ppermute | solution.py:28
  125.9 3.2 %collective-permute-start.34 = (bf16[512,128]{1,0:T(8,128)(2,1)S(1)}, bf16[512,128]{1,0:T(8,128)(2,1)S(1)}, u32[]{:S(2)}, u32[]{:S(2)}) collective-permute-start(bf16[512,128]{1,0:T(8,128)(2,1)S(1)} %add.44), channel_id=1, source_target_pairs={{0,224},{32,0},{64,32},{96,64},{128,96},{160,128},{192,160},{224,1... | collective-permute-start | bytes 393224 | tf_op jit(solution)/shard_map/ppermute | solution.py:23
  129.3 2.1 %collective-permute-start.20 = (bf16[1024,128]{1,0:T(8,128)(2,1)S(1)}, bf16[1024,128]{1,0:T(8,128)(2,1)S(1)}, u32[]{:S(2)}, u32[]{:S(2)}) collective-permute-start(bf16[1024,128]{1,0:T(8,128)(2,1)S(1)} %fusion.2), channel_id=1, source_target_pairs={{0,12},{4,0},{8,4},{12,8},{1,13},{5,1},{9,5},{13,9},{2,14},{6,2},{... | collective-permute-start | bytes 786440 | tf_op jit(solution)/shard_map/ppermute | solution.py:23
  131.4 2.2 %collective-permute-done.35 = bf16[512,128]{1,0:T(8,128)(2,1)S(1)} collective-permute-done((bf16[512,128]{1,0:T(8,128)(2,1)S(1)}, bf16[512,128]{1,0:T(8,128)(2,1)S(1)}, u32[]{:S(2)}, u32[]{:S(2)}) %collective-permute-start.35) | collective-permute-done | bytes 131104 | tf_op jit(solution)/shard_map/ppermute | solution.py:23
  133.6 2.7 %collective-permute-start.37 = (bf16[512,128]{1,0:T(8,128)(2,1)S(1)}, bf16[512,128]{1,0:T(8,128)(2,1)S(1)}, u32[]{:S(2)}, u32[]{:S(2)}) collective-permute-start(bf16[512,128]{1,0:T(8,128)(2,1)S(1)} %get-tuple-element.38), channel_id=1, source_target_pairs={{0,96},{32,128},{64,160},{96,192},{128,224},{160,0},{192,32},{224,... | collective-permute-start | bytes 393224 | tf_op jit(solution)/shard_map/ppermute | solution.py:23
  136.3 2.4 %collective-permute-start.36 = (bf16[512,128]{1,0:T(8,128)(2,1)S(1)}, bf16[512,128]{1,0:T(8,128)(2,1)S(1)}, u32[]{:S(2)}, u32[]{:S(2)}) collective-permute-start(bf16[512,128]{1,0:T(8,128)(2,1)S(1)} %get-tuple-element.37), channel_id=1, source_target_pairs={{0,160},{32,192},{64,224},{96,0},{128,32},{160,64},{192,96},{224,1... | collective-permute-start | bytes 393224 | tf_op jit(solution)/shard_map/ppermute | solution.py:23
  138.7 0.9 pack.1
  139.7 2.1 %collective-permute-done.37 = bf16[512,128]{1,0:T(8,128)(2,1)S(1)} collective-permute-done((bf16[512,128]{1,0:T(8,128)(2,1)S(1)}, bf16[512,128]{1,0:T(8,128)(2,1)S(1)}, u32[]{:S(2)}, u32[]{:S(2)}) %collective-permute-start.37) | collective-permute-done | bytes 131104 | tf_op jit(solution)/shard_map/ppermute | solution.py:23
  141.8 2.0 %collective-permute-done.36 = bf16[512,128]{1,0:T(8,128)(2,1)S(1)} collective-permute-done((bf16[512,128]{1,0:T(8,128)(2,1)S(1)}, bf16[512,128]{1,0:T(8,128)(2,1)S(1)}, u32[]{:S(2)}, u32[]{:S(2)}) %collective-permute-start.36) | collective-permute-done | bytes 131104 | tf_op jit(solution)/shard_map/ppermute | solution.py:23
  143.9 1.5 late.1.late_ref
  145.3 0.7 collective-permute-done.21.came_ref
  146.1 0.8 last.1
  (112 shorter events, 1.1 us)
Async XLA Ops:
  1.0 61.2 %copy-start.21 = (s32[5]{0:T(128)}, s32[5]{0:T(128)S(1)}, u32[]{:S(2)}) copy-start(s32[5]{0:T(128)S(1)} %stack.62.at) | copy-start | bytes 64
  1.7 1.4 collective-permute-start.1
  3.2 7.2 %collective-permute-start.2 = (bf16[2,64,512]{2,1,0:T(8,128)(2,1)S(1)}, bf16[2,64,512]{2,1,0:T(8,128)(2,1)S(1)}, u32[]{:S(2)}, u32[]{:S(2)}) collective-permute-start(bf16[2,64,512]{2,1,0:T(8,128)(2,1)S(1)} %get-tuple-element.39), channel_id=1, source_target_pairs={{0,16},{16,0},{1,17},{17,1},{2,18},{18,2},{3,19},{19,3},{4,20},{20... | collective-permute-start | bytes 393224 | tf_op jit(solution)/shard_map/ppermute | solution.py:28
  7.2 9.2 %collective-permute-start.22 = (bf16[2,2,64,256]{3,2,1,0:T(8,128)(2,1)S(1)}, bf16[2,2,64,256]{3,2,1,0:T(8,128)(2,1)S(1)}, u32[]{:S(2)}, u32[]{:S(2)}) collective-permute-start(bf16[2,2,64,256]{3,2,1,0:T(8,128)(2,1)S(1)} %get-tuple-element.44), channel_id=1, source_target_pairs={{0,2},{2,0},{1,3},{3,1},{4,6},{6,4},{5,7},{7,5},{8,10},{10,8},{9,1... | collective-permute-start | bytes 393224 | tf_op jit(solution)/shard_map/ppermute | solution.py:28
  10.4 49.0 %copy-start = (bf16[3,2,64,512]{3,2,1,0:T(8,128)(2,1)}, bf16[3,2,64,512]{3,2,1,0:T(8,128)(2,1)S(1)}, u32[]{:S(2)}) copy-start(bf16[3,2,64,512]{3,2,1,0:T(8,128)(2,1)S(1)} %fusion.refs_0_) | copy-start | bytes 1179652
  10.4 15.8 %collective-permute-start.3 = (bf16[3,2,64,512]{3,2,1,0:T(8,128)(2,1)S(1)}, bf16[3,2,64,512]{3,2,1,0:T(8,128)(2,1)S(1)}, u32[]{:S(2)}, u32[]{:S(2)}) collective-permute-start(bf16[3,2,64,512]{3,2,1,0:T(8,128)(2,1)S(1)} %fusion.refs_0_), channel_id=1, source_target_pairs={{0,32},{32,64},{64,96},{96,128},{128,160},{160,192},{192,224},{224... | collective-permute-start | bytes 1179656 | tf_op jit(solution)/shard_map/ppermute | solution.py:23
  12.4 13.9 %collective-permute-start.4 = (bf16[3,2,64,512]{3,2,1,0:T(8,128)(2,1)S(1)}, bf16[3,2,64,512]{3,2,1,0:T(8,128)(2,1)S(1)}, u32[]{:S(2)}, u32[]{:S(2)}) collective-permute-start(bf16[3,2,64,512]{3,2,1,0:T(8,128)(2,1)S(1)} %fusion.refs_0_), channel_id=1, source_target_pairs={{0,224},{32,0},{64,32},{96,64},{128,96},{160,128},{192,160},{224,1... | collective-permute-start | bytes 1179656 | tf_op jit(solution)/shard_map/ppermute | solution.py:23
  16.4 7.3 %collective-permute-start.23 = (bf16[2,2,2,64,256]{4,3,2,1,0:T(8,128)(2,1)S(1)}, bf16[2,2,2,64,256]{4,3,2,1,0:T(8,128)(2,1)S(1)}, u32[]{:S(2)}, u32[]{:S(2)}) collective-permute-start(bf16[2,2,2,64,256]{4,3,2,1,0:T(8,128)(2,1)S(1)} %pad_maximum_fusion.4.refs_0_), channel_id=1, source_target_pairs={{0,12},{4,0},{8,4},{12,8},{1,13},{5,1},{9,5},{13,9},{2,14},{6,2},{... | collective-permute-start | bytes 786440 | tf_op jit(solution)/shard_map/ppermute | solution.py:23
  17.0 70.9 %collective-permute-start.15 = (bf16[2,2,1024,256]{3,2,1,0:T(8,128)(2,1)}, bf16[2,2,1024,256]{3,2,1,0:T(8,128)(2,1)}, u32[]{:S(2)}, u32[]{:S(2)}) collective-permute-start(bf16[2,2,1024,256]{3,2,1,0:T(8,128)(2,1)} %refs_13_.3), channel_id=1, source_target_pairs={{0,1},{1,0},{2,3},{3,2},{4,5},{5,4},{6,7},{7,6},{8,9},{9,8},{10,11... | collective-permute-start | bytes 6291464 | tf_op jit(solution)/shard_map/ppermute | solution.py:28
  17.0 70.9 %collective-permute-start.16 = (bf16[2,2,1024,256]{3,2,1,0:T(8,128)(2,1)}, bf16[2,2,1024,256]{3,2,1,0:T(8,128)(2,1)}, u32[]{:S(2)}, u32[]{:S(2)}) collective-permute-start(bf16[2,2,1024,256]{3,2,1,0:T(8,128)(2,1)} %refs_15_.3), channel_id=1, source_target_pairs={{0,1},{1,0},{2,3},{3,2},{4,5},{5,4},{6,7},{7,6},{8,9},{9,8},{10,11... | collective-permute-start | bytes 6291464 | tf_op jit(solution)/shard_map/ppermute | solution.py:28
  23.7 6.5 %collective-permute-start.24 = (bf16[2,2,2,64,256]{4,3,2,1,0:T(8,128)(2,1)S(1)}, bf16[2,2,2,64,256]{4,3,2,1,0:T(8,128)(2,1)}, u32[]{:S(2)}, u32[]{:S(2)}) collective-permute-start(bf16[2,2,2,64,256]{4,3,2,1,0:T(8,128)(2,1)S(1)} %pad_maximum_fusion.4.refs_0_), channel_id=1, source_target_pairs={{0,4},{4,8},{8,12},{12,0},{1,5},{5,9},{9,13},{13,1},{2,6},{6,10},{... | collective-permute-start | bytes 786440 | tf_op jit(solution)/shard_map/ppermute | solution.py:23
  26.2 33.2 %copy-start.3 = (bf16[3,2,64,512]{3,2,1,0:T(8,128)(2,1)}, bf16[3,2,64,512]{3,2,1,0:T(8,128)(2,1)S(1)}, u32[]{:S(2)}) copy-start(bf16[3,2,64,512]{3,2,1,0:T(8,128)(2,1)S(1)} %collective-permute-done.3.refs_1_) | copy-start | bytes 1179652
  26.2 10.7 %collective-permute-start.5 = (bf16[3,2,64,512]{3,2,1,0:T(8,128)(2,1)S(1)}, bf16[3,2,64,512]{3,2,1,0:T(8,128)(2,1)S(1)}, u32[]{:S(2)}, u32[]{:S(2)}) collective-permute-start(bf16[3,2,64,512]{3,2,1,0:T(8,128)(2,1)S(1)} %collective-permute-done.3.refs_1_), channel_id=1, source_target_pairs={{0,32},{32,64},{64,96},{96,128},{128,160},{160,192},{192,224},{224... | collective-permute-start | bytes 1179656 | tf_op jit(solution)/shard_map/ppermute | solution.py:23
  26.3 33.2 %copy-start.4 = (bf16[3,2,64,512]{3,2,1,0:T(8,128)(2,1)}, bf16[3,2,64,512]{3,2,1,0:T(8,128)(2,1)S(1)}, u32[]{:S(2)}) copy-start(bf16[3,2,64,512]{3,2,1,0:T(8,128)(2,1)S(1)} %collective-permute-done.4.refs_2_) | copy-start | bytes 1179652
  26.3 10.6 %collective-permute-start.6 = (bf16[3,2,64,512]{3,2,1,0:T(8,128)(2,1)S(1)}, bf16[3,2,64,512]{3,2,1,0:T(8,128)(2,1)S(1)}, u32[]{:S(2)}, u32[]{:S(2)}) collective-permute-start(bf16[3,2,64,512]{3,2,1,0:T(8,128)(2,1)S(1)} %collective-permute-done.4.refs_2_), channel_id=1, source_target_pairs={{0,224},{32,0},{64,32},{96,64},{128,96},{160,128},{192,160},{224,1... | collective-permute-start | bytes 1179656 | tf_op jit(solution)/shard_map/ppermute | solution.py:23
  30.2 9.9 %collective-permute-start.26 = (bf16[2,2,2,64,256]{4,3,2,1,0:T(8,128)(2,1)S(1)}, bf16[2,2,2,64,256]{4,3,2,1,0:T(8,128)(2,1)S(1)}, u32[]{:S(2)}, u32[]{:S(2)}) collective-permute-start(bf16[2,2,2,64,256]{4,3,2,1,0:T(8,128)(2,1)S(1)} %pad_maximum_fusion.4.refs_0_), channel_id=1, source_target_pairs={{0,1},{1,0},{2,3},{3,2},{4,5},{5,4},{6,7},{7,6},{8,9},{9,8},{10,11... | collective-permute-start | bytes 786440 | tf_op jit(solution)/shard_map/ppermute | solution.py:28
  36.9 22.5 %copy-start.5 = (bf16[3,2,64,512]{3,2,1,0:T(8,128)(2,1)}, bf16[3,2,64,512]{3,2,1,0:T(8,128)(2,1)S(1)}, u32[]{:S(2)}) copy-start(bf16[3,2,64,512]{3,2,1,0:T(8,128)(2,1)S(1)} %collective-permute-done.5.refs_3_) | copy-start | bytes 1179652
  36.9 11.4 %collective-permute-start.7 = (bf16[3,2,64,512]{3,2,1,0:T(8,128)(2,1)S(1)}, bf16[3,2,64,512]{3,2,1,0:T(8,128)(2,1)S(1)}, u32[]{:S(2)}, u32[]{:S(2)}) collective-permute-start(bf16[3,2,64,512]{3,2,1,0:T(8,128)(2,1)S(1)} %collective-permute-done.5.refs_3_), channel_id=1, source_target_pairs={{0,32},{32,64},{64,96},{96,128},{128,160},{160,192},{192,224},{224... | collective-permute-start | bytes 1179656 | tf_op jit(solution)/shard_map/ppermute | solution.py:23
  36.9 22.5 %copy-start.6 = (bf16[3,2,64,512]{3,2,1,0:T(8,128)(2,1)}, bf16[3,2,64,512]{3,2,1,0:T(8,128)(2,1)S(1)}, u32[]{:S(2)}) copy-start(bf16[3,2,64,512]{3,2,1,0:T(8,128)(2,1)S(1)} %collective-permute-done.6.refs_4_) | copy-start | bytes 1179652
  36.9 11.9 %collective-permute-start.8 = (bf16[3,2,64,512]{3,2,1,0:T(8,128)(2,1)S(1)}, bf16[3,2,64,512]{3,2,1,0:T(8,128)(2,1)S(1)}, u32[]{:S(2)}, u32[]{:S(2)}) collective-permute-start(bf16[3,2,64,512]{3,2,1,0:T(8,128)(2,1)S(1)} %collective-permute-done.6.refs_4_), channel_id=1, source_target_pairs={{0,224},{32,0},{64,32},{96,64},{128,96},{160,128},{192,160},{224,1... | collective-permute-start | bytes 1179656 | tf_op jit(solution)/shard_map/ppermute | solution.py:23
  40.9 6.7 %collective-permute-start.25 = (bf16[2,2,2,64,256]{4,3,2,1,0:T(8,128)(2,1)}, bf16[2,2,2,64,256]{4,3,2,1,0:T(8,128)(2,1)}, u32[]{:S(2)}, u32[]{:S(2)}) collective-permute-start(bf16[2,2,2,64,256]{4,3,2,1,0:T(8,128)(2,1)} %collective-permute-done.24.refs_3_), channel_id=1, source_target_pairs={{0,4},{4,8},{8,12},{12,0},{1,5},{5,9},{9,13},{13,1},{2,6},{6,10},{... | collective-permute-start | bytes 786440 | tf_op jit(solution)/shard_map/ppermute | solution.py:23
  47.6 1.6 %collective-permute-start.27 = (bf16[2,2,2,64,256]{4,3,2,1,0:T(8,128)(2,1)S(1)}, bf16[2,2,2,64,256]{4,3,2,1,0:T(8,128)(2,1)S(1)}, u32[]{:S(2)}, u32[]{:S(2)}) collective-permute-start(bf16[2,2,2,64,256]{4,3,2,1,0:T(8,128)(2,1)S(1)} %collective-permute-done.23.refs_1_), channel_id=1, source_target_pairs={{0,1},{1,0},{2,3},{3,2},{4,5},{5,4},{6,7},{7,6},{8,9},{9,8},{10,11... | collective-permute-start | bytes 786440 | tf_op jit(solution)/shard_map/ppermute | solution.py:28
  48.3 11.2 %copy-start.1 = (bf16[3,2,64,512]{3,2,1,0:T(8,128)(2,1)}, bf16[3,2,64,512]{3,2,1,0:T(8,128)(2,1)S(1)}, u32[]{:S(2)}) copy-start(bf16[3,2,64,512]{3,2,1,0:T(8,128)(2,1)S(1)} %collective-permute-done.7.refs_5_) | copy-start | bytes 1179652
  48.3 2.0 %collective-permute-start.29 = (bf16[2,2,2,64,256]{4,3,2,1,0:T(8,128)(2,1)}, bf16[2,2,2,64,256]{4,3,2,1,0:T(8,128)(2,1)}, u32[]{:S(2)}, u32[]{:S(2)}) collective-permute-start(bf16[2,2,2,64,256]{4,3,2,1,0:T(8,128)(2,1)} %collective-permute-done.24.refs_3_), channel_id=1, source_target_pairs={{0,1},{1,0},{2,3},{3,2},{4,5},{5,4},{6,7},{7,6},{8,9},{9,8},{10,11... | collective-permute-start | bytes 786440 | tf_op jit(solution)/shard_map/ppermute | solution.py:28
  48.8 10.7 %copy-start.2 = (bf16[3,2,64,512]{3,2,1,0:T(8,128)(2,1)}, bf16[3,2,64,512]{3,2,1,0:T(8,128)(2,1)S(1)}, u32[]{:S(2)}) copy-start(bf16[3,2,64,512]{3,2,1,0:T(8,128)(2,1)S(1)} %collective-permute-done.8.refs_6_) | copy-start | bytes 1179652
  48.8 4.4 %collective-permute-start.28 = (bf16[2,2,2,64,256]{4,3,2,1,0:T(8,128)(2,1)}, bf16[2,2,2,64,256]{4,3,2,1,0:T(8,128)(2,1)}, u32[]{:S(2)}, u32[]{:S(2)}) collective-permute-start(bf16[2,2,2,64,256]{4,3,2,1,0:T(8,128)(2,1)} %collective-permute-done.25.refs_2_), channel_id=1, source_target_pairs={{0,1},{1,0},{2,3},{3,2},{4,5},{5,4},{6,7},{7,6},{8,9},{9,8},{10,11... | collective-permute-start | bytes 786440 | tf_op jit(solution)/shard_map/ppermute | solution.py:28
  49.1 5.8 %copy-start.13 = (bf16[2,2,2,64,256]{4,3,2,1,0:T(8,128)(2,1)S(1)}, bf16[2,2,2,64,256]{4,3,2,1,0:T(8,128)(2,1)}, u32[]{:S(2)}) copy-start(bf16[2,2,2,64,256]{4,3,2,1,0:T(8,128)(2,1)} %copy-done.12) | copy-start | bytes 786436
  49.1 5.8 %copy-start.15 = (bf16[2,2,2,64,256]{4,3,2,1,0:T(8,128)(2,1)S(1)}, bf16[2,2,2,64,256]{4,3,2,1,0:T(8,128)(2,1)}, u32[]{:S(2)}) copy-start(bf16[2,2,2,64,256]{4,3,2,1,0:T(8,128)(2,1)} %copy-done.14) | copy-start | bytes 786436
  49.1 5.8 %copy-start.17 = (bf16[2,2,2,64,256]{4,3,2,1,0:T(8,128)(2,1)S(1)}, bf16[2,2,2,64,256]{4,3,2,1,0:T(8,128)(2,1)}, u32[]{:S(2)}) copy-start(bf16[2,2,2,64,256]{4,3,2,1,0:T(8,128)(2,1)} %copy-done.16) | copy-start | bytes 786436
  49.9 12.3 %collective-permute-start.9 = (bf16[3,64,512]{2,1,0:T(8,128)(2,1)S(1)}, bf16[3,64,512]{2,1,0:T(8,128)(2,1)S(1)}, u32[]{:S(2)}, u32[]{:S(2)}) collective-permute-start(bf16[3,64,512]{2,1,0:T(8,128)(2,1)S(1)} %slice.44), channel_id=1, source_target_pairs={{0,32},{32,64},{64,96},{96,128},{128,160},{160,192},{192,224},{224... | collective-permute-start | bytes 589832 | tf_op jit(solution)/shard_map/ppermute | solution.py:23
  50.3 12.0 %collective-permute-start.10 = (bf16[3,64,512]{2,1,0:T(8,128)(2,1)S(1)}, bf16[3,64,512]{2,1,0:T(8,128)(2,1)S(1)}, u32[]{:S(2)}, u32[]{:S(2)}) collective-permute-start(bf16[3,64,512]{2,1,0:T(8,128)(2,1)S(1)} %slice.45), channel_id=1, source_target_pairs={{0,224},{32,0},{64,32},{96,64},{128,96},{160,128},{192,160},{224,1... | collective-permute-start | bytes 589832 | tf_op jit(solution)/shard_map/ppermute | solution.py:23
  53.2 14.1 %collective-permute-start.11 = (bf16[3,2,64,512]{3,2,1,0:T(8,128)(2,1)S(1)}, bf16[3,2,64,512]{3,2,1,0:T(8,128)(2,1)S(1)}, u32[]{:S(2)}, u32[]{:S(2)}) collective-permute-start(bf16[3,2,64,512]{3,2,1,0:T(8,128)(2,1)S(1)} %fusion.1), channel_id=1, source_target_pairs={{0,16},{16,0},{1,17},{17,1},{2,18},{18,2},{3,19},{19,3},{4,20},{20... | collective-permute-start | bytes 1179656 | tf_op jit(solution)/shard_map/ppermute | solution.py:28
  54.9 1.0 copy-start.19
  58.3 1.0 copy-start.7
  59.5 2.7 %copy-start.30 = (s32[2,2]{1,0:T(2,128)S(1)}, s32[2,2]{1,0:T(2,128)}, u32[]{:S(2)}) copy-start(s32[2,2]{1,0:T(2,128)} %rank_a.3) | copy-start | bytes 52
  59.5 2.8 %copy-start.23 = (s32[32]{0:T(128)S(1)}, s32[32]{0:T(128)}, u32[]{:S(2)}) copy-start(s32[32]{0:T(128)} %rank.3) | copy-start | bytes 388
  62.2 12.6 %copy-start.9 = (bf16[3,64,512]{2,1,0:T(8,128)(2,1)}, bf16[3,64,512]{2,1,0:T(8,128)(2,1)S(1)}, u32[]{:S(2)}) copy-start(bf16[3,64,512]{2,1,0:T(8,128)(2,1)S(1)} %collective-permute-done.9.refs_7_.a_ref) | copy-start | bytes 589828
  62.2 2.3 %collective-permute-start = (s32[2,2]{1,0:T(2,128)S(1)}, s32[2,2]{1,0:T(2,128)S(1)}, u32[]{:S(2)}, u32[]{:S(2)}) collective-permute-start(s32[2,2]{1,0:T(2,128)S(1)} %copy-done.30), channel_id=1, source_target_pairs={{0,1},{1,0},{2,3},{3,2},{4,5},{5,4},{6,7},{7,6},{8,9},{9,8},{10,11... | collective-permute-start | bytes 56 | tf_op jit(solution)/shard_map/ppermute | solution.py:28
  62.3 12.5 %copy-start.11 = (bf16[3,64,512]{2,1,0:T(8,128)(2,1)}, bf16[3,64,512]{2,1,0:T(8,128)(2,1)S(1)}, u32[]{:S(2)}) copy-start(bf16[3,64,512]{2,1,0:T(8,128)(2,1)S(1)} %collective-permute-done.10.refs_8_.b_ref) | copy-start | bytes 589828
  63.6 9.3 %collective-permute-start.30 = (bf16[4,256,128]{2,1,0:T(8,128)(2,1)S(1)}, bf16[4,256,128]{2,1,0:T(8,128)(2,1)S(1)}, u32[]{:S(2)}, u32[]{:S(2)}) collective-permute-start(bf16[4,256,128]{2,1,0:T(8,128)(2,1)S(1)} %get-tuple-element.35), channel_id=1, source_target_pairs={{0,2},{2,0},{1,3},{3,1},{4,6},{6,4},{5,7},{7,5},{8,10},{10,8},{9,1... | collective-permute-start | bytes 786440 | tf_op jit(solution)/shard_map/ppermute | solution.py:28
  64.5 23.4 %copy-start.31 = (s32[2,2]{1,0:T(2,128)}, s32[2,2]{1,0:T(2,128)S(1)}, u32[]{:S(2)}) copy-start(s32[2,2]{1,0:T(2,128)S(1)} %collective-permute-done.rank_b) | copy-start | bytes 52
  64.5 15.5 %collective-permute-start.12 = (bf16[2,2,64,512]{3,2,1,0:T(8,128)(2,1)S(1)}, bf16[2,2,64,512]{3,2,1,0:T(8,128)(2,1)S(1)}, u32[]{:S(2)}, u32[]{:S(2)}) collective-permute-start(bf16[2,2,64,512]{3,2,1,0:T(8,128)(2,1)S(1)} %pad_maximum_fusion.2), channel_id=1, source_target_pairs={{0,16},{16,0},{1,17},{17,1},{2,18},{18,2},{3,19},{19,3},{4,20},{20... | collective-permute-start | bytes 786440 | tf_op jit(solution)/shard_map/ppermute | solution.py:28
  67.3 12.6 %copy-start.24 = (bf16[3,2,64,512]{3,2,1,0:T(8,128)(2,1)}, bf16[3,2,64,512]{3,2,1,0:T(8,128)(2,1)S(1)}, u32[]{:S(2)}) copy-start(bf16[3,2,64,512]{3,2,1,0:T(8,128)(2,1)S(1)} %collective-permute-done.11.refs_9_) | copy-start | bytes 1179652
  67.3 18.2 %collective-permute-start.13 = (bf16[2,2,64,512]{3,2,1,0:T(8,128)(2,1)S(1)}, bf16[2,2,64,512]{3,2,1,0:T(8,128)(2,1)S(1)}, u32[]{:S(2)}, u32[]{:S(2)}) collective-permute-start(bf16[2,2,64,512]{3,2,1,0:T(8,128)(2,1)S(1)} %pad_maximum_fusion.3), channel_id=1, source_target_pairs={{0,16},{16,0},{1,17},{17,1},{2,18},{18,2},{3,19},{19,3},{4,20},{20... | collective-permute-start | bytes 786440 | tf_op jit(solution)/shard_map/ppermute | solution.py:28
  72.8 15.0 %collective-permute-start.14 = (bf16[1,2,64,512]{3,2,1,0:T(8,128)(2,1)S(1)}, bf16[1,2,64,512]{3,2,1,0:T(8,128)(2,1)S(1)}, u32[]{:S(2)}, u32[]{:S(2)}) collective-permute-start(bf16[1,2,64,512]{3,2,1,0:T(8,128)(2,1)S(1)} %slice_bitcast_fusion.2), channel_id=1, source_target_pairs={{0,16},{16,0},{1,17},{17,1},{2,18},{18,2},{3,19},{19,3},{4,20},{20... | collective-permute-start | bytes 393224 | tf_op jit(solution)/shard_map/ppermute | solution.py:28
  79.9 8.0 %copy-start.25 = (bf16[2,2,64,512]{3,2,1,0:T(8,128)(2,1)}, bf16[2,2,64,512]{3,2,1,0:T(8,128)(2,1)S(1)}, u32[]{:S(2)}) copy-start(bf16[2,2,64,512]{3,2,1,0:T(8,128)(2,1)S(1)} %collective-permute-done.12.refs_10_) | copy-start | bytes 786436
  79.9 23.1 %collective-permute-start.31 = (bf16[2,256,128]{2,1,0:T(8,128)(2,1)S(1)}, bf16[2,256,128]{2,1,0:T(8,128)(2,1)S(1)}, u32[]{:S(2)}, u32[]{:S(2)}) collective-permute-start(bf16[2,256,128]{2,1,0:T(8,128)(2,1)S(1)} %constant_dynamic-slice_fusion), channel_id=1, source_target_pairs={{0,8},{4,12},{8,0},{12,4},{1,9},{5,13},{9,1},{13,5},{2,10},{6,14},... | collective-permute-start | bytes 393224 | tf_op jit(solution)/shard_map/ppermute | solution.py:28
  85.5 2.3 %copy-start.26 = (bf16[2,2,64,512]{3,2,1,0:T(8,128)(2,1)}, bf16[2,2,64,512]{3,2,1,0:T(8,128)(2,1)S(1)}, u32[]{:S(2)}) copy-start(bf16[2,2,64,512]{3,2,1,0:T(8,128)(2,1)S(1)} %collective-permute-done.13.refs_11_) | copy-start | bytes 786436
  95.5 22.7 %copy-start.8 = (bf16[2,1024,256]{2,1,0:T(8,128)(2,1)S(1)}, bf16[2,1024,256]{2,1,0:T(8,128)(2,1)}, u32[]{:S(2)}) copy-start(bf16[2,1024,256]{2,1,0:T(8,128)(2,1)} %copy-done.7) | copy-start | bytes 3145732
  95.5 22.7 %copy-start.22 = (s32[5]{0:T(128)S(1)}, s32[5]{0:T(128)}, u32[]{:S(2)}) copy-start(s32[5]{0:T(128)} %copy-done.21) | copy-start | bytes 64
  102.6 26.6 %copy-start.29 = (bf16[1024,128]{1,0:T(8,128)(2,1)S(1)}, bf16[1024,128]{1,0:T(8,128)(2,1)}, u32[]{:S(2)}) copy-start(bf16[1024,128]{1,0:T(8,128)(2,1)} %get-tuple-element.29) | copy-start | bytes 786436
  102.6 26.7 %copy-start.28 = (bf16[1024,128]{1,0:T(8,128)(2,1)S(1)}, bf16[1024,128]{1,0:T(8,128)(2,1)}, u32[]{:S(2)}) copy-start(bf16[1024,128]{1,0:T(8,128)(2,1)} %get-tuple-element.30) | copy-start | bytes 786436
  102.6 26.5 %collective-permute-start.17 = (bf16[2,1024,128]{2,1,0:T(8,128)(2,1)}, bf16[2,1024,128]{2,1,0:T(8,128)(2,1)S(1)}, u32[]{:S(2)}, u32[]{:S(2)}) collective-permute-start(bf16[2,1024,128]{2,1,0:T(8,128)(2,1)} %get-tuple-element.27), channel_id=1, source_target_pairs={{0,4},{4,8},{8,12},{12,0},{1,5},{5,9},{9,13},{13,1},{2,6},{6,10},{... | collective-permute-start | bytes 1572872 | tf_op jit(solution)/shard_map/ppermute | solution.py:23
  103.1 35.6 %copy-start.10 = (bf16[2,1024,128]{2,1,0:T(8,128)(2,1)S(1)}, bf16[2,1024,128]{2,1,0:T(8,128)(2,1)}, u32[]{:S(2)}) copy-start(bf16[2,1024,128]{2,1,0:T(8,128)(2,1)} %get-tuple-element.26.own_ref) | copy-start | bytes 1572868
  103.1 26.2 %collective-permute-start.18 = (bf16[2,1024,128]{2,1,0:T(8,128)(2,1)}, bf16[2,1024,128]{2,1,0:T(8,128)(2,1)S(1)}, u32[]{:S(2)}, u32[]{:S(2)}) collective-permute-start(bf16[2,1024,128]{2,1,0:T(8,128)(2,1)} %get-tuple-element.28), channel_id=1, source_target_pairs={{0,12},{4,0},{8,4},{12,8},{1,13},{5,1},{9,5},{13,9},{2,14},{6,2},{... | collective-permute-start | bytes 1572872 | tf_op jit(solution)/shard_map/ppermute | solution.py:23
  105.0 13.1 %collective-permute-start.32 = (bf16[256,128]{1,0:T(8,128)(2,1)S(1)}, bf16[256,128]{1,0:T(8,128)(2,1)S(1)}, u32[]{:S(2)}, u32[]{:S(2)}) collective-permute-start(bf16[256,128]{1,0:T(8,128)(2,1)S(1)} %get-tuple-element.41), channel_id=1, source_target_pairs={{0,4},{4,0},{8,12},{12,8},{1,5},{5,1},{9,13},{13,9},{2,6},{6,2},{1... | collective-permute-start | bytes 196616 | tf_op jit(solution)/shard_map/ppermute | solution.py:28
  119.2 6.6 %collective-permute-start.33 = (bf16[512,128]{1,0:T(8,128)(2,1)S(1)}, bf16[512,128]{1,0:T(8,128)(2,1)S(1)}, u32[]{:S(2)}, u32[]{:S(2)}) collective-permute-start(bf16[512,128]{1,0:T(8,128)(2,1)S(1)} %sweep_part.1), channel_id=1, source_target_pairs={{0,16},{16,0},{1,17},{17,1},{2,18},{18,2},{3,19},{19,3},{4,20},{20... | collective-permute-start | bytes 393224 | tf_op jit(solution)/shard_map/ppermute | solution.py:28
  125.8 7.7 %collective-permute-start.35 = (bf16[512,128]{1,0:T(8,128)(2,1)S(1)}, bf16[512,128]{1,0:T(8,128)(2,1)S(1)}, u32[]{:S(2)}, u32[]{:S(2)}) collective-permute-start(bf16[512,128]{1,0:T(8,128)(2,1)S(1)} %add.44), channel_id=1, source_target_pairs={{0,32},{32,64},{64,96},{96,128},{128,160},{160,192},{192,224},{224... | collective-permute-start | bytes 393224 | tf_op jit(solution)/shard_map/ppermute | solution.py:23
  125.9 7.6 %collective-permute-start.34 = (bf16[512,128]{1,0:T(8,128)(2,1)S(1)}, bf16[512,128]{1,0:T(8,128)(2,1)S(1)}, u32[]{:S(2)}, u32[]{:S(2)}) collective-permute-start(bf16[512,128]{1,0:T(8,128)(2,1)S(1)} %add.44), channel_id=1, source_target_pairs={{0,224},{32,0},{64,32},{96,64},{128,96},{160,128},{192,160},{224,1... | collective-permute-start | bytes 393224 | tf_op jit(solution)/shard_map/ppermute | solution.py:23
  129.2 9.5 %collective-permute-start.19 = (bf16[1024,128]{1,0:T(8,128)(2,1)S(1)}, bf16[1024,128]{1,0:T(8,128)(2,1)S(1)}, u32[]{:S(2)}, u32[]{:S(2)}) collective-permute-start(bf16[1024,128]{1,0:T(8,128)(2,1)S(1)} %fusion.3), channel_id=1, source_target_pairs={{0,4},{4,8},{8,12},{12,0},{1,5},{5,9},{9,13},{13,1},{2,6},{6,10},{... | collective-permute-start | bytes 786440 | tf_op jit(solution)/shard_map/ppermute | solution.py:23
  129.3 9.4 %collective-permute-start.20 = (bf16[1024,128]{1,0:T(8,128)(2,1)S(1)}, bf16[1024,128]{1,0:T(8,128)(2,1)S(1)}, u32[]{:S(2)}, u32[]{:S(2)}) collective-permute-start(bf16[1024,128]{1,0:T(8,128)(2,1)S(1)} %fusion.2), channel_id=1, source_target_pairs={{0,12},{4,0},{8,4},{12,8},{1,13},{5,1},{9,5},{13,9},{2,14},{6,2},{... | collective-permute-start | bytes 786440 | tf_op jit(solution)/shard_map/ppermute | solution.py:23
  133.6 8.3 %collective-permute-start.37 = (bf16[512,128]{1,0:T(8,128)(2,1)S(1)}, bf16[512,128]{1,0:T(8,128)(2,1)S(1)}, u32[]{:S(2)}, u32[]{:S(2)}) collective-permute-start(bf16[512,128]{1,0:T(8,128)(2,1)S(1)} %get-tuple-element.38), channel_id=1, source_target_pairs={{0,96},{32,128},{64,160},{96,192},{128,224},{160,0},{192,32},{224,... | collective-permute-start | bytes 393224 | tf_op jit(solution)/shard_map/ppermute | solution.py:23
  136.3 7.5 %collective-permute-start.36 = (bf16[512,128]{1,0:T(8,128)(2,1)S(1)}, bf16[512,128]{1,0:T(8,128)(2,1)S(1)}, u32[]{:S(2)}, u32[]{:S(2)}) collective-permute-start(bf16[512,128]{1,0:T(8,128)(2,1)S(1)} %get-tuple-element.37), channel_id=1, source_target_pairs={{0,160},{32,192},{64,224},{96,0},{128,32},{160,64},{192,96},{224,1... | collective-permute-start | bytes 393224 | tf_op jit(solution)/shard_map/ppermute | solution.py:23
  139.6 6.5 %collective-permute-start.21 = (bf16[1024,128]{1,0:T(8,128)(2,1)S(1)}, bf16[1024,128]{1,0:T(8,128)(2,1)S(1)}, u32[]{:S(2)}, u32[]{:S(2)}) collective-permute-start(bf16[1024,128]{1,0:T(8,128)(2,1)S(1)} %get-tuple-element.32), channel_id=1, source_target_pairs={{0,2},{2,0},{1,3},{3,1},{4,6},{6,4},{5,7},{7,5},{8,10},{10,8},{9,1... | collective-permute-start | bytes 786440 | tf_op jit(solution)/shard_map/ppermute | solution.py:28
  (6 other events, 4.5 us)
